TPU v7x, 32 devices: a whole 2x2x4 slice. The times are simulated.
32 devices in a mesh: lon: 4 (over y, x), lat: 8 (over z, core).
Axes of the slice: x: 2, y: 2, z: 4, core: 2. Of those that a mesh axis runs over, the one named last changes fastest.
Arguments:
- wind_east: float32 [16, 64, 2048], P(None, 'lat', 'lon'), may hold values from -6 to 6
- wind_north: float32 [16, 64, 2048], P(None, 'lat', 'lon'), may hold values from -6 to 6
- potential_temp: float32 [16, 64, 2048], P(None, 'lat', 'lon'), may hold values from -6 to 6
- pressure: float32 [16, 64, 2048], P(None, 'lat', 'lon'), may hold values from -6 to 6
- moisture: float32 [16, 64, 2048], P(None, 'lat', 'lon'), may hold values from -6 to 6
- map_factor: float32 [64], P('lat'), may hold values from 1 to 4
- filter_rows: int32 [32], replicated, may hold values from 0 to 63, as said below
- filter_cutoff: int32 [32], replicated, may hold values from 1 to 1025, as said below
Outputs:
- new_east: float32 [16, 64, 2048], P(None, 'lat', 'lon')
- new_north: float32 [16, 64, 2048], P(None, 'lat', 'lon')
- new_temp: float32 [16, 64, 2048], P(None, 'lat', 'lon')
- new_pressure: float32 [16, 64, 2048], P(None, 'lat', 'lon')
- new_moisture: float32 [16, 64, 2048], P(None, 'lat', 'lon')
Inputs may be any that keep to these rules, and one draw needn't show every extreme that they name: `filter_rows`: ascending and without repeats; the rows are the first m and the last 32 - m latitude rows, for some m with 1 <= m <= 31. `filter_cutoff`: within each polar cap the count does not fall with the row's distance from the nearer pole; the row farthest from the pole in each cap keeps 1025.
All inputs are finite; a program needn't handle non-finite values.
Results may differ from a plain program's by a relative error of at most 0.000073.
Values sent between devices are 32-bit elements; how exact they have to be, the bound alone decides.
No kernel may reach another device: no remote copies, remote signals or barrier semaphores. Data moves between devices by JAX's collectives and lax.ppermute only.
A program may use at most 128 MiB of HBM per device.

v0:
```python
import math

import jax
import jax.numpy as jnp
from jax import lax
from jax.sharding import PartitionSpec as P

SUBSTEPS = 4


ADV_COEF = 0.1
SOUND = 0.4
THETA_DIV = 0.3


def extended_2(array, sides, width, wrap):
    for axis, dim in sides:
        devices, length = (lax.axis_size(axis), array.shape[dim])
        up = [(i, (i + 1) % devices) for i in range(devices if wrap else devices - 1)]
        down = [(j, i) for i, j in up]
        last = lax.slice_in_dim(array, length - width, length, axis=dim)
        initial = lax.slice_in_dim(array, 0, width, axis=dim)
        before = lax.ppermute(last, axis, up)
        after = lax.ppermute(initial, axis, down)
        array = jnp.concatenate([before, array, after], axis=dim)
    return array


def centred(shifted):
    return (
        shifted[0]
        - 9.0 * shifted[1]
        + 45.0 * shifted[2]
        - 45.0 * shifted[3]
        + 9.0 * shifted[4]
        - shifted[5]
    ) / 60.0


def damping(shifted, centre):
    return (
        shifted[0]
        - 6.0 * shifted[1]
        + 15.0 * shifted[2]
        - 20.0 * centre
        + 15.0 * shifted[3]
        - 6.0 * shifted[4]
        + shifted[5]
    ) / 60.0


def wave_table(circle):
    half = circle // 2
    points = jnp.arange(circle, dtype=jnp.int32)
    cos_waves = jnp.arange(half + 1, dtype=jnp.int32)
    sin_waves = jnp.arange(1, half, dtype=jnp.int32)
    cos_angles = (points[:, None] * cos_waves[None, :] % circle).astype(jnp.float32) * (
        2.0 * math.pi / circle
    )
    sin_angles = (points[:, None] * sin_waves[None, :] % circle).astype(jnp.float32) * (
        2.0 * math.pi / circle
    )
    table = jnp.concatenate([jnp.cos(cos_angles), jnp.sin(sin_angles)], axis=1)
    wave_index = jnp.concatenate([cos_waves, sin_waves])
    return (table, wave_index)


def filter_circles(circles, table, wave_index, item_cut, flagged, circle):
    spectra = jnp.dot(circles, table, precision=lax.Precision.HIGHEST)
    single = (wave_index == 0) | (wave_index == circle // 2)
    weights = jnp.where(single, 1.0, 2.0) / circle
    kept_mask = wave_index[None, :] < item_cut[:, None]
    spectra = jnp.where(kept_mask, spectra * weights[None, :], 0.0)
    smooth = lax.dot_general(
        spectra, table, (((1,), (1,)), ((), ())), precision=lax.Precision.HIGHEST
    )
    return jnp.where(flagged[:, None], smooth, circles)


def item_tables(item_rows, row_cut, row_flag, rows_dev):
    picked = item_rows[:, None] == jnp.arange(rows_dev, dtype=jnp.int32)[None, :]
    item_cut = jnp.sum(jnp.where(picked, row_cut[None, :], 0), axis=1)
    flagged = jnp.any(picked & row_flag[None, :], axis=1)
    return (item_cut, flagged)


def pole_mask(extended, lat_place, rows_dev, total_rows, depth, row_dim):
    ext_rows = lat_place * rows_dev - depth + jnp.arange(rows_dev + 2 * depth, dtype=jnp.int32)
    inside = (ext_rows >= 0) & (ext_rows < total_rows)
    shape_mask = [1] * extended.ndim
    shape_mask[row_dim] = rows_dev + 2 * depth
    return jnp.where(inside.reshape(shape_mask), extended, 0.0)


def shards(
    wind_east,
    wind_north,
    potential_temp,
    pressure,
    moisture,
    map_factor,
    filter_rows,
    filter_cutoff,
):
    levels, rows_dev, cols_dev = wind_east.shape
    lon_count = lax.axis_size("lon")
    lat_count = lax.axis_size("lat")
    lon_place = lax.axis_index("lon")
    lat_place = lax.axis_index("lat")
    circle = cols_dev * lon_count
    total_rows = rows_dev * lat_count
    local_rows = lat_place * rows_dev + jnp.arange(rows_dev, dtype=jnp.int32)
    matches = filter_rows[:, None] == local_rows[None, :]
    row_flag = jnp.any(matches, axis=0)
    row_cut = jnp.sum(jnp.where(matches, filter_cutoff[:, None], 0), axis=0)
    table, wave_index = wave_table(circle)
    stacked = jnp.stack([wind_east, wind_north, potential_temp, pressure, moisture])
    per_dev = levels * rows_dev // lon_count
    item_ids = lon_place * per_dev + jnp.arange(per_dev, dtype=jnp.int32)
    item_cut, flagged = item_tables(item_ids % rows_dev, row_cut, row_flag, rows_dev)
    results = []
    for field_index in range(5):
        blocks = stacked[field_index].reshape(lon_count, per_dev, cols_dev)
        circles = lax.all_to_all(blocks, "lon", split_axis=0, concat_axis=2, tiled=True)[0]
        smooth = filter_circles(circles, table, wave_index, item_cut, flagged, circle)
        returned = lax.all_to_all(smooth[None], "lon", split_axis=2, concat_axis=0, tiled=True)
        results.append(returned.reshape(levels, rows_dev, cols_dev))
    stacked = jnp.stack(results)
    extended = extended_2(stacked, (("lon", 3), ("lat", 2)), 3, True)
    extended = pole_mask(extended, lat_place, rows_dev, total_rows, 3, 2)
    along = [
        extended[:, :, 3 : 3 + rows_dev, 3 + offset : 3 + offset + cols_dev]
        for offset in (3, 2, 1, -1, -2, -3)
    ]
    across = [
        extended[:, :, 3 + offset : 3 + offset + rows_dev, 3 : 3 + cols_dev]
        for offset in (3, 2, 1, -1, -2, -3)
    ]
    east_wind = stacked[0]
    north_wind = stacked[1]
    coef_x = (ADV_COEF * map_factor)[:, None]
    zonal = east_wind[None] * centred(along) - jnp.abs(east_wind[None]) * damping(along, stacked)
    meridional = north_wind[None] * centred(across) - jnp.abs(north_wind[None]) * damping(
        across, stacked
    )
    tendency = -coef_x * zonal - ADV_COEF * meridional
    tend_east, tend_north, tend_temp, tend_press, tend_moist = (
        tendency[0],
        tendency[1],
        tendency[2],
        tendency[3],
        tendency[4],
    )
    theta_now = stacked[2]
    press_now = stacked[3]
    moist_now = stacked[4]
    grad_x = (SOUND * map_factor)[:, None]
    latitude = -0.5 * math.pi + (local_rows.astype(jnp.float32) + 0.5) * (math.pi / total_rows)
    coriolis = (0.5 * jnp.sin(latitude))[:, None]
    substep_dt = 1.0 / SUBSTEPS
    for substep in range(SUBSTEPS):
        press_ext = extended_2(press_now, (("lon", 2), ("lat", 1)), 1, True)
        press_ext = pole_mask(press_ext, lat_place, rows_dev, total_rows, 1, 1)
        press_dx = (press_ext[:, 1:-1, 2:] - press_ext[:, 1:-1, :-2]) * 0.5
        press_dy = (press_ext[:, 2:, 1:-1] - press_ext[:, :-2, 1:-1]) * 0.5
        east_wind = east_wind + substep_dt * (tend_east - grad_x * press_dx + coriolis * north_wind)
        north_wind = north_wind + substep_dt * (
            tend_north - SOUND * press_dy - coriolis * east_wind
        )
        east_ext = extended_2(east_wind, (("lon", 2),), 1, True)
        north_ext = extended_2(north_wind, (("lat", 1),), 1, False)
        diverge = (
            grad_x * (east_ext[:, :, 2:] - east_ext[:, :, :-2]) * 0.5
            + SOUND * (north_ext[:, 2:, :] - north_ext[:, :-2, :]) * 0.5
        )
        press_now = press_now + substep_dt * (tend_press - diverge)
        theta_now = theta_now + substep_dt * (tend_temp - THETA_DIV * diverge)
        moist_now = moist_now + substep_dt * tend_moist
    return (east_wind, north_wind, theta_now, press_now, moist_now)


def solution(mesh):
    in_specs = (
        P(None, "lat", "lon"),
        P(None, "lat", "lon"),
        P(None, "lat", "lon"),
        P(None, "lat", "lon"),
        P(None, "lat", "lon"),
        P("lat"),
        P(),
        P(),
    )
    out_specs = (
        P(None, "lat", "lon"),
        P(None, "lat", "lon"),
        P(None, "lat", "lon"),
        P(None, "lat", "lon"),
        P(None, "lat", "lon"),
    )
    return jax.shard_map(shards, mesh=mesh, in_specs=in_specs, out_specs=out_specs, check_vma=False)
```

profile of v0, /device:TPU:0, one launch (start us, length us, event | category | flops | bytes accessed | tf_op | source)
XLA Modules:
  0.0 494.1 jit_solution(3201918005113495006)
XLA Ops:
  0.6 5.2 %all-to-all-start = ((f32[4,32,512]{2,1,0:T(8,128)}), f32[4,32,512]{2,1,0:T(8,128)S(1)}, u32[]{:S(2)}, u32[]{:S(2)}) async-start(f32[4,32,512]{2,1,0:T(8,128)} %bitcast.201), calls=%async_computation | async-start | bytes 524288 | tf_op jit(solution)/shard_map/all_to_all | solution.py:124
  5.9 35.4 %fusion.3 = f32[2048,1025]{1,0:T(8,128)} fusion(), kind=kLoop, calls=%fused_computation.10 | loop fusion | flops 29388800 | bytes 8396800 | tf_op jit(solution)/shard_map/cos | solution.py:63
  41.7 32.0 %fusion.10 = f32[2048,1023]{1,0:T(8,128)} fusion(s32[1023]{0:T(1024)S(1)} %iota_add_fusion), kind=kLoop, calls=%fused_computation.17 | loop fusion | flops 29331456 | bytes 8384508 | tf_op jit(solution)/shard_map/sin | solution.py:63
  78.2 5.3 %all-to-all-done.4 = f32[4,32,512]{2,1,0:T(8,128)S(1)} async-done(((f32[4,32,512]{2,1,0:T(8,128)}), f32[4,32,512]{2,1,0:T(8,128)S(1)}, u32[]{:S(2)}, u32[]{:S(2)}) %all-to-all-start.4) | async-done | bytes 262176 | tf_op jit(solution)/shard_map/all_to_all | solution.py:124
  87.5 4.8 all-to-all-done.8
  96.3 17.9 %fusion.26 = f32[32,2048]{1,0:T(8,128)} fusion(f32[32,2048]{1,0:T(8,128)S(1)} %bitcast.182, f32[2048]{0:T(1024)S(1)} %get-tuple-element.18, s32[2048]{0:T(1024)S(1)} %get-tuple-element.19, s32[32]{0:T(128)S(1)} %select_reduce_fusion, f32[2048,1023]{1,0:T(8,128)} %fusion.10, f32[2048,1025]{1,0:T(8,128)} %fusion.3), kind=kOutput, calls=%fused_computation.44 | convolution fusion | flops 1615003648 | bytes 17318016 | tf_op jit(solution)/shard_map/dot_general | solution.py:69
  114.2 15.2 %fusion.28 = f32[32,2048]{1,0:T(8,128)} fusion(f32[32,2048]{1,0:T(8,128)S(1)} %bitcast.184, f32[2048]{0:T(1024)S(1)} %get-tuple-element.18, s32[2048]{0:T(1024)S(1)} %get-tuple-element.19, s32[32]{0:T(128)S(1)} %select_reduce_fusion, f32[2048,1023]{1,0:T(8,128)} %fusion.10, f32[2048,1025]{1,0:T(8,128)S(1)} %bitcast.148), kind=kOutput, calls=%fused_computation.46 | convolution fusion | flops 1615003648 | bytes 17318016 | tf_op jit(solution)/shard_map/dot_general | solution.py:69
  129.4 16.1 %fusion.18 = f32[1,32,2048]{2,1,0:T(8,128)S(1)} fusion(f32[32,2048]{1,0:T(8,128)S(1)} %bitcast.183, f32[32,2048]{1,0:T(8,128)} %fusion.26, pred[32]{0:T(512)(128)(4,1)S(1)} %fusion.96, f32[2048,1023]{1,0:T(8,128)S(1)} %bitcast.150, f32[2048,1025]{1,0:T(8,128)S(1)} %bitcast.148), kind=kOutput, calls=%fused_computation.31 | convolution fusion | flops 1614872576 | bytes 17563680 | tf_op jit(solution)/shard_map/dot_general | solution.py:74
  145.5 16.3 %fusion.14 = f32[1,32,2048]{2,1,0:T(8,128)S(1)} fusion(f32[32,2048]{1,0:T(8,128)S(1)} %bitcast.185, f32[32,2048]{1,0:T(8,128)} %fusion.28, pred[32]{0:T(512)(128)(4,1)S(1)} %fusion.96, f32[2048,1023]{1,0:T(8,128)S(1)} %bitcast.150, f32[2048,1025]{1,0:T(8,128)S(1)} %bitcast.148), kind=kOutput, calls=%fused_computation.23 | convolution fusion | flops 1614872576 | bytes 17563680 | tf_op jit(solution)/shard_map/dot_general | solution.py:74
  161.8 11.5 %fusion.24 = f32[32,2048]{1,0:T(8,128)} fusion(f32[32,2048]{1,0:T(8,128)S(1)} %bitcast.178, f32[2048]{0:T(1024)S(1)} %get-tuple-element.18, s32[2048]{0:T(1024)S(1)} %get-tuple-element.19, s32[32]{0:T(128)S(1)} %select_reduce_fusion, f32[2048,1023]{1,0:T(8,128)S(1)} %bitcast.150, f32[2048,1025]{1,0:T(8,128)S(1)} %bitcast.148), kind=kOutput, calls=%fused_computation.42 | convolution fusion | flops 1615003648 | bytes 17318016 | tf_op jit(solution)/shard_map/dot_general | solution.py:69
  173.3 4.6 all-to-all-start.2
  177.9 20.0 %fusion.22 = f32[1,32,2048]{2,1,0:T(8,128)S(1)} fusion(f32[32,2048]{1,0:T(8,128)S(1)} %bitcast.179, f32[32,2048]{1,0:T(8,128)} %fusion.24, pred[32]{0:T(512)(128)(4,1)S(1)} %fusion.96, f32[2048,1023]{1,0:T(8,128)} %fusion.10, f32[2048,1025]{1,0:T(8,128)} %fusion.3), kind=kOutput, calls=%fused_computation.39 | convolution fusion | flops 1614872576 | bytes 17563680 | tf_op jit(solution)/shard_map/dot_general | solution.py:74
  199.2 9.3 %reduce.4 = f32[2048,32]{1,0:T(8,128)S(1)} reduce(f32[2048,1,32]{2,1,0:T(1,128)S(1)} %bitcast.156, f32[]{:T(128)} %broadcast.311), dimensions={1}, to_apply=%bitcast.123.reduce_sub_computation | reduce | bytes 524292
  214.8 15.9 %fusion.27 = f32[32,2048]{1,0:T(8,128)} fusion(f32[32,2048]{1,0:T(8,128)S(1)} %bitcast.180, f32[2048]{0:T(1024)S(1)} %get-tuple-element.18, s32[2048]{0:T(1024)S(1)} %get-tuple-element.19, s32[32]{0:T(128)S(1)} %select_reduce_fusion, f32[2048,1023]{1,0:T(8,128)} %fusion.10, f32[2048,1025]{1,0:T(8,128)} %fusion.3), kind=kOutput, calls=%fused_computation.45 | convolution fusion | flops 1615003648 | bytes 17318016 | tf_op jit(solution)/shard_map/dot_general | solution.py:69
  231.2 9.3 %reduce.8 = f32[2048,32]{1,0:T(8,128)S(1)} reduce(f32[2048,1,32]{2,1,0:T(1,128)S(1)} %bitcast.157, f32[]{:T(128)} %broadcast.311), dimensions={1}, to_apply=%bitcast.131.reduce_sub_computation | reduce | bytes 524292
  246.2 20.0 %fusion.16 = f32[1,32,2048]{2,1,0:T(8,128)S(1)} fusion(f32[32,2048]{1,0:T(8,128)S(1)} %bitcast.181, f32[32,2048]{1,0:T(8,128)} %fusion.27, pred[32]{0:T(512)(128)(4,1)S(1)} %fusion.96, f32[2048,1023]{1,0:T(8,128)} %fusion.10, f32[2048,1025]{1,0:T(8,128)} %fusion.3), kind=kOutput, calls=%fused_computation.27 | convolution fusion | flops 1614872576 | bytes 17563680 | tf_op jit(solution)/shard_map/dot_general | solution.py:74
  267.0 9.3 %reduce.2 = f32[2048,32]{1,0:T(8,128)S(1)} reduce(f32[2048,1,32]{2,1,0:T(1,128)S(1)} %bitcast.158, f32[]{:T(128)} %broadcast.311), dimensions={1}, to_apply=%bitcast.125.reduce_sub_computation | reduce | bytes 524292
  277.6 4.6 all-to-all-start.7
  282.2 15.9 %fusion.25 = f32[32,2048]{1,0:T(8,128)} fusion(f32[32,2048]{1,0:T(8,128)S(1)} %bitcast.176, f32[2048]{0:T(1024)S(1)} %get-tuple-element.18, s32[2048]{0:T(1024)S(1)} %get-tuple-element.19, s32[32]{0:T(128)S(1)} %select_reduce_fusion, f32[2048,1023]{1,0:T(8,128)} %fusion.10, f32[2048,1025]{1,0:T(8,128)} %fusion.3), kind=kOutput, calls=%fused_computation.43 | convolution fusion | flops 1615003648 | bytes 17318016 | tf_op jit(solution)/shard_map/dot_general | solution.py:69
  298.6 9.3 %reduce.6 = f32[2048,32]{1,0:T(8,128)S(1)} reduce(f32[2048,1,32]{2,1,0:T(1,128)S(1)} %bitcast.159, f32[]{:T(128)} %broadcast.311), dimensions={1}, to_apply=%bitcast.129.reduce_sub_computation | reduce | bytes 524292
  313.5 20.0 %fusion.20 = f32[1,32,2048]{2,1,0:T(8,128)S(1)} fusion(f32[32,2048]{1,0:T(8,128)S(1)} %bitcast.177, f32[32,2048]{1,0:T(8,128)} %fusion.25, pred[32]{0:T(512)(128)(4,1)S(1)} %fusion.96, f32[2048,1023]{1,0:T(8,128)} %fusion.10, f32[2048,1025]{1,0:T(8,128)} %fusion.3), kind=kOutput, calls=%fused_computation.35 | convolution fusion | flops 1614872576 | bytes 17563680 | tf_op jit(solution)/shard_map/dot_general | solution.py:74
  334.0 9.6 %reduce = f32[2048,32]{1,0:T(8,128)S(1)} reduce(f32[2048,1,32]{2,1,0:T(1,128)S(1)} %bitcast.160, f32[]{:T(128)} %broadcast.311), dimensions={1}, to_apply=%bitcast.127.reduce_sub_computation | reduce | bytes 524292
  383.6 12.2 %collective-permute-done.3 = f32[5,16,3,518]{3,1,2,0:T(8,128)S(1)} collective-permute-done((f32[5,16,3,518]{3,1,2,0:T(8,128)S(1)}, f32[5,16,3,518]{3,1,2,0:T(8,128)S(1)}, u32[]{:S(2)}, u32[]{:S(2)}) %collective-permute-start.3) | collective-permute-done | bytes 497312 | tf_op jit(solution)/shard_map/ppermute | solution.py:24
  396.2 4.4 collective-permute-done.2
  (209 shorter events, 168.3 us)
Async XLA Ops:
  0.6 73.3 %all-to-all-start = ((f32[4,32,512]{2,1,0:T(8,128)}), f32[4,32,512]{2,1,0:T(8,128)S(1)}, u32[]{:S(2)}, u32[]{:S(2)}) async-start(f32[4,32,512]{2,1,0:T(8,128)} %bitcast.201), calls=%async_computation | async-start | bytes 524288 | tf_op jit(solution)/shard_map/all_to_all | solution.py:124
  73.9 9.6 %all-to-all-start.4 = ((f32[4,32,512]{2,1,0:T(8,128)}), f32[4,32,512]{2,1,0:T(8,128)S(1)}, u32[]{:S(2)}, u32[]{:S(2)}) async-start(f32[4,32,512]{2,1,0:T(8,128)} %bitcast.17), calls=%async_computation.4 | async-start | bytes 524288 | tf_op jit(solution)/shard_map/all_to_all | solution.py:124
  92.2 81.1 %all-to-all-start.6 = ((f32[4,32,512]{2,1,0:T(8,128)}), f32[4,32,512]{2,1,0:T(8,128)S(1)}, u32[]{:S(2)}, u32[]{:S(2)}) async-start(f32[4,32,512]{2,1,0:T(8,128)} %bitcast.25), calls=%async_computation.6 | async-start | bytes 524288 | tf_op jit(solution)/shard_map/all_to_all | solution.py:124
  173.3 36.4 %all-to-all-start.2 = ((f32[4,32,512]{2,1,0:T(8,128)}), f32[4,32,512]{2,1,0:T(8,128)S(1)}, u32[]{:S(2)}, u32[]{:S(2)}) async-start(f32[4,32,512]{2,1,0:T(8,128)} %bitcast.202), calls=%async_computation.2 | async-start | bytes 524288 | tf_op jit(solution)/shard_map/all_to_all | solution.py:124
  210.4 31.3 %all-to-all-start.1 = ((f32[4,1,16384]{2,1,0:T(1,128)}), f32[4,1,16384]{2,1,0:T(1,128)S(1)}, u32[]{:S(2)}, u32[]{:S(2)}) async-start(f32[4,1,16384]{2,1,0:T(1,128)} %reshape.128), calls=%async_computation.1 | async-start | bytes 524288 | tf_op jit(solution)/shard_map/all_to_all | solution.py:126
  241.8 35.8 %all-to-all-start.9 = ((f32[4,1,16384]{2,1,0:T(1,128)}), f32[4,1,16384]{2,1,0:T(1,128)S(1)}, u32[]{:S(2)}, u32[]{:S(2)}) async-start(f32[4,1,16384]{2,1,0:T(1,128)} %reshape.136), calls=%async_computation.9 | async-start | bytes 524288 | tf_op jit(solution)/shard_map/all_to_all | solution.py:126
  277.6 31.5 %all-to-all-start.7 = ((f32[4,1,16384]{2,1,0:T(1,128)}), f32[4,1,16384]{2,1,0:T(1,128)S(1)}, u32[]{:S(2)}, u32[]{:S(2)}) async-start(f32[4,1,16384]{2,1,0:T(1,128)} %reshape.130), calls=%async_computation.7 | async-start | bytes 524288 | tf_op jit(solution)/shard_map/all_to_all | solution.py:126
  309.1 45.8 %all-to-all-start.5 = ((f32[4,1,16384]{2,1,0:T(1,128)}), f32[4,1,16384]{2,1,0:T(1,128)S(1)}, u32[]{:S(2)}, u32[]{:S(2)}) async-start(f32[4,1,16384]{2,1,0:T(1,128)} %reshape.134), calls=%async_computation.5 | async-start | bytes 524288 | tf_op jit(solution)/shard_map/all_to_all | solution.py:126
  354.9 11.1 %all-to-all-start.3 = ((f32[4,1,16384]{2,1,0:T(1,128)}), f32[4,1,16384]{2,1,0:T(1,128)S(1)}, u32[]{:S(2)}, u32[]{:S(2)}) async-start(f32[4,1,16384]{2,1,0:T(1,128)} %reshape.132), calls=%async_computation.3 | async-start | bytes 524288 | tf_op jit(solution)/shard_map/all_to_all | solution.py:126
  359.2 13.5 %collective-permute-start.4 = (f32[16,8,1]{2,1,0:T(8,128)S(1)}, f32[16,8,1]{2,1,0:T(8,128)S(1)}, u32[]{:S(2)}, u32[]{:S(2)}) collective-permute-start(f32[16,8,1]{2,1,0:T(8,128)S(1)} %get-tuple-element.60), channel_id=1, source_target_pairs={{0,8},{8,16},{16,24},{24,0},{1,9},{9,17},{17,25},{25,1},{2,10},{10... | collective-permute-start | bytes 1544 | tf_op jit(solution)/shard_map/ppermute | solution.py:23
  361.2 11.4 %collective-permute-start.5 = (f32[16,8,1]{2,1,0:T(8,128)S(1)}, f32[16,8,1]{2,1,0:T(8,128)S(1)}, u32[]{:S(2)}, u32[]{:S(2)}) collective-permute-start(f32[16,8,1]{2,1,0:T(8,128)S(1)} %get-tuple-element.61), channel_id=1, source_target_pairs={{8,0},{16,8},{24,16},{0,24},{9,1},{17,9},{25,17},{1,25},{10,2},{18... | collective-permute-start | bytes 1544 | tf_op jit(solution)/shard_map/ppermute | solution.py:24
  370.8 10.9 %collective-permute-start.1 = (f32[5,16,8,3]{3,2,1,0:T(8,128)S(1)}, f32[5,16,8,3]{3,2,1,0:T(8,128)S(1)}, u32[]{:S(2)}, u32[]{:S(2)}) collective-permute-start(f32[5,16,8,3]{3,2,1,0:T(8,128)S(1)} %get-tuple-element.25), channel_id=1, source_target_pairs={{8,0},{16,8},{24,16},{0,24},{9,1},{17,9},{25,17},{1,25},{10,2},{18... | collective-permute-start | bytes 23048 | tf_op jit(solution)/shard_map/ppermute | solution.py:24
  372.9 10.4 %collective-permute-start.6 = (f32[16,1,514]{2,1,0:T(1,128)S(1)}, f32[16,1,514]{2,1,0:T(1,128)S(1)}, u32[]{:S(2)}, u32[]{:S(2)}) collective-permute-start(f32[16,1,514]{2,1,0:T(1,128)S(1)} %get-tuple-element.32), channel_id=1, source_target_pairs={{0,1},{1,2},{2,3},{3,4},{4,5},{5,6},{6,7},{7,0},{8,9},{9,10},{10,1... | collective-permute-start | bytes 98696 | tf_op jit(solution)/shard_map/ppermute | solution.py:23
  373.0 10.3 %collective-permute-start.7 = (f32[16,1,514]{2,1,0:T(1,128)S(1)}, f32[16,1,514]{2,1,0:T(1,128)S(1)}, u32[]{:S(2)}, u32[]{:S(2)}) collective-permute-start(f32[16,1,514]{2,1,0:T(1,128)S(1)} %get-tuple-element.33), channel_id=1, source_target_pairs={{1,0},{2,1},{3,2},{4,3},{5,4},{6,5},{7,6},{0,7},{9,8},{10,9},{11,1... | collective-permute-start | bytes 98696 | tf_op jit(solution)/shard_map/ppermute | solution.py:24
  382.6 13.2 %collective-permute-start.3 = (f32[5,16,3,518]{3,1,2,0:T(8,128)S(1)}, f32[5,16,3,518]{3,1,2,0:T(8,128)S(1)}, u32[]{:S(2)}, u32[]{:S(2)}) collective-permute-start(f32[5,16,3,518]{3,1,2,0:T(8,128)S(1)} %copy.108), channel_id=1, source_target_pairs={{1,0},{2,1},{3,2},{4,3},{5,4},{6,5},{7,6},{0,7},{9,8},{10,9},{11,1... | collective-permute-start | bytes 1491848 | tf_op jit(solution)/shard_map/ppermute | solution.py:24
  382.7 17.9 %collective-permute-start.2 = (f32[5,16,3,518]{3,1,2,0:T(8,128)S(1)}, f32[5,16,3,518]{3,1,2,0:T(8,128)S(1)}, u32[]{:S(2)}, u32[]{:S(2)}) collective-permute-start(f32[5,16,3,518]{3,1,2,0:T(8,128)S(1)} %copy.107), channel_id=1, source_target_pairs={{0,1},{1,2},{2,3},{3,4},{4,5},{5,6},{6,7},{7,0},{8,9},{9,10},{10,1... | collective-permute-start | bytes 1491848 | tf_op jit(solution)/shard_map/ppermute | solution.py:23
  406.9 10.3 %collective-permute-start.10 = (f32[16,1,512]{2,1,0:T(1,128)S(1)}, f32[16,1,512]{2,1,0:T(1,128)S(1)}, u32[]{:S(2)}, u32[]{:S(2)}) collective-permute-start(f32[16,1,512]{2,1,0:T(1,128)S(1)} %get-tuple-element.54), channel_id=1, source_target_pairs={{1,0},{2,1},{3,2},{4,3},{5,4},{6,5},{7,6},{9,8},{10,9},{11,10},{12... | collective-permute-start | bytes 98312 | tf_op jit(solution)/shard_map/ppermute | solution.py:24
  408.2 9.1 %collective-permute-start.11 = (f32[16,1,512]{2,1,0:T(1,128)S(1)}, f32[16,1,512]{2,1,0:T(1,128)S(1)}, u32[]{:S(2)}, u32[]{:S(2)}) collective-permute-start(f32[16,1,512]{2,1,0:T(1,128)S(1)} %get-tuple-element.55), channel_id=1, source_target_pairs={{0,1},{1,2},{2,3},{3,4},{4,5},{5,6},{6,7},{8,9},{9,10},{10,11},{11... | collective-permute-start | bytes 98312 | tf_op jit(solution)/shard_map/ppermute | solution.py:23
  430.1 11.8 %collective-permute-start.18 = (f32[16,1,512]{2,1,0:T(1,128)S(1)}, f32[16,1,512]{2,1,0:T(1,128)S(1)}, u32[]{:S(2)}, u32[]{:S(2)}) collective-permute-start(f32[16,1,512]{2,1,0:T(1,128)S(1)} %get-tuple-element.48), channel_id=1, source_target_pairs={{1,0},{2,1},{3,2},{4,3},{5,4},{6,5},{7,6},{9,8},{10,9},{11,10},{12... | collective-permute-start | bytes 98312 | tf_op jit(solution)/shard_map/ppermute | solution.py:24
  431.4 10.5 %collective-permute-start.19 = (f32[16,1,512]{2,1,0:T(1,128)S(1)}, f32[16,1,512]{2,1,0:T(1,128)S(1)}, u32[]{:S(2)}, u32[]{:S(2)}) collective-permute-start(f32[16,1,512]{2,1,0:T(1,128)S(1)} %get-tuple-element.49), channel_id=1, source_target_pairs={{0,1},{1,2},{2,3},{3,4},{4,5},{5,6},{6,7},{8,9},{9,10},{10,11},{11... | collective-permute-start | bytes 98312 | tf_op jit(solution)/shard_map/ppermute | solution.py:23
  454.4 11.8 %collective-permute-start.26 = (f32[16,1,512]{2,1,0:T(1,128)S(1)}, f32[16,1,512]{2,1,0:T(1,128)S(1)}, u32[]{:S(2)}, u32[]{:S(2)}) collective-permute-start(f32[16,1,512]{2,1,0:T(1,128)S(1)} %get-tuple-element.42), channel_id=1, source_target_pairs={{1,0},{2,1},{3,2},{4,3},{5,4},{6,5},{7,6},{9,8},{10,9},{11,10},{12... | collective-permute-start | bytes 98312 | tf_op jit(solution)/shard_map/ppermute | solution.py:24
  455.7 10.5 %collective-permute-start.27 = (f32[16,1,512]{2,1,0:T(1,128)S(1)}, f32[16,1,512]{2,1,0:T(1,128)S(1)}, u32[]{:S(2)}, u32[]{:S(2)}) collective-permute-start(f32[16,1,512]{2,1,0:T(1,128)S(1)} %get-tuple-element.43), channel_id=1, source_target_pairs={{0,1},{1,2},{2,3},{3,4},{4,5},{5,6},{6,7},{8,9},{9,10},{10,11},{11... | collective-permute-start | bytes 98312 | tf_op jit(solution)/shard_map/ppermute | solution.py:23
  479.5 11.8 %collective-permute-start.34 = (f32[16,1,512]{2,1,0:T(1,128)S(1)}, f32[16,1,512]{2,1,0:T(1,128)S(1)}, u32[]{:S(2)}, u32[]{:S(2)}) collective-permute-start(f32[16,1,512]{2,1,0:T(1,128)S(1)} %get-tuple-element.36), channel_id=1, source_target_pairs={{1,0},{2,1},{3,2},{4,3},{5,4},{6,5},{7,6},{9,8},{10,9},{11,10},{12... | collective-permute-start | bytes 98312 | tf_op jit(solution)/shard_map/ppermute | solution.py:24
  480.8 10.5 %collective-permute-start.35 = (f32[16,1,512]{2,1,0:T(1,128)S(1)}, f32[16,1,512]{2,1,0:T(1,128)S(1)}, u32[]{:S(2)}, u32[]{:S(2)}) collective-permute-start(f32[16,1,512]{2,1,0:T(1,128)S(1)} %get-tuple-element.37), channel_id=1, source_target_pairs={{0,1},{1,2},{2,3},{3,4},{4,5},{5,6},{6,7},{8,9},{9,10},{10,11},{11... | collective-permute-start | bytes 98312 | tf_op jit(solution)/shard_map/ppermute | solution.py:23
  (34 other events, 387.8 us)
where the time goes:
time: 500 us; the launch traced here: 494 us
  matrix products  169 us (34%)
  other arithmetic  136 us (27%)
  starting transfers between devices  99.5 us (20%)
  waiting for transfers between devices  65.2 us (13%)
  local copies, waits for them, and re-layouts  23.2 us (5%)
    dot_general x5, matrix products, filter_circles(): lax.dot_general(spectra, table, (((1,), (1,)), ((), ())), precision=lax.P...  92.3 us
    dot_general x5, matrix products, filter_circles(): spectra = jnp.dot(circles, table, precision=lax.Precision.HIGHEST)  76.2 us
    unnamed x7, other arithmetic  46.9 us
    ppermute x18, starting transfers between devices, extended_2(): after = lax.ppermute(initial, axis, down)  37.2 us
    cos x1, other arithmetic, wave_table(): table = jnp.concatenate([jnp.cos(cos_angles), jnp.sin(sin_angles)], axis=1)  35.4 us
    sin x1, other arithmetic, wave_table(): table = jnp.concatenate([jnp.cos(cos_angles), jnp.sin(sin_angles)], axis=1)  32 us
    ppermute x18, waiting for transfers between devices, extended_2(): after = lax.ppermute(initial, axis, down)  27.7 us
    ppermute x18, waiting for transfers between devices, extended_2(): before = lax.ppermute(last, axis, up)  27.5 us
  transfers between devices with their start and end apart: 46, of which 23 were waited for; matrix products, arithmetic and copies ran while one was open for 63% of the time, Pallas kernels for 0%

commit v1 on v0

v1 whole, which is shorter than its diff:
```python
import functools
import math

import jax
import jax.numpy as jnp
import numpy as np
from jax import lax
from jax.experimental import pallas as pl
from jax.experimental.pallas import tpu as pltpu
from jax.sharding import Mesh
from jax.sharding import PartitionSpec as P

SUBSTEPS = 4
ADV_COEF = 0.1
SOUND = 0.4
THETA_DIV = 0.3

LANES = 128
RADIX = 16
HALF = RADIX // 2
CIRCLE = LANES * RADIX
WIND_HALO = 10
TRACER_HALO = 3
PAD = 16
KEEP_ALL = 1 << 20
VMEM_BYTES = 32 * 1024 * 1024


def transform_tables():
    lane = np.arange(LANES)
    angle = 2.0 * np.pi * np.outer(lane, lane) / LANES
    cos, sin = np.cos(angle), np.sin(angle)
    matrix = np.block([[cos, -sin], [sin, cos]]).astype(np.float32)
    high = matrix.astype(jnp.bfloat16)
    low = (matrix - high.astype(np.float32)).astype(jnp.bfloat16)
    turn = 2.0 * np.pi * np.outer(np.arange(HALF + 1), lane) / CIRCLE
    twiddle = np.stack([np.cos(turn), np.sin(turn)], axis=1).astype(np.float32)
    twiddle = np.broadcast_to(twiddle[:, :, None, :], (HALF + 1, 2, 8, LANES))
    return high, low, np.ascontiguousarray(twiddle)


def times_root(value, step, size, sign):
    re, im = value
    if step == 0:
        return value
    if 4 * step == size:
        if im is None:
            return (jnp.zeros_like(re), re if sign > 0 else -re)
        return (-im, re) if sign > 0 else (im, -re)
    c = math.cos(2.0 * math.pi * step / size)
    s = sign * math.sin(2.0 * math.pi * step / size)
    if im is None:
        return (re * c, re * s)
    return (re * c - im * s, re * s + im * c)


def added(a, b):
    im = a[1] if b[1] is None else b[1] if a[1] is None else a[1] + b[1]
    return (a[0] + b[0], im)


def taken(a, b):
    im = a[1] if b[1] is None else -b[1] if a[1] is None else a[1] - b[1]
    return (a[0] - b[0], im)


def conj(a):
    return (a[0], None if a[1] is None else -a[1])


def real_forward(values):
    size = len(values)
    if size == 1:
        return [(values[0], None)]
    even, odd = real_forward(values[0::2]), real_forward(values[1::2])
    out = [None] * (size // 2 + 1)
    for k in range(size // 4 + 1):
        turned = times_root(odd[k], k, size, -1)
        out[k] = added(even[k], turned)
        if k != size // 2 - k:
            out[size // 2 - k] = conj(taken(even[k], turned))
    return out


def real_inverse(spectrum, size):
    if size == 1:
        return [spectrum[0][0]]
    even, odd = [], []
    for k in range(size // 4 + 1):
        mirror = conj(spectrum[size // 2 - k])
        even.append(added(spectrum[k], mirror))
        odd.append(times_root(taken(spectrum[k], mirror), k, size, 1))
    out = [None] * size
    out[0::2] = real_inverse(even, size // 2)
    out[1::2] = real_inverse(odd, size // 2)
    return out


def split_dot(values, high, low):
    top = values.astype(jnp.bfloat16)
    rest = (values - top.astype(jnp.float32)).astype(jnp.bfloat16)
    dot = functools.partial(jnp.dot, preferred_element_type=jnp.float32)
    return dot(top, high) + (dot(rest, high) + dot(top, low))


def filter_kernel(dims, *refs):
    fields, levels, sub, rows, tiles_dev, halo = dims
    circles_ref, cut_ref, twiddle_ref, high_ref, low_ref = refs[:5]
    own_ref = refs[5]
    waves_ref = refs[-1]
    sends = refs[6:-1]
    groups = fields * levels

    def tile(group, t):
        f, l = group // levels, group % levels
        q, h = t // tiles_dev, t % tiles_dev
        parts = [
            circles_ref[q * sub + c, f, l, :, h * LANES : (h + 1) * LANES] for c in range(sub)
        ]
        return parts[0] if sub == 1 else jnp.concatenate(parts, axis=0)

    def root(k):
        c, s = twiddle_ref[k, 0], twiddle_ref[k, 1]
        if sub > 1:
            c, s = jnp.concatenate([c] * sub, axis=0), jnp.concatenate([s] * sub, axis=0)
        return c, s

    def spread(group, carry):
        start = pl.multiple_of(group * rows, 8)
        spectrum = real_forward([tile(group, t) for t in range(RADIX)])
        for k in range(HALF + 1):
            re, im = spectrum[k]
            if k == 0:
                re, im = re, jnp.zeros_like(re)
            else:
                c, s = root(k)
                if im is None:
                    re, im = re * c, -re * s
                else:
                    re, im = re * c + im * s, im * c - re * s
            waves_ref[k, pl.ds(start, rows), :LANES] = re
            waves_ref[k, pl.ds(start, rows), LANES:] = im
        return carry

    lax.fori_loop(0, groups, spread, 0)

    lane = lax.broadcasted_iota(jnp.int32, (rows, LANES), 1)
    high, low = high_ref[...], low_ref[...]
    for k in range(HALF + 1):
        wave = k + RADIX * lane
        wave = jnp.minimum(wave, CIRCLE - wave)
        kept = jnp.where(wave < cut_ref[...], 1.0 / CIRCLE, 0.0)
        weight = jnp.concatenate([kept, -kept], axis=1)
        spectra = split_dot(waves_ref[k], high, low)
        spectra = spectra.reshape(groups, rows, 2 * LANES) * weight[None]
        waves_ref[k] = split_dot(spectra.reshape(groups * rows, 2 * LANES), high, low)

    flagged = cut_ref[...] < KEEP_ALL

    def gather(group, carry):
        start = pl.multiple_of(group * rows, 8)
        f, l = group // levels, group % levels
        spectrum = []
        for k in range(HALF + 1):
            re = waves_ref[k, pl.ds(start, rows), :LANES]
            if k == 0:
                spectrum.append((re, None))
                continue
            im = waves_ref[k, pl.ds(start, rows), LANES:]
            c, s = root(k)
            spectrum.append((re * c + im * s, None if k == HALF else re * s - im * c))
        smooth = real_inverse(spectrum, RADIX)
        for t in range(RADIX):
            value = jnp.where(flagged, smooth[t], tile(group, t))
            own_ref[f, l, t] = value
            if sends:
                sends[0][group, t * halo : (t + 1) * halo, :] = value[:halo]
                sends[1][group, t * halo : (t + 1) * halo, :] = value[rows - halo :]
        return carry

    lax.fori_loop(0, groups, gather, 0)


def filtered(circles, cut, tables, sub, halo):
    sources, fields, levels, _, cols = circles.shape
    rows = 8 * sub
    high, low, twiddle = tables
    whole = pl.BlockSpec(memory_space=pltpu.VMEM)
    outs = [jax.ShapeDtypeStruct((fields, levels, RADIX, rows, LANES), jnp.float32)]
    if rows >= halo:
        packed = jax.ShapeDtypeStruct((fields * levels, RADIX * halo, LANES), jnp.float32)
        outs += [packed, packed]
    return pl.pallas_call(
        functools.partial(
            filter_kernel, (fields, levels, sub, rows, cols // LANES, halo)
        ),
        out_shape=outs,
        in_specs=[whole] * 5,
        out_specs=[whole] * len(outs),
        scratch_shapes=[pltpu.VMEM((HALF + 1, fields * levels * rows, 2 * LANES), jnp.float32)],
        compiler_params=pltpu.CompilerParams(vmem_limit_bytes=VMEM_BYTES),
        cost_estimate=pl.CostEstimate(flops=10**9, bytes_accessed=4 * 10**6, transcendentals=0),
        name="filter_circles",
    )(circles, cut, twiddle, high, low)


def exchanged(own, sends, halo):
    blocks = lax.axis_size("blk")
    fields, levels, tiles, rows, lanes = own.shape

    def moved(value, step):
        pairs = [(i, i + step) for i in range(blocks) if 0 <= i + step < blocks]
        return lax.ppermute(value, "blk", pairs)

    if sends:
        first, last = sends
        return moved(last, 1), moved(first, -1)
    hops = -(-halo // rows)
    above = jnp.concatenate([moved(own, h) for h in range(hops, 0, -1)], axis=3)
    below = jnp.concatenate([moved(own, -h) for h in range(1, hops + 1)], axis=3)
    packed = (fields * levels, tiles * halo, lanes)
    return above[:, :, :, hops * rows - halo :].reshape(packed), below[:, :, :, :halo].reshape(packed)


class Circle:
    def __init__(self, load):
        self.load = load
        self.cache = {}

    def rolled(self, t, offset):
        t = t % RADIX
        if (t, offset) not in self.cache:
            value = self.load(t)
            self.cache[t, offset] = (
                value if offset == 0 else pltpu.roll(value, (-offset) % LANES, 1)
            )
        return self.cache[t, offset]

    def at(self, t, offset, lane):
        here = self.rolled(t, offset)
        if offset > 0:
            return jnp.where(lane < LANES - offset, here, self.rolled(t + 1, offset))
        return jnp.where(lane >= -offset, here, self.rolled(t - 1, offset))


def upwind(wind, coef):
    u, a = -coef * wind, coef * jnp.abs(wind)
    return (
        [45.0 * u + 15.0 * a, 15.0 * a - 45.0 * u],
        [-9.0 * u - 6.0 * a, 9.0 * u - 6.0 * a],
        [u + a, a - u],
        -20.0 * a,
    )


def advected(field_ref, index, row, t, circle, lane, zonal, merid):
    (x1, x2, x3, x0), (y1, y2, y3, y0) = zonal, merid
    total = (x0 + y0) * circle.rolled(t, 0)
    for offset, (ahead, behind) in ((1, x1), (2, x2), (3, x3)):
        total += ahead * circle.at(t, offset, lane) + behind * circle.at(t, -offset, lane)
    for offset, (ahead, behind) in ((1, y1), (2, y2), (3, y3)):
        total += ahead * field_ref[index + (t, slice(row + offset, row + offset + 8), slice(None))]
        total += behind * field_ref[index + (t, slice(row - offset, row - offset + 8), slice(None))]
    return total


def assemble(ref, own_ref, above_ref, below_ref, level, halo):
    fields, levels, tiles, rows, _ = own_ref.shape
    for f in range(fields):
        for t in range(tiles):
            packed = slice(t * halo, (t + 1) * halo)
            ref[f, t, PAD - halo : PAD, :] = above_ref[f * levels + level, packed, :]
            ref[f, t, PAD : PAD + rows, :] = own_ref[f, level, t]
            ref[f, t, PAD + rows : PAD + rows + halo, :] = below_ref[f * levels + level, packed, :]


def put(out_ref, field, level, t, value, sub, tiles_dev):
    q, h = t // tiles_dev, t % tiles_dev
    for c in range(sub):
        out_ref[q * sub + c, field, level, :, h * LANES : (h + 1) * LANES] = value[8 * c : 8 * c + 8]


def section_kernel(dims, own_ref, above_ref, below_ref, coef_ref, out_ref, now_ref, tend_ref):
    levels, sub, rows, tiles_dev = dims
    lane = lax.broadcasted_iota(jnp.int32, (8, LANES), 1)
    y_coef = ADV_COEF / (60.0 * SUBSTEPS)
    end = PAD + rows

    def level_step(level, carry):
        assemble(now_ref, own_ref, above_ref, below_ref, level, WIND_HALO)

        for row in range(PAD - 8, end + 8, 8):
            here = slice(row, row + 8)
            circles = [
                Circle(lambda t, f=f: now_ref[f, t % RADIX, here, :]) for f in range(3)
            ]
            coef_x = coef_ref[0, here, :]
            for t in range(RADIX):
                zonal = upwind(circles[0].rolled(t, 0), coef_x)
                merid = upwind(circles[1].rolled(t, 0), y_coef)
                for f in range(3):
                    tend_ref[f, t, here, :] = advected(
                        now_ref, (f,), row, t, circles[f], lane, zonal, merid
                    )

        for step in range(SUBSTEPS):
            reach = 2 * (SUBSTEPS - step) - 1
            first = PAD - reach
            for row in range(first, end + reach, 8):
                here = slice(row, row + 8)
                circle = Circle(lambda t: now_ref[2, t % RADIX, here, :])
                grad_x, coriolis, grad_y = (coef_ref[i, here, :] for i in (1, 2, 3))
                for t in range(RADIX):
                    east, north = now_ref[0, t, here, :], now_ref[1, t, here, :]
                    dx = circle.at(t, 1, lane) - circle.at(t, -1, lane)
                    dy = now_ref[2, t, row + 1 : row + 9, :] - now_ref[2, t, row - 1 : row + 7, :]
                    east = east + (tend_ref[0, t, here, :] - grad_x * dx + coriolis * north)
                    north = north + (tend_ref[1, t, here, :] - grad_y * dy - coriolis * east)
                    now_ref[0, t, here, :] = east
                    now_ref[1, t, here, :] = north
            reach -= 1
            for row in range(PAD - reach, end + reach, 8):
                here = slice(row, row + 8)
                circle = Circle(lambda t: now_ref[0, t % RADIX, here, :])
                grad_x, grad_y = coef_ref[1, here, :], coef_ref[3, here, :]
                for t in range(RADIX):
                    dx = circle.at(t, 1, lane) - circle.at(t, -1, lane)
                    dy = now_ref[1, t, row + 1 : row + 9, :] - now_ref[1, t, row - 1 : row + 7, :]
                    now_ref[2, t, here, :] = now_ref[2, t, here, :] + (
                        tend_ref[2, t, here, :] - (grad_x * dx + grad_y * dy)
                    )

        for f in range(3):
            for t in range(RADIX):
                put(out_ref, f, level, t, now_ref[f, t, PAD:end, :], sub, tiles_dev)
        return carry

    lax.fori_loop(0, levels, level_step, 0)


def tracer_kernel(
    dims, wind_ref, wind_above, wind_below, own_ref, above_ref, below_ref, coef_ref, out_ref,
    now_ref, press_ref,
):
    levels, sub, rows, tiles_dev = dims
    lane = lax.broadcasted_iota(jnp.int32, (8, LANES), 1)
    y_coef = ADV_COEF / 60.0
    skip = WIND_HALO - TRACER_HALO

    def level_step(level, carry):
        assemble(now_ref, own_ref, above_ref, below_ref, level, TRACER_HALO)
        for t in range(RADIX):
            press_ref[t, PAD - TRACER_HALO : PAD, :] = wind_above[
                2 * levels + level, t * WIND_HALO + skip : (t + 1) * WIND_HALO, :
            ]
            press_ref[t, PAD : PAD + rows, :] = wind_ref[2, level, t]
            press_ref[t, PAD + rows : PAD + rows + TRACER_HALO, :] = wind_below[
                2 * levels + level, t * WIND_HALO : t * WIND_HALO + TRACER_HALO, :
            ]
        for row in range(PAD, PAD + rows, 8):
            here = slice(row, row + 8)
            block = slice(row - PAD, row - PAD + 8)
            circles = [
                Circle(lambda t, f=f: now_ref[f, t % RADIX, here, :]) for f in range(2)
            ]
            press = Circle(lambda t: press_ref[t % RADIX, here, :])
            coef_x = coef_ref[0, here, :] * SUBSTEPS
            for t in range(RADIX):
                zonal = upwind(wind_ref[0, level, t, block, :], coef_x)
                merid = upwind(wind_ref[1, level, t, block, :], y_coef)
                temp, moist = (
                    circles[f].rolled(t, 0)
                    + advected(now_ref, (f,), row, t, circles[f], lane, zonal, merid)
                    for f in range(2)
                )
                free = press.rolled(t, 0) + advected(press_ref, (), row, t, press, lane, zonal, merid)
                q, h = t // tiles_dev, t % tiles_dev
                place = (q * sub + (row - PAD) // 8,)
                lanes = slice(h * LANES, (h + 1) * LANES)
                out_ref[place + (0, level, slice(None), lanes)] = temp - THETA_DIV * free
                out_ref[place + (1, level, slice(None), lanes)] = moist
        return carry

    lax.fori_loop(0, levels, level_step, 0)


def kernel_call(body, dims, shape, scratch, name, *args):
    whole = pl.BlockSpec(memory_space=pltpu.VMEM)
    return pl.pallas_call(
        functools.partial(body, dims),
        out_shape=jax.ShapeDtypeStruct(shape, jnp.float32),
        in_specs=[whole] * len(args),
        out_specs=whole,
        scratch_shapes=[pltpu.VMEM(s, jnp.float32) for s in scratch],
        compiler_params=pltpu.CompilerParams(vmem_limit_bytes=VMEM_BYTES),
        cost_estimate=pl.CostEstimate(flops=10**8, bytes_accessed=4 * 10**6, transcendentals=0),
        name=name,
    )(*args)


def shards(tables, east, north, temp, press, moist, map_factor, filter_rows, filter_cutoff):
    levels_all, rows_dev, cols = east.shape
    lon_count, blocks, sub = (lax.axis_size(a) for a in ("lon", "blk", "sub"))
    block = lax.axis_index("blk")
    peers = lon_count * sub
    levels = levels_all // peers
    rows = rows_dev * sub
    total_rows = rows * blocks
    group = ("lon", "sub")

    ring = jnp.arange(rows + 2 * PAD, dtype=jnp.int32) + block * rows - PAD
    inside = (ring >= 0) & (ring < total_rows)
    maps = lax.all_gather(map_factor, ("blk", "sub"), tiled=True)
    maps = jnp.concatenate([maps[:PAD], maps, maps[:PAD]])
    maps = lax.dynamic_slice(maps, (block * rows,), (rows + 2 * PAD,))
    latitude = -0.5 * math.pi + (ring.astype(jnp.float32) + 0.5) * (math.pi / total_rows)
    tau = 1.0 / SUBSTEPS
    coefs = jnp.stack(
        [
            (tau * ADV_COEF / 60.0) * maps,
            (tau * SOUND * 0.5) * maps,
            (tau * 0.5) * jnp.sin(latitude),
            jnp.where(inside, tau * SOUND * 0.5, 0.0),
        ]
    )
    coefs = jnp.broadcast_to(coefs[:, :, None], coefs.shape + (LANES,))

    local = jnp.arange(rows, dtype=jnp.int32) + block * rows
    matches = filter_rows[:, None] == local[None, :]
    cut = jnp.sum(jnp.where(matches, filter_cutoff[:, None], 0), axis=0)
    cut = jnp.where(jnp.any(matches, axis=0), cut, KEEP_ALL)
    cut = jnp.broadcast_to(cut[:, None], (rows, LANES))

    def to_circles(fields):
        stacked = jnp.stack([f.reshape(peers, levels, rows_dev, cols) for f in fields], axis=1)
        return lax.all_to_all(stacked, group, split_axis=0, concat_axis=0, tiled=True)

    def to_blocks(value):
        back = lax.all_to_all(value, group, split_axis=0, concat_axis=0, tiled=True)
        return [back[:, i].reshape(levels_all, rows_dev, cols) for i in range(value.shape[1])]

    dims = (levels, sub, rows, cols // LANES)
    winds, *wind_sends = filtered(to_circles((east, north, press)), cut, tables, sub, WIND_HALO)
    tracers, *tracer_sends = filtered(to_circles((temp, moist)), cut, tables, sub, TRACER_HALO)
    wind_halos = exchanged(winds, wind_sends, WIND_HALO)
    tracer_halos = exchanged(tracers, tracer_sends, TRACER_HALO)

    tall = rows + 2 * PAD
    tracer_out = kernel_call(
        tracer_kernel,
        dims,
        (peers, 2, levels, rows_dev, cols),
        [(2, RADIX, tall, LANES), (RADIX, tall, LANES)],
        "advect_tracers",
        winds, *wind_halos, tracers, *tracer_halos, coefs,
    )
    part_temp, new_moist = to_blocks(tracer_out)
    wind_out = kernel_call(
        section_kernel,
        dims,
        (peers, 3, levels, rows_dev, cols),
        [(3, RADIX, tall, LANES), (3, RADIX, tall, LANES)],
        "acoustic_section",
        winds, *wind_halos, coefs,
    )
    new_east, new_north, new_press = to_blocks(wind_out)
    return (new_east, new_north, part_temp + THETA_DIV * new_press, new_press, new_moist)


def solution(mesh):
    lon, lat = mesh.shape["lon"], mesh.shape["lat"]
    tables = transform_tables()

    def section(*args):
        levels = args[0].shape[0]
        sub = 2 if lat % 2 == 0 and levels % (2 * lon) == 0 else 1
        finer = Mesh(mesh.devices.reshape(lon, lat // sub, sub), ("lon", "blk", "sub"))
        field = P(None, ("blk", "sub"), "lon")
        return jax.shard_map(
            functools.partial(shards, tables),
            mesh=finer,
            in_specs=(field,) * 5 + (P(("blk", "sub")), P(), P()),
            out_specs=(field,) * 5,
            check_vma=False,
        )(*args)

    return section
```

time: 500 us -> 97.4 us (0.19); the launches traced: 494 us -> 96.7 us
  matrix products: 169 us -> 0 us
  other arithmetic: 136 us -> 4.81 us
  starting transfers between devices: 99.5 us -> 24.7 us
  waiting for transfers between devices: 65.2 us -> 30.4 us
  blocking collectives: 0 us -> 17.2 us
  local copies, waits for them, and re-layouts: 23.2 us -> 6.49 us
  Pallas kernels: 0 us -> 11.7 us
    dot_general x10 -> x0, matrix products: 169 us -> none  [the longest x5 92.3 us: filter_circles(): lax.dot_general(spectra, table, (((1,), (1,)), ((), ())), precision=lax.P...]
    ppermute x36 -> x4, waiting for transfers between devices: 55.1 us -> 4.53 us  [moved(): return lax.ppermute(value, 'blk', pairs)]
    ppermute x36 -> x4, starting transfers between devices: 56.6 us -> 8.46 us  [moved(): return lax.ppermute(value, 'blk', pairs)]
    unnamed x7 -> x0, other arithmetic: 46.9 us -> none
    cos x1 -> x0, other arithmetic: 35.4 us -> none  [wave_table(): table = jnp.concatenate([jnp.cos(cos_angles), jnp.sin(sin_angles)], axis=1)]
    sin x1 -> x0, other arithmetic: 32 us -> none  [wave_table(): table = jnp.concatenate([jnp.cos(cos_angles), jnp.sin(sin_angles)], axis=1)]
    all_to_all x10 -> x4, starting transfers between devices: 43 us -> 16.2 us  [the longest x2 8.79 us: to_circles(): lax.all_to_all(stacked, group, split_axis=0, concat_axis=0, tiled=True)]
    unnamed x0 -> x1, blocking collectives: none -> 17.2 us
  transfers between devices with their start and end apart: 46 -> 8, of which waited for: 23 -> 5; matrix products, arithmetic and copies ran while one was open for 63% -> 4% of each run, Pallas kernels for 0% -> 10%
where the time goes in v1:
time: 97.4 us; the launch traced here: 96.7 us
  waiting for transfers between devices  30.4 us (31%)
  starting transfers between devices  24.7 us (25%)
  blocking collectives  17.2 us (18%)
  Pallas kernels  11.7 us (12%)
  local copies, waits for them, and re-layouts  6.49 us (7%)
  other arithmetic  4.81 us (5%)
  between operations  1.46 us (1%)
    unnamed x1, blocking collectives  17.2 us
    all_to_all x2, waiting for transfers between devices, to_blocks(): back = lax.all_to_all(value, group, split_axis=0, concat_axis=0, tiled=True)  15.7 us
    all_to_all x2, waiting for transfers between devices, to_circles(): lax.all_to_all(stacked, group, split_axis=0, concat_axis=0, tiled=True)  10.2 us
    all_to_all x2, starting transfers between devices, to_circles(): lax.all_to_all(stacked, group, split_axis=0, concat_axis=0, tiled=True)  8.79 us
    ppermute x4, starting transfers between devices, moved(): return lax.ppermute(value, 'blk', pairs)  8.46 us
    pallas_call x2, Pallas kernels, kernel_call(): pl.pallas_call(functools.partial(body, dims), out_shape=jax.ShapeDtypeStr...  8.11 us
    all_to_all x2, starting transfers between devices, to_blocks(): back = lax.all_to_all(value, group, split_axis=0, concat_axis=0, tiled=True)  7.42 us
    unnamed x29, local copies, waits for them, and re-layouts  4.74 us
  transfers between devices with their start and end apart: 8, of which 5 were waited for; matrix products, arithmetic and copies ran while one was open for 4% of the time, Pallas kernels for 10%

profile of v1, /device:TPU:0, one launch (start us, length us, event | category | flops | bytes accessed | tf_op | source)
XLA Modules:
  0.0 96.7 jit_solution(14999480633377625725)
XLA Ops:
  0.6 2.1 %pad_maximum_fusion = f32[8,3,2,8,512]{4,3,2,1,0:T(8,128)} fusion(f32[8,1,2,8,512]{4,3,2,1,0:T(8,128)} %bitcast.19, f32[8,1,2,8,512]{4,3,2,1,0:T(8,128)} %bitcast.20, f32[8,1,2,8,512]{4,3,2,1,0:T(8,128)} %bitcast.21), kind=kLoop, calls=%fused_computation | loop fusion | flops 393216 | bytes 1572864 | tf_op jit(solution)/shard_map/stack | solution.py:435
  2.7 5.3 %all-to-all-start = ((f32[8,3,2,8,512]{4,3,2,1,0:T(8,128)}), f32[8,3,2,8,512]{4,3,2,1,0:T(8,128)S(1)}, u32[]{:S(2)}, u32[]{:S(2)}) async-start(f32[8,3,2,8,512]{4,3,2,1,0:T(8,128)} %pad_maximum_fusion), calls=%async_computation | async-start | bytes 1572864 | tf_op jit(solution)/shard_map/all_to_all | solution.py:436
  9.5 0.8 pad_maximum_fusion.1
  10.4 10.2 %all-to-all-done.refs_0_ = f32[8,3,2,8,512]{4,3,2,1,0:T(8,128)S(1)} async-done(((f32[8,3,2,8,512]{4,3,2,1,0:T(8,128)}), f32[8,3,2,8,512]{4,3,2,1,0:T(8,128)S(1)}, u32[]{:S(2)}, u32[]{:S(2)}) %all-to-all-start) | async-done | bytes 786464 | tf_op jit(solution)/shard_map/all_to_all | solution.py:436
  20.6 3.5 %all-to-all-start.2 = ((f32[8,2,2,8,512]{4,3,2,1,0:T(8,128)}), f32[8,2,2,8,512]{4,3,2,1,0:T(8,128)S(1)}, u32[]{:S(2)}, u32[]{:S(2)}) async-start(f32[8,2,2,8,512]{4,3,2,1,0:T(8,128)} %pad_maximum_fusion.1), calls=%async_computation.2 | async-start | bytes 1048576 | tf_op jit(solution)/shard_map/all_to_all | solution.py:436
  24.2 0.6 copy-done.12
  26.9 17.2 %all-reduce = f32[64]{0:T(128)S(1)} all-reduce(f32[64]{0:T(128)S(1)} %dynamic-update-slice), channel_id=1, replica_groups=mesh['lon'=4,'blk'=4,'sub'=2] {'blk','sub'}, use_global_device_ids=true, to_apply=%add | all-reduce | flops 64 | bytes 512
  44.1 1.9 %filter_circles.2 = (f32[3,2,16,16,128]{4,3,2,1,0:T(8,128)S(1)}, f32[6,160,128]{2,1,0:T(8,128)S(1)}, f32[6,160,128]{2,1,0:T(8,128)S(1)}) custom-call(f32[8,3,2,8,512]{4,3,2,1,0:T(8,128)S(1)} %all-to-all-done.refs_0_, s32[16,128]{1,0:T(8,128)S(1)} %broadcast_in_dim.40.refs_1_, f32[9,2,8,128]{3,2,1,0:T(8,128)S(1)} %copy-done.2, bf16[256,256]{1,0:T(8,128)(2,1)S(1)} %copy-done, ...), custom_call_target="tpu_custom_call" | custom-call | flops 1000000000 | bytes 4000000 | tf_op jit(solution)/shard_map/filter_circles/pallas_call | solution.py:193
  46.0 1.3 %collective-permute-start = (f32[6,160,128]{2,1,0:T(8,128)S(1)}, f32[6,160,128]{2,1,0:T(8,128)S(1)}, u32[]{:S(2)}, u32[]{:S(2)}) collective-permute-start(f32[6,160,128]{2,1,0:T(8,128)S(1)} %get-tuple-element.12), channel_id=1, source_target_pairs={{0,2},{2,4},{4,6},{1,3},{3,5},{5,7},{8,10},{10,12},{12,14},{9,11},... | collective-permute-start | bytes 1474568 | tf_op jit(solution)/shard_map/ppermute | solution.py:213
  47.4 1.3 %collective-permute-start.1 = (f32[6,160,128]{2,1,0:T(8,128)S(1)}, f32[6,160,128]{2,1,0:T(8,128)S(1)}, u32[]{:S(2)}, u32[]{:S(2)}) collective-permute-start(f32[6,160,128]{2,1,0:T(8,128)S(1)} %get-tuple-element.13), channel_id=1, source_target_pairs={{2,0},{4,2},{6,4},{3,1},{5,3},{7,5},{10,8},{12,10},{14,12},{11,9},... | collective-permute-start | bytes 1474568 | tf_op jit(solution)/shard_map/ppermute | solution.py:213
  49.4 0.9 copy-done.3
  50.3 1.7 %filter_circles.3 = (f32[2,2,16,16,128]{4,3,2,1,0:T(8,128)S(1)}, f32[4,48,128]{2,1,0:T(8,128)S(1)}, f32[4,48,128]{2,1,0:T(8,128)S(1)}) custom-call(f32[8,2,2,8,512]{4,3,2,1,0:T(8,128)S(1)} %all-to-all-done.2.refs_0_, s32[16,128]{1,0:T(8,128)S(1)} %broadcast_in_dim.40.refs_1_, f32[9,2,8,128]{3,2,1,0:T(8,128)S(1)} %copy-done.3, bf16[256,256]{1,0:T(8,128)(2,1)S(1)} %copy-done, ...), custom_call_target="tpu_custom_call" | custom-call | flops 1000000000 | bytes 4000000 | tf_op jit(solution)/shard_map/filter_circles/pallas_call | solution.py:193
  52.0 4.6 %collective-permute-start.2 = (f32[4,48,128]{2,1,0:T(8,128)S(1)}, f32[4,48,128]{2,1,0:T(8,128)S(1)}, u32[]{:S(2)}, u32[]{:S(2)}) collective-permute-start(f32[4,48,128]{2,1,0:T(8,128)S(1)} %get-tuple-element.15), channel_id=1, source_target_pairs={{0,2},{2,4},{4,6},{1,3},{3,5},{5,7},{8,10},{10,12},{12,14},{9,11},... | collective-permute-start | bytes 294920 | tf_op jit(solution)/shard_map/ppermute | solution.py:213
  56.5 1.3 %collective-permute-start.3 = (f32[4,48,128]{2,1,0:T(8,128)S(1)}, f32[4,48,128]{2,1,0:T(8,128)S(1)}, u32[]{:S(2)}, u32[]{:S(2)}) collective-permute-start(f32[4,48,128]{2,1,0:T(8,128)S(1)} %get-tuple-element.16), channel_id=1, source_target_pairs={{2,0},{4,2},{6,4},{3,1},{5,3},{7,5},{10,8},{12,10},{14,12},{11,9},... | collective-permute-start | bytes 294920 | tf_op jit(solution)/shard_map/ppermute | solution.py:213
  58.7 4.3 %collective-permute-done.3.below_ref = f32[4,48,128]{2,1,0:T(8,128)S(1)} collective-permute-done((f32[4,48,128]{2,1,0:T(8,128)S(1)}, f32[4,48,128]{2,1,0:T(8,128)S(1)}, u32[]{:S(2)}, u32[]{:S(2)}) %collective-permute-start.3) | collective-permute-done | bytes 98336 | tf_op jit(solution)/shard_map/ppermute | solution.py:213
  63.1 2.2 %advect_tracers.1 = f32[8,2,2,8,512]{4,3,2,1,0:T(8,128)} custom-call(f32[3,2,16,16,128]{4,3,2,1,0:T(8,128)S(1)} %get-tuple-element.11.own_ref.wind_ref, f32[6,160,128]{2,1,0:T(8,128)S(1)} %collective-permute-done.above_ref.wind_above, f32[6,160,128]{2,1,0:T(8,128)S(1)} %collective-permute-done.1.below_ref.wind_below, ...), custom_call_target="tpu_custom_call" | custom-call | flops 100000000 | bytes 4000000 | tf_op jit(solution)/shard_map/advect_tracers/pallas_call | solution.py:389
  65.4 3.9 %all-to-all-start.3 = ((f32[8,2,2,8,512]{4,3,2,1,0:T(8,128)}), f32[8,2,2,8,512]{4,3,2,1,0:T(8,128)S(1)}, u32[]{:S(2)}, u32[]{:S(2)}) async-start(f32[8,2,2,8,512]{4,3,2,1,0:T(8,128)} %advect_tracers.1), calls=%async_computation.3 | async-start | bytes 1048576 | tf_op jit(solution)/shard_map/all_to_all | solution.py:439
  69.3 5.9 %acoustic_section.1 = f32[8,3,2,8,512]{4,3,2,1,0:T(8,128)} custom-call(f32[3,2,16,16,128]{4,3,2,1,0:T(8,128)S(1)} %get-tuple-element.11.own_ref.wind_ref, f32[6,160,128]{2,1,0:T(8,128)S(1)} %collective-permute-done.above_ref.wind_above, f32[6,160,128]{2,1,0:T(8,128)S(1)} %collective-permute-done.1.below_ref.wind_below, ...), custom_call_target="tpu_custom_call" | custom-call | flops 100000000 | bytes 4000000 | tf_op jit(solution)/shard_map/acoustic_section/pallas_call | solution.py:389
  75.1 3.9 %all-to-all-done.3 = f32[8,2,2,8,512]{4,3,2,1,0:T(8,128)S(1)} async-done(((f32[8,2,2,8,512]{4,3,2,1,0:T(8,128)}), f32[8,2,2,8,512]{4,3,2,1,0:T(8,128)S(1)}, u32[]{:S(2)}, u32[]{:S(2)}) %all-to-all-start.3) | async-done | bytes 524320 | tf_op jit(solution)/shard_map/all_to_all | solution.py:439
  79.0 3.5 %all-to-all-start.1 = ((f32[8,3,2,8,512]{4,3,2,1,0:T(8,128)}), f32[8,3,2,8,512]{4,3,2,1,0:T(8,128)S(1)}, u32[]{:S(2)}, u32[]{:S(2)}) async-start(f32[8,3,2,8,512]{4,3,2,1,0:T(8,128)} %acoustic_section.1), calls=%async_computation.1 | async-start | bytes 1572864 | tf_op jit(solution)/shard_map/all_to_all | solution.py:439
  82.6 0.7 fusion.2
  83.3 11.8 %all-to-all-done.1 = f32[8,3,2,8,512]{4,3,2,1,0:T(8,128)S(1)} async-done(((f32[8,3,2,8,512]{4,3,2,1,0:T(8,128)}), f32[8,3,2,8,512]{4,3,2,1,0:T(8,128)S(1)}, u32[]{:S(2)}, u32[]{:S(2)}) %all-to-all-start.1) | async-done | bytes 786464 | tf_op jit(solution)/shard_map/all_to_all | solution.py:439
  95.1 0.9 fusion.1
  95.9 0.8 bitcast_add_fusion
  (41 shorter events, 4.7 us)
Async XLA Ops:
  2.7 6.8 %copy-start.5 = (f32[16,8,512]{2,1,0:T(8,128)S(1)}, f32[16,8,512]{2,1,0:T(8,128)}, u32[]{:S(2)}) copy-start(f32[16,8,512]{2,1,0:T(8,128)} %param.15) | copy-start | bytes 786436
  2.7 6.8 %copy-start.6 = (f32[16,8,512]{2,1,0:T(8,128)S(1)}, f32[16,8,512]{2,1,0:T(8,128)}, u32[]{:S(2)}) copy-start(f32[16,8,512]{2,1,0:T(8,128)} %param.13) | copy-start | bytes 786436
  2.7 17.9 %all-to-all-start = ((f32[8,3,2,8,512]{4,3,2,1,0:T(8,128)}), f32[8,3,2,8,512]{4,3,2,1,0:T(8,128)S(1)}, u32[]{:S(2)}, u32[]{:S(2)}) async-start(f32[8,3,2,8,512]{4,3,2,1,0:T(8,128)} %pad_maximum_fusion), calls=%async_computation | async-start | bytes 1572864 | tf_op jit(solution)/shard_map/all_to_all | solution.py:436
  8.0 0.7 copy-start.7
  8.7 0.7 copy-start.8
  10.4 33.7 %copy-start = (bf16[256,256]{1,0:T(8,128)(2,1)S(1)}, bf16[256,256]{1,0:T(8,128)(2,1)}, u32[]{:S(2)}) copy-start(bf16[256,256]{1,0:T(8,128)(2,1)} %constant.46.clone.refs_3_) | copy-start | bytes 393220
  10.4 33.7 %copy-start.1 = (bf16[256,256]{1,0:T(8,128)(2,1)S(1)}, bf16[256,256]{1,0:T(8,128)(2,1)}, u32[]{:S(2)}) copy-start(bf16[256,256]{1,0:T(8,128)(2,1)} %constant.47.clone.refs_4_) | copy-start | bytes 393220
  10.4 33.7 %copy-start.2 = (f32[9,2,8,128]{3,2,1,0:T(8,128)S(1)}, f32[9,2,8,128]{3,2,1,0:T(8,128)}, u32[]{:S(2)}) copy-start(f32[9,2,8,128]{3,2,1,0:T(8,128)} %constant.45.clone.refs_2_) | copy-start | bytes 221188
  20.6 28.8 %all-to-all-start.2 = ((f32[8,2,2,8,512]{4,3,2,1,0:T(8,128)}), f32[8,2,2,8,512]{4,3,2,1,0:T(8,128)S(1)}, u32[]{:S(2)}, u32[]{:S(2)}) async-start(f32[8,2,2,8,512]{4,3,2,1,0:T(8,128)} %pad_maximum_fusion.1), calls=%async_computation.2 | async-start | bytes 1048576 | tf_op jit(solution)/shard_map/all_to_all | solution.py:436
  24.1 0.7 copy-start.12
  26.0 0.7 copy-start.11
  46.0 17.0 %collective-permute-start = (f32[6,160,128]{2,1,0:T(8,128)S(1)}, f32[6,160,128]{2,1,0:T(8,128)S(1)}, u32[]{:S(2)}, u32[]{:S(2)}) collective-permute-start(f32[6,160,128]{2,1,0:T(8,128)S(1)} %get-tuple-element.12), channel_id=1, source_target_pairs={{0,2},{2,4},{4,6},{1,3},{3,5},{5,7},{8,10},{10,12},{12,14},{9,11},... | collective-permute-start | bytes 1474568 | tf_op jit(solution)/shard_map/ppermute | solution.py:213
  47.4 15.7 %collective-permute-start.1 = (f32[6,160,128]{2,1,0:T(8,128)S(1)}, f32[6,160,128]{2,1,0:T(8,128)S(1)}, u32[]{:S(2)}, u32[]{:S(2)}) collective-permute-start(f32[6,160,128]{2,1,0:T(8,128)S(1)} %get-tuple-element.13), channel_id=1, source_target_pairs={{2,0},{4,2},{6,4},{3,1},{5,3},{7,5},{10,8},{12,10},{14,12},{11,9},... | collective-permute-start | bytes 1474568 | tf_op jit(solution)/shard_map/ppermute | solution.py:213
  49.4 0.9 copy-start.3
  52.0 6.8 %collective-permute-start.2 = (f32[4,48,128]{2,1,0:T(8,128)S(1)}, f32[4,48,128]{2,1,0:T(8,128)S(1)}, u32[]{:S(2)}, u32[]{:S(2)}) collective-permute-start(f32[4,48,128]{2,1,0:T(8,128)S(1)} %get-tuple-element.15), channel_id=1, source_target_pairs={{0,2},{2,4},{4,6},{1,3},{3,5},{5,7},{8,10},{10,12},{12,14},{9,11},... | collective-permute-start | bytes 294920 | tf_op jit(solution)/shard_map/ppermute | solution.py:213
  56.5 6.5 %collective-permute-start.3 = (f32[4,48,128]{2,1,0:T(8,128)S(1)}, f32[4,48,128]{2,1,0:T(8,128)S(1)}, u32[]{:S(2)}, u32[]{:S(2)}) collective-permute-start(f32[4,48,128]{2,1,0:T(8,128)S(1)} %get-tuple-element.16), channel_id=1, source_target_pairs={{2,0},{4,2},{6,4},{3,1},{5,3},{7,5},{10,8},{12,10},{14,12},{11,9},... | collective-permute-start | bytes 294920 | tf_op jit(solution)/shard_map/ppermute | solution.py:213
  57.8 0.7 copy-start.9
  57.8 0.7 copy-start.10
  65.4 13.6 %all-to-all-start.3 = ((f32[8,2,2,8,512]{4,3,2,1,0:T(8,128)}), f32[8,2,2,8,512]{4,3,2,1,0:T(8,128)S(1)}, u32[]{:S(2)}, u32[]{:S(2)}) async-start(f32[8,2,2,8,512]{4,3,2,1,0:T(8,128)} %advect_tracers.1), calls=%async_computation.3 | async-start | bytes 1048576 | tf_op jit(solution)/shard_map/all_to_all | solution.py:439
  79.0 16.1 %all-to-all-start.1 = ((f32[8,3,2,8,512]{4,3,2,1,0:T(8,128)}), f32[8,3,2,8,512]{4,3,2,1,0:T(8,128)S(1)}, u32[]{:S(2)}, u32[]{:S(2)}) async-start(f32[8,3,2,8,512]{4,3,2,1,0:T(8,128)} %acoustic_section.1), calls=%async_computation.1 | async-start | bytes 1572864 | tf_op jit(solution)/shard_map/all_to_all | solution.py:439
  95.9 0.8 copy-start.4

commit v2 on v1

v2 whole, which is shorter than its diff:
```python
import functools
import math

import jax
import jax.numpy as jnp
import numpy as np
from jax import lax
from jax.experimental import pallas as pl
from jax.experimental.pallas import tpu as pltpu
from jax.sharding import Mesh
from jax.sharding import PartitionSpec as P

SUBSTEPS = 4
ADV_COEF = 0.1
SOUND = 0.4
THETA_DIV = 0.3

LANES = 128
RADIX = 16
HALF = RADIX // 2
CIRCLE = LANES * RADIX
WIND_HALO = 10
TRACER_HALO = 3
PAD = 16
KEEP_ALL = 1 << 20
VMEM_BYTES = 32 * 1024 * 1024


def transform_tables():
    lane = np.arange(LANES)
    angle = 2.0 * np.pi * np.outer(lane, lane) / LANES
    cos, sin = np.cos(angle), np.sin(angle)
    matrix = np.block([[cos, -sin], [sin, cos]]).astype(np.float32)
    high = matrix.astype(jnp.bfloat16)
    low = (matrix - high.astype(np.float32)).astype(jnp.bfloat16)
    turn = 2.0 * np.pi * np.outer(np.arange(HALF + 1), lane) / CIRCLE
    twiddle = np.stack([np.cos(turn), np.sin(turn)], axis=1).astype(np.float32)
    twiddle = np.broadcast_to(twiddle[:, :, None, :], (HALF + 1, 2, 8, LANES))
    return high, low, np.ascontiguousarray(twiddle)


def times_root(value, step, size, sign):
    re, im = value
    if step == 0:
        return value
    if 4 * step == size:
        if im is None:
            return (jnp.zeros_like(re), re if sign > 0 else -re)
        return (-im, re) if sign > 0 else (im, -re)
    c = math.cos(2.0 * math.pi * step / size)
    s = sign * math.sin(2.0 * math.pi * step / size)
    if im is None:
        return (re * c, re * s)
    return (re * c - im * s, re * s + im * c)


def added(a, b):
    im = a[1] if b[1] is None else b[1] if a[1] is None else a[1] + b[1]
    return (a[0] + b[0], im)


def taken(a, b):
    im = a[1] if b[1] is None else -b[1] if a[1] is None else a[1] - b[1]
    return (a[0] - b[0], im)


def conj(a):
    return (a[0], None if a[1] is None else -a[1])


def real_forward(values):
    size = len(values)
    if size == 1:
        return [(values[0], None)]
    even, odd = real_forward(values[0::2]), real_forward(values[1::2])
    out = [None] * (size // 2 + 1)
    for k in range(size // 4 + 1):
        turned = times_root(odd[k], k, size, -1)
        out[k] = added(even[k], turned)
        if k != size // 2 - k:
            out[size // 2 - k] = conj(taken(even[k], turned))
    return out


def real_inverse(spectrum, size):
    if size == 1:
        return [spectrum[0][0]]
    even, odd = [], []
    for k in range(size // 4 + 1):
        mirror = conj(spectrum[size // 2 - k])
        even.append(added(spectrum[k], mirror))
        odd.append(times_root(taken(spectrum[k], mirror), k, size, 1))
    out = [None] * size
    out[0::2] = real_inverse(even, size // 2)
    out[1::2] = real_inverse(odd, size // 2)
    return out


def split_dot(values, high, low):
    top = values.astype(jnp.bfloat16)
    rest = (values - top.astype(jnp.float32)).astype(jnp.bfloat16)
    dot = functools.partial(jnp.dot, preferred_element_type=jnp.float32)
    return dot(top, high) + (dot(rest, high) + dot(top, low))


def tile_rows(group, h, tiles_dev):
    return pl.ds(pl.multiple_of((group * tiles_dev + h) * 8, 8), 8)


def pack_kernel(*refs):
    *field_refs, out_ref = refs
    maps_ref = None
    if len(field_refs[-1].shape) == 2:
        *field_refs, maps_ref = field_refs
    peers, levels, _, cols = field_refs[0].shape
    tiles_dev = cols // LANES
    for f, ref in enumerate(field_refs):
        for l in range(levels):
            for h in range(tiles_dev):
                out_ref[:, tile_rows(f * levels + l, h, tiles_dev), :] = ref[
                    :, l, :, h * LANES : (h + 1) * LANES
                ]
    if maps_ref is not None:
        size = out_ref.shape[1]
        out_ref[:, size - 8 : size, :] = jnp.broadcast_to(maps_ref[...][None], (peers, 8, LANES))


def unpack_kernel(in_ref, *field_refs):
    _, levels, _, cols = field_refs[0].shape
    tiles_dev = cols // LANES
    for f, ref in enumerate(field_refs):
        for l in range(levels):
            for h in range(tiles_dev):
                ref[:, l, :, h * LANES : (h + 1) * LANES] = in_ref[
                    :, tile_rows(f * levels + l, h, tiles_dev), :
                ]


def filter_kernel(dims, *refs):
    fields, levels, sub, rows, tiles_dev, halo, with_maps = dims
    circles_ref, cut_ref, twiddle_ref, high_ref, low_ref = refs[:5]
    own_ref, *refs = refs[5:]
    waves_ref = refs.pop()
    maps_ref = refs.pop(0) if with_maps else None
    sends = refs
    groups = fields * levels
    wide = groups * RADIX * halo

    if with_maps:
        size = circles_ref.shape[1]
        for c in range(sub):
            value = circles_ref[c, size - 8 : size, :]
            maps_ref[8 * c : 8 * c + 8, :] = value
            for ref in sends:
                ref[wide + 8 * c : wide + 8 * c + 8, :] = value

    def tile(group, t):
        q, h = t // tiles_dev, t % tiles_dev
        parts = [
            circles_ref[q * sub + c, tile_rows(group, h, tiles_dev), :] for c in range(sub)
        ]
        return parts[0] if sub == 1 else jnp.concatenate(parts, axis=0)

    def root(k):
        c, s = twiddle_ref[k, 0], twiddle_ref[k, 1]
        if sub > 1:
            c, s = jnp.concatenate([c] * sub, axis=0), jnp.concatenate([s] * sub, axis=0)
        return c, s

    def spread(group, carry):
        start = pl.multiple_of(group * rows, 8)
        spectrum = real_forward([tile(group, t) for t in range(RADIX)])
        for k in range(HALF + 1):
            re, im = spectrum[k]
            if k == 0:
                re, im = re, jnp.zeros_like(re)
            else:
                c, s = root(k)
                if im is None:
                    re, im = re * c, -re * s
                else:
                    re, im = re * c + im * s, im * c - re * s
            waves_ref[k, pl.ds(start, rows), :LANES] = re
            waves_ref[k, pl.ds(start, rows), LANES:] = im
        return carry

    lax.fori_loop(0, groups, spread, 0)

    lane = lax.broadcasted_iota(jnp.int32, (rows, LANES), 1)
    high, low = high_ref[...], low_ref[...]
    for k in range(HALF + 1):
        wave = k + RADIX * lane
        wave = jnp.minimum(wave, CIRCLE - wave)
        kept = jnp.where(wave < cut_ref[...], 1.0 / CIRCLE, 0.0)
        weight = jnp.concatenate([kept, -kept], axis=1)
        spectra = split_dot(waves_ref[k], high, low)
        spectra = spectra.reshape(groups, rows, 2 * LANES) * weight[None]
        waves_ref[k] = split_dot(spectra.reshape(groups * rows, 2 * LANES), high, low)

    flagged = cut_ref[...] < KEEP_ALL

    def gather(group, carry):
        start = pl.multiple_of(group * rows, 8)
        f, l = group // levels, group % levels
        spectrum = []
        for k in range(HALF + 1):
            re = waves_ref[k, pl.ds(start, rows), :LANES]
            if k == 0:
                spectrum.append((re, None))
                continue
            im = waves_ref[k, pl.ds(start, rows), LANES:]
            c, s = root(k)
            spectrum.append((re * c + im * s, None if k == HALF else re * s - im * c))
        smooth = real_inverse(spectrum, RADIX)
        for t in range(RADIX):
            value = jnp.where(flagged, smooth[t], tile(group, t))
            own_ref[f, l, t] = value
            if sends:
                part = pl.ds(pl.multiple_of(group * RADIX * halo, 8), RADIX * halo)
                place = slice(t * halo, (t + 1) * halo)
                sends[0].at[part][place, :] = value[:halo]
                sends[1].at[part][place, :] = value[rows - halo :]
        return carry

    lax.fori_loop(0, groups, gather, 0)


def filtered(circles, cut, tables, fields, levels, sub, halo, with_maps):
    rows = 8 * sub
    tiles_dev = RADIX * sub // circles.shape[0]
    high, low, twiddle = tables
    outs = [(fields, levels, RADIX, rows, LANES)]
    if with_maps:
        outs.append((rows, LANES))
    if rows >= halo:
        outs += [(fields * levels * RADIX * halo + with_maps * rows, LANES)] * 2
    own, *rest = kernel_call(
        functools.partial(filter_kernel, (fields, levels, sub, rows, tiles_dev, halo, with_maps)),
        outs,
        [(HALF + 1, fields * levels * rows, 2 * LANES)],
        "filter_circles",
        circles, cut, twiddle, high, low,
    )
    maps = rest.pop(0) if with_maps else None
    return own, maps, rest


def exchanged(own, maps, sends, halo):
    blocks = lax.axis_size("blk")
    rows = own.shape[3]

    def moved(value, step):
        pairs = [(i, i + step) for i in range(blocks) if 0 <= i + step < blocks]
        return lax.ppermute(value, "blk", pairs)

    if sends:
        first, last = sends
        return moved(last, 1), moved(first, -1)
    hops = -(-halo // rows)
    up, down = list(range(hops, 0, -1)), list(range(-1, -hops - 1, -1))
    above = jnp.concatenate([moved(own, h) for h in up], axis=3)[:, :, :, hops * rows - halo :]
    below = jnp.concatenate([moved(own, h) for h in down], axis=3)[:, :, :, :halo]
    above, below = above.reshape(-1, LANES), below.reshape(-1, LANES)
    if maps is not None:
        above = jnp.concatenate([above] + [moved(maps, h) for h in up])
        below = jnp.concatenate([below] + [moved(maps, h) for h in down])
    return above, below


class Circle:
    def __init__(self, load):
        self.load = load
        self.cache = {}

    def rolled(self, t, offset):
        t = t % RADIX
        if (t, offset) not in self.cache:
            value = self.load(t)
            self.cache[t, offset] = (
                value if offset == 0 else pltpu.roll(value, (-offset) % LANES, 1)
            )
        return self.cache[t, offset]

    def at(self, t, offset, lane):
        here = self.rolled(t, offset)
        if offset > 0:
            return jnp.where(lane < LANES - offset, here, self.rolled(t + 1, offset))
        return jnp.where(lane >= -offset, here, self.rolled(t - 1, offset))


def upwind(wind, coef):
    u, a = -coef * wind, coef * jnp.abs(wind)
    return (
        [45.0 * u + 15.0 * a, 15.0 * a - 45.0 * u],
        [-9.0 * u - 6.0 * a, 9.0 * u - 6.0 * a],
        [u + a, a - u],
        -20.0 * a,
    )


def advected(field_ref, index, row, t, circle, lane, zonal, merid):
    (x1, x2, x3, x0), (y1, y2, y3, y0) = zonal, merid
    total = (x0 + y0) * circle.rolled(t, 0)
    for offset, (ahead, behind) in ((1, x1), (2, x2), (3, x3)):
        total += ahead * circle.at(t, offset, lane) + behind * circle.at(t, -offset, lane)
    for offset, (ahead, behind) in ((1, y1), (2, y2), (3, y3)):
        total += ahead * field_ref[index, t, row + offset : row + offset + 8, :]
        total += behind * field_ref[index, t, row - offset : row - offset + 8, :]
    return total


def assemble(ref, own_ref, above_ref, below_ref, level, halo):
    fields, levels, tiles, rows, _ = own_ref.shape
    for f in range(fields):
        part = pl.ds(pl.multiple_of((f * levels + level) * tiles * halo, 8), tiles * halo)
        for t in range(tiles):
            packed = slice(t * halo, (t + 1) * halo)
            ref[f, t, PAD - halo : PAD, :] = above_ref.at[part][packed, :]
            ref[f, t, PAD : PAD + rows, :] = own_ref[f, level, t]
            ref[f, t, PAD + rows : PAD + rows + halo, :] = below_ref.at[part][packed, :]


def section_kernel(
    dims, wind_ref, wind_above, wind_below, maps_ref, tracer_ref, tracer_above, tracer_below,
    coef_ref, out_ref, now_ref, tend_ref, free_ref, tracer_now, map_ref,
):
    levels, sub, rows, tiles_dev = dims
    lane = lax.broadcasted_iota(jnp.int32, (8, LANES), 1)
    tau = 1.0 / SUBSTEPS
    y_coef = tau * ADV_COEF / 60.0
    end = PAD + rows
    wide = 3 * levels * RADIX * WIND_HALO
    reach = wind_above.shape[0] - wide

    map_ref[PAD - reach : PAD, :] = wind_above[wide : wide + reach, :]
    map_ref[PAD:end, :] = maps_ref[...]
    map_ref[end : end + reach, :] = wind_below[wide : wide + reach, :]

    def put(field, level, row, t, value):
        q, h = t // tiles_dev, t % tiles_dev
        out_ref[q * sub + (row - PAD) // 8, tile_rows(field * levels + level, h, tiles_dev), :] = value

    def level_step(level, carry):
        assemble(now_ref, wind_ref, wind_above, wind_below, level, WIND_HALO)
        assemble(tracer_now, tracer_ref, tracer_above, tracer_below, level, TRACER_HALO)

        for row in range(PAD - 8, end + 8, 8):
            here = slice(row, row + 8)
            own = PAD <= row < end
            circles = [
                Circle(lambda t, f=f: now_ref[f, t % RADIX, here, :]) for f in range(3)
            ]
            tracers = [
                Circle(lambda t, f=f: tracer_now[f, t % RADIX, here, :]) for f in range(2)
            ]
            coef_x = (tau * ADV_COEF / 60.0) * map_ref[here, :]
            for t in range(RADIX):
                zonal = upwind(circles[0].rolled(t, 0), coef_x)
                merid = upwind(circles[1].rolled(t, 0), y_coef)
                for f in range(3):
                    tend = advected(now_ref, f, row, t, circles[f], lane, zonal, merid)
                    tend_ref[f, t, here, :] = tend
                if own:
                    temp, moist = (
                        tracers[f].rolled(t, 0)
                        + SUBSTEPS
                        * advected(tracer_now, f, row, t, tracers[f], lane, zonal, merid)
                        for f in range(2)
                    )
                    free = circles[2].rolled(t, 0) + SUBSTEPS * tend
                    free_ref[t, row - PAD : row - PAD + 8, :] = temp - THETA_DIV * free
                    put(4, level, row, t, moist)

        for step in range(SUBSTEPS):
            reach = 2 * (SUBSTEPS - step) - 1
            for row in range(PAD - reach, end + reach, 8):
                here = slice(row, row + 8)
                circle = Circle(lambda t: now_ref[2, t % RADIX, here, :])
                grad_x = (tau * SOUND * 0.5) * map_ref[here, :]
                coriolis, grad_y = coef_ref[0, here, :], coef_ref[1, here, :]
                for t in range(RADIX):
                    east, north = now_ref[0, t, here, :], now_ref[1, t, here, :]
                    dx = circle.at(t, 1, lane) - circle.at(t, -1, lane)
                    dy = now_ref[2, t, row + 1 : row + 9, :] - now_ref[2, t, row - 1 : row + 7, :]
                    east = east + (tend_ref[0, t, here, :] - grad_x * dx + coriolis * north)
                    north = north + (tend_ref[1, t, here, :] - grad_y * dy - coriolis * east)
                    now_ref[0, t, here, :] = east
                    now_ref[1, t, here, :] = north
            reach -= 1
            for row in range(PAD - reach, end + reach, 8):
                here = slice(row, row + 8)
                circle = Circle(lambda t: now_ref[0, t % RADIX, here, :])
                grad_x = (tau * SOUND * 0.5) * map_ref[here, :]
                grad_y = coef_ref[1, here, :]
                for t in range(RADIX):
                    dx = circle.at(t, 1, lane) - circle.at(t, -1, lane)
                    dy = now_ref[1, t, row + 1 : row + 9, :] - now_ref[1, t, row - 1 : row + 7, :]
                    now_ref[2, t, here, :] = now_ref[2, t, here, :] + (
                        tend_ref[2, t, here, :] - (grad_x * dx + grad_y * dy)
                    )

        for row in range(PAD, end, 8):
            here = slice(row, row + 8)
            for t in range(RADIX):
                east, north, press = (now_ref[f, t, here, :] for f in range(3))
                put(0, level, row, t, east)
                put(1, level, row, t, north)
                put(2, level, row, t, free_ref[t, row - PAD : row - PAD + 8, :] + THETA_DIV * press)
                put(3, level, row, t, press)
        return carry

    lax.fori_loop(0, levels, level_step, 0)


def kernel_call(body, shapes, scratch, name, *args):
    whole = pl.BlockSpec(memory_space=pltpu.VMEM)
    return pl.pallas_call(
        body,
        out_shape=[jax.ShapeDtypeStruct(s, jnp.float32) for s in shapes],
        in_specs=[whole] * len(args),
        out_specs=[whole] * len(shapes),
        scratch_shapes=[pltpu.VMEM(s, jnp.float32) for s in scratch],
        compiler_params=pltpu.CompilerParams(vmem_limit_bytes=VMEM_BYTES),
        cost_estimate=pl.CostEstimate(flops=10**8, bytes_accessed=4 * 10**6, transcendentals=0),
        name=name,
    )(*args)


def shards(tables, east, north, temp, press, moist, map_factor, filter_rows, filter_cutoff):
    levels_all, rows_dev, cols = east.shape
    lon_count, blocks, sub = (lax.axis_size(a) for a in ("lon", "blk", "sub"))
    block = lax.axis_index("blk")
    peers = lon_count * sub
    levels = levels_all // peers
    rows = rows_dev * sub
    total_rows = rows * blocks
    group = ("lon", "sub")

    ring = jnp.arange(rows + 2 * PAD, dtype=jnp.int32) + block * rows - PAD
    inside = (ring >= 0) & (ring < total_rows)
    latitude = -0.5 * math.pi + (ring.astype(jnp.float32) + 0.5) * (math.pi / total_rows)
    tau = 1.0 / SUBSTEPS
    coefs = jnp.stack([(tau * 0.5) * jnp.sin(latitude), jnp.where(inside, tau * SOUND * 0.5, 0.0)])
    coefs = jnp.broadcast_to(coefs[:, :, None], coefs.shape + (LANES,))
    maps = jnp.broadcast_to(map_factor[:, None], (rows_dev, LANES))

    local = jnp.arange(rows, dtype=jnp.int32) + block * rows
    matches = filter_rows[:, None] == local[None, :]
    cut = jnp.sum(jnp.where(matches, filter_cutoff[:, None], 0), axis=0)
    cut = jnp.where(jnp.any(matches, axis=0), cut, KEEP_ALL)
    cut = jnp.broadcast_to(cut[:, None], (rows, LANES))

    tiles_dev = cols // LANES
    field = (peers, levels, rows_dev, cols)

    def to_circles(fields, *extra):
        size = len(fields) * levels * tiles_dev * 8 + 8 * len(extra)
        (packed,) = kernel_call(
            pack_kernel,
            [(peers, size, LANES)],
            [],
            "pack_fields",
            *(f.reshape(field) for f in fields), *extra,
        )
        return lax.all_to_all(packed, group, split_axis=0, concat_axis=0, tiled=True)

    winds, maps, wind_sends = filtered(
        to_circles((east, north, press), maps), cut, tables, 3, levels, sub, WIND_HALO, True
    )
    tracers, _, tracer_sends = filtered(
        to_circles((temp, moist)), cut, tables, 2, levels, sub, TRACER_HALO, False
    )
    wind_halos = exchanged(winds, maps, wind_sends, WIND_HALO)
    tracer_halos = exchanged(tracers, None, tracer_sends, TRACER_HALO)

    tall = rows + 2 * PAD
    (out,) = kernel_call(
        functools.partial(section_kernel, (levels, sub, rows, tiles_dev)),
        [(peers, 5 * levels * tiles_dev * 8, LANES)],
        [
            (3, RADIX, tall, LANES),
            (3, RADIX, tall, LANES),
            (RADIX, rows, LANES),
            (2, RADIX, tall, LANES),
            (tall, LANES),
        ],
        "section",
        winds, *wind_halos, maps, tracers, *tracer_halos, coefs,
    )
    out = lax.all_to_all(out, group, split_axis=0, concat_axis=0, tiled=True)
    return tuple(
        value.reshape(levels_all, rows_dev, cols)
        for value in kernel_call(unpack_kernel, [field] * 5, [], "unpack_fields", out)
    )


def solution(mesh):
    lon, lat = mesh.shape["lon"], mesh.shape["lat"]
    tables = transform_tables()

    def section(*args):
        levels = args[0].shape[0]
        sub = 2 if lat % 2 == 0 and levels % (2 * lon) == 0 else 1
        finer = Mesh(mesh.devices.reshape(lon, lat // sub, sub), ("lon", "blk", "sub"))
        field = P(None, ("blk", "sub"), "lon")
        return jax.shard_map(
            functools.partial(shards, tables),
            mesh=finer,
            in_specs=(field,) * 5 + (P(("blk", "sub")), P(), P()),
            out_specs=(field,) * 5,
            check_vma=False,
        )(*args)

    return section
```

time: 97.4 us -> 80 us (0.82)
  waiting for transfers between devices: 30.4 us -> 21.3 us
  starting transfers between devices: 24.7 us -> 18.4 us
  blocking collectives: 17.2 us -> 21.8 us
  other arithmetic: 4.81 us -> 0.43 us
  local copies, waits for them, and re-layouts: 6.49 us -> 3.75 us
  Pallas kernels: 11.7 us -> 13.1 us
    all_to_all x0 -> x1, blocking collectives: none -> 21.8 us  [shards(): out = lax.all_to_all(out, group, split_axis=0, concat_axis=0, tiled=True)]
    unnamed x1 -> x0, blocking collectives: 17.2 us -> none
    all_to_all x4 -> x2, waiting for transfers between devices: 25.9 us -> 13.8 us  [to_circles(): lax.all_to_all(packed, group, split_axis=0, concat_axis=0, tiled=True)]
    all_to_all x4 -> x2, starting transfers between devices: 16.2 us -> 8.79 us  [to_circles(): lax.all_to_all(packed, group, split_axis=0, concat_axis=0, tiled=True)]
    ppermute x4, waiting for transfers between devices: 4.53 us -> 7.57 us  [moved(): return lax.ppermute(value, 'blk', pairs)]
    another operation x4 -> x1, other arithmetic: 3.01 us -> 0.01 us  [shards(): jnp.stack([tau * 0.5 * jnp.sin(latitude), jnp.where(inside, tau * SOUND *...]
    unnamed x29 -> x20, local copies, waits for them, and re-layouts: 4.74 us -> 2.88 us
    slice x2 -> x0, local copies, waits for them, and re-layouts: 1.61 us -> none  [to_blocks(): back[:, i].reshape(levels_all, rows_dev, cols)]
  transfers between devices with their start and end apart: 8 -> 6, of which waited for: 5 -> 4; matrix products, arithmetic and copies ran while one was open for 4% -> 1% of each run, Pallas kernels for 10% -> 6%
where the time goes in v2:
time: 80 us; the launch traced here: 79.6 us
  blocking collectives  21.8 us (27%)
  waiting for transfers between devices  21.3 us (27%)
  starting transfers between devices  18.4 us (23%)
  Pallas kernels  13.1 us (16%)
  local copies, waits for them, and re-layouts  3.75 us (5%)
    all_to_all x1, blocking collectives, shards(): out = lax.all_to_all(out, group, split_axis=0, concat_axis=0, tiled=True)  21.8 us
    all_to_all x2, waiting for transfers between devices, to_circles(): lax.all_to_all(packed, group, split_axis=0, concat_axis=0, tiled=True)  13.8 us
    pallas_call x6, Pallas kernels, kernel_call(): pl.pallas_call(body, out_shape=[jax.ShapeDtypeStruct(s, jnp.float32) for...  13.1 us
    ppermute x4, starting transfers between devices, moved(): return lax.ppermute(value, 'blk', pairs)  9.57 us
    all_to_all x2, starting transfers between devices, to_circles(): lax.all_to_all(packed, group, split_axis=0, concat_axis=0, tiled=True)  8.79 us
    ppermute x4, waiting for transfers between devices, moved(): return lax.ppermute(value, 'blk', pairs)  7.57 us
    unnamed x20, local copies, waits for them, and re-layouts  2.88 us
  transfers between devices with their start and end apart: 6, of which 4 were waited for; matrix products, arithmetic and copies ran while one was open for 1% of the time, Pallas kernels for 6%

profile of v2, /device:TPU:0, one launch (start us, length us, event | category | flops | bytes accessed | tf_op | source)
XLA Modules:
  0.0 79.6 jit_solution(10268602678794555413)
XLA Ops:
  0.6 0.7 broadcast_in_dim.45.refs_3_
  1.4 0.9 %copy-done.3 = f32[16,8,512]{2,1,0:T(8,128)S(1)} copy-done((f32[16,8,512]{2,1,0:T(8,128)S(1)}, f32[16,8,512]{2,1,0:T(8,128)}, u32[]{:S(2)}) %copy-start.3) | copy-done | bytes 262168
  2.3 0.9 %copy-done.4 = f32[16,8,512]{2,1,0:T(8,128)S(1)} copy-done((f32[16,8,512]{2,1,0:T(8,128)S(1)}, f32[16,8,512]{2,1,0:T(8,128)}, u32[]{:S(2)}) %copy-start.4) | copy-done | bytes 262168
  3.3 0.9 %copy-done.5 = f32[16,8,512]{2,1,0:T(8,128)S(1)} copy-done((f32[16,8,512]{2,1,0:T(8,128)S(1)}, f32[16,8,512]{2,1,0:T(8,128)}, u32[]{:S(2)}) %copy-start.5) | copy-done | bytes 262168
  4.2 1.0 %pack_fields.2 = f32[8,200,128]{2,1,0:T(8,128)} custom-call(f32[8,2,8,512]{3,2,1,0:T(8,128)S(1)} %bitcast.10, f32[8,2,8,512]{3,2,1,0:T(8,128)S(1)} %bitcast.11, f32[8,2,8,512]{3,2,1,0:T(8,128)S(1)} %bitcast.12, f32[8,128]{1,0:T(8,128)S(1)} %broadcast_in_dim.45.refs_3_), custom_call_target="tpu_custom_call" | custom-call | flops 100000000 | bytes 4000000 | tf_op jit(solution)/shard_map/pack_fields/pallas_call | solution.py:417
  5.2 5.3 %all-to-all-start = ((f32[8,200,128]{2,1,0:T(8,128)}), f32[8,200,128]{2,1,0:T(8,128)S(1)}, u32[]{:S(2)}, u32[]{:S(2)}) async-start(f32[8,200,128]{2,1,0:T(8,128)} %pack_fields.2), calls=%async_computation | async-start | bytes 1638400 | tf_op jit(solution)/shard_map/all_to_all | solution.py:465
  10.5 0.8 %pack_fields.3 = f32[8,128,128]{2,1,0:T(8,128)} custom-call(f32[8,2,8,512]{3,2,1,0:T(8,128)S(1)} %bitcast.13, f32[8,2,8,512]{3,2,1,0:T(8,128)S(1)} %bitcast.14), custom_call_target="tpu_custom_call" | custom-call | flops 100000000 | bytes 4000000 | tf_op jit(solution)/shard_map/pack_fields/pallas_call | solution.py:417
  11.4 0.2 compare_reduce_fusion
  11.6 0.2 fusion
  11.7 11.7 %all-to-all-done.refs_0_ = f32[8,200,128]{2,1,0:T(8,128)S(1)} async-done(((f32[8,200,128]{2,1,0:T(8,128)}), f32[8,200,128]{2,1,0:T(8,128)S(1)}, u32[]{:S(2)}, u32[]{:S(2)}) %all-to-all-start) | async-done | bytes 819232 | tf_op jit(solution)/shard_map/all_to_all | solution.py:465
  23.4 3.5 %all-to-all-start.1 = ((f32[8,128,128]{2,1,0:T(8,128)}), f32[8,128,128]{2,1,0:T(8,128)S(1)}, u32[]{:S(2)}, u32[]{:S(2)}) async-start(f32[8,128,128]{2,1,0:T(8,128)} %pack_fields.3), calls=%async_computation.1 | async-start | bytes 1048576 | tf_op jit(solution)/shard_map/all_to_all | solution.py:465
  27.0 2.6 %filter_circles.2 = (f32[3,2,16,16,128]{4,3,2,1,0:T(8,128)S(1)}, f32[16,128]{1,0:T(8,128)S(1)}, f32[976,128]{1,0:T(8,128)S(1)}, f32[976,128]{1,0:T(8,128)}) custom-call(f32[8,200,128]{2,1,0:T(8,128)S(1)} %all-to-all-done.refs_0_, s32[16,128]{1,0:T(8,128)S(1)} %broadcast_in_dim.49.refs_1_, f32[9,2,8,128]{3,2,1,0:T(8,128)S(1)} %copy-done.2, ...), custom_call_target="tpu_custom_call" | custom-call | flops 100000000 | bytes 4000000 | tf_op jit(solution)/shard_map/filter_circles/pallas_call | solution.py:417
  29.7 3.5 %collective-permute-start = (f32[976,128]{1,0:T(8,128)}, f32[976,128]{1,0:T(8,128)S(1)}, u32[]{:S(2)}, u32[]{:S(2)}) collective-permute-start(f32[976,128]{1,0:T(8,128)} %get-tuple-element.18), channel_id=1, source_target_pairs={{0,2},{2,4},{4,6},{1,3},{3,5},{5,7},{8,10},{10,12},{12,14},{9,11},... | collective-permute-start | bytes 1499144 | tf_op jit(solution)/shard_map/ppermute | solution.py:254
  33.2 1.3 %collective-permute-start.1 = (f32[976,128]{1,0:T(8,128)S(1)}, f32[976,128]{1,0:T(8,128)S(1)}, u32[]{:S(2)}, u32[]{:S(2)}) collective-permute-start(f32[976,128]{1,0:T(8,128)S(1)} %get-tuple-element.19), channel_id=1, source_target_pairs={{2,0},{4,2},{6,4},{3,1},{5,3},{7,5},{10,8},{12,10},{14,12},{11,9},... | collective-permute-start | bytes 1499144 | tf_op jit(solution)/shard_map/ppermute | solution.py:254
  34.5 2.1 %all-to-all-done.1.refs_0_ = f32[8,128,128]{2,1,0:T(8,128)S(1)} async-done(((f32[8,128,128]{2,1,0:T(8,128)}), f32[8,128,128]{2,1,0:T(8,128)S(1)}, u32[]{:S(2)}, u32[]{:S(2)}) %all-to-all-start.1) | async-done | bytes 524320 | tf_op jit(solution)/shard_map/all_to_all | solution.py:465
  36.6 1.6 %filter_circles.3 = (f32[2,2,16,16,128]{4,3,2,1,0:T(8,128)S(1)}, f32[192,128]{1,0:T(8,128)S(1)}, f32[192,128]{1,0:T(8,128)S(1)}) custom-call(f32[8,128,128]{2,1,0:T(8,128)S(1)} %all-to-all-done.1.refs_0_, s32[16,128]{1,0:T(8,128)S(1)} %broadcast_in_dim.49.refs_1_, f32[9,2,8,128]{3,2,1,0:T(8,128)S(1)} %copy-done.2, bf16[256,256]{1,0:T(8,128)(2,1)S(1)} %copy-done.1, ...), custom_call_target="tpu_custom_call" | custom-call | flops 100000000 | bytes 4000000 | tf_op jit(solution)/shard_map/filter_circles/pallas_call | solution.py:417
  38.3 3.5 %collective-permute-start.2 = (f32[192,128]{1,0:T(8,128)S(1)}, f32[192,128]{1,0:T(8,128)S(1)}, u32[]{:S(2)}, u32[]{:S(2)}) collective-permute-start(f32[192,128]{1,0:T(8,128)S(1)} %get-tuple-element.22), channel_id=1, source_target_pairs={{0,2},{2,4},{4,6},{1,3},{3,5},{5,7},{8,10},{10,12},{12,14},{9,11},... | collective-permute-start | bytes 294920 | tf_op jit(solution)/shard_map/ppermute | solution.py:254
  41.7 1.3 %collective-permute-start.3 = (f32[192,128]{1,0:T(8,128)S(1)}, f32[192,128]{1,0:T(8,128)S(1)}, u32[]{:S(2)}, u32[]{:S(2)}) collective-permute-start(f32[192,128]{1,0:T(8,128)S(1)} %get-tuple-element.23), channel_id=1, source_target_pairs={{2,0},{4,2},{6,4},{3,1},{5,3},{7,5},{10,8},{12,10},{14,12},{11,9},... | collective-permute-start | bytes 294920 | tf_op jit(solution)/shard_map/ppermute | solution.py:254
  43.1 3.6 %collective-permute-done.2.tracer_above = f32[192,128]{1,0:T(8,128)S(1)} collective-permute-done((f32[192,128]{1,0:T(8,128)S(1)}, f32[192,128]{1,0:T(8,128)S(1)}, u32[]{:S(2)}, u32[]{:S(2)}) %collective-permute-start.2) | collective-permute-done | bytes 98336 | tf_op jit(solution)/shard_map/ppermute | solution.py:254
  46.7 3.9 %collective-permute-done.3.tracer_below = f32[192,128]{1,0:T(8,128)S(1)} collective-permute-done((f32[192,128]{1,0:T(8,128)S(1)}, f32[192,128]{1,0:T(8,128)S(1)}, u32[]{:S(2)}, u32[]{:S(2)}) %collective-permute-start.3) | collective-permute-done | bytes 98336 | tf_op jit(solution)/shard_map/ppermute | solution.py:254
  50.6 0.1 broadcast_in_dim.52.coef_ref
  50.7 5.9 %section.1 = f32[8,320,128]{2,1,0:T(8,128)S(1)} custom-call(f32[3,2,16,16,128]{4,3,2,1,0:T(8,128)S(1)} %get-tuple-element.17.wind_ref, f32[976,128]{1,0:T(8,128)S(1)} %collective-permute-done.wind_above, f32[976,128]{1,0:T(8,128)S(1)} %collective-permute-done.1.wind_below, f32[16,128]{1,0:T(8,128)S(1)} %get-tuple-element.20.maps_ref, ...), custom_call_target="tpu_custom_call" | custom-call | flops 100000000 | bytes 4000000 | tf_op jit(solution)/shard_map/section/pallas_call | solution.py:417
  56.6 21.8 %all_to_all.15.in_ref = f32[8,320,128]{2,1,0:T(8,128)S(1)} all-to-all(f32[8,320,128]{2,1,0:T(8,128)S(1)} %section.1), channel_id=1, replica_groups=mesh['lon'=4,'blk'=4,'sub'=2] {'lon','sub'}, dimensions={0} | all-to-all | bytes 2621440 | tf_op jit(solution)/shard_map/all_to_all | solution.py:490
  78.4 1.1 %unpack_fields.1 = (f32[8,2,8,512]{3,2,1,0:T(8,128)}, f32[8,2,8,512]{3,2,1,0:T(8,128)}, f32[8,2,8,512]{3,2,1,0:T(8,128)}, f32[8,2,8,512]{3,2,1,0:T(8,128)}, f32[8,2,8,512]{3,2,1,0:T(8,128)}) custom-call(f32[8,320,128]{2,1,0:T(8,128)S(1)} %all_to_all.15.in_ref), custom_call_target="tpu_custom_call" | custom-call | flops 100000000 | bytes 4000000 | tf_op jit(solution)/shard_map/unpack_fields/pallas_call | solution.py:417
  (24 shorter events, 0.2 us)
Async XLA Ops:
  1.4 0.9 %copy-start.3 = (f32[16,8,512]{2,1,0:T(8,128)S(1)}, f32[16,8,512]{2,1,0:T(8,128)}, u32[]{:S(2)}) copy-start(f32[16,8,512]{2,1,0:T(8,128)} %param.11) | copy-start | bytes 786436
  2.3 0.9 %copy-start.4 = (f32[16,8,512]{2,1,0:T(8,128)S(1)}, f32[16,8,512]{2,1,0:T(8,128)}, u32[]{:S(2)}) copy-start(f32[16,8,512]{2,1,0:T(8,128)} %param.12) | copy-start | bytes 786436
  3.3 0.9 %copy-start.5 = (f32[16,8,512]{2,1,0:T(8,128)S(1)}, f32[16,8,512]{2,1,0:T(8,128)}, u32[]{:S(2)}) copy-start(f32[16,8,512]{2,1,0:T(8,128)} %param.14) | copy-start | bytes 786436
  4.2 6.3 %copy-start.6 = (f32[16,8,512]{2,1,0:T(8,128)S(1)}, f32[16,8,512]{2,1,0:T(8,128)}, u32[]{:S(2)}) copy-start(f32[16,8,512]{2,1,0:T(8,128)} %param.13) | copy-start | bytes 786436
  4.2 6.3 %copy-start.7 = (f32[16,8,512]{2,1,0:T(8,128)S(1)}, f32[16,8,512]{2,1,0:T(8,128)}, u32[]{:S(2)}) copy-start(f32[16,8,512]{2,1,0:T(8,128)} %param.15) | copy-start | bytes 786436
  5.2 6.2 %copy-start.8 = (s32[32]{0:T(128)S(1)}, s32[32]{0:T(128)}, u32[]{:S(2)}) copy-start(s32[32]{0:T(128)} %param.17) | copy-start | bytes 388
  5.2 6.4 %copy-start.9 = (s32[32]{0:T(128)S(1)}, s32[32]{0:T(128)}, u32[]{:S(2)}) copy-start(s32[32]{0:T(128)} %param.18) | copy-start | bytes 388
  5.2 18.3 %all-to-all-start = ((f32[8,200,128]{2,1,0:T(8,128)}), f32[8,200,128]{2,1,0:T(8,128)S(1)}, u32[]{:S(2)}, u32[]{:S(2)}) async-start(f32[8,200,128]{2,1,0:T(8,128)} %pack_fields.2), calls=%async_computation | async-start | bytes 1638400 | tf_op jit(solution)/shard_map/all_to_all | solution.py:465
  10.5 16.5 %copy-start = (bf16[256,256]{1,0:T(8,128)(2,1)S(1)}, bf16[256,256]{1,0:T(8,128)(2,1)}, u32[]{:S(2)}) copy-start(bf16[256,256]{1,0:T(8,128)(2,1)} %constant.40.clone.refs_4_) | copy-start | bytes 393220
  10.5 16.5 %copy-start.1 = (bf16[256,256]{1,0:T(8,128)(2,1)S(1)}, bf16[256,256]{1,0:T(8,128)(2,1)}, u32[]{:S(2)}) copy-start(bf16[256,256]{1,0:T(8,128)(2,1)} %constant.39.clone.refs_3_) | copy-start | bytes 393220
  10.5 16.5 %copy-start.2 = (f32[9,2,8,128]{3,2,1,0:T(8,128)S(1)}, f32[9,2,8,128]{3,2,1,0:T(8,128)}, u32[]{:S(2)}) copy-start(f32[9,2,8,128]{3,2,1,0:T(8,128)} %constant.38.clone.refs_2_) | copy-start | bytes 221188
  23.4 13.2 %all-to-all-start.1 = ((f32[8,128,128]{2,1,0:T(8,128)}), f32[8,128,128]{2,1,0:T(8,128)S(1)}, u32[]{:S(2)}, u32[]{:S(2)}) async-start(f32[8,128,128]{2,1,0:T(8,128)} %pack_fields.3), calls=%async_computation.1 | async-start | bytes 1048576 | tf_op jit(solution)/shard_map/all_to_all | solution.py:465
  29.7 21.0 %collective-permute-start = (f32[976,128]{1,0:T(8,128)}, f32[976,128]{1,0:T(8,128)S(1)}, u32[]{:S(2)}, u32[]{:S(2)}) collective-permute-start(f32[976,128]{1,0:T(8,128)} %get-tuple-element.18), channel_id=1, source_target_pairs={{0,2},{2,4},{4,6},{1,3},{3,5},{5,7},{8,10},{10,12},{12,14},{9,11},... | collective-permute-start | bytes 1499144 | tf_op jit(solution)/shard_map/ppermute | solution.py:254
  33.2 17.5 %collective-permute-start.1 = (f32[976,128]{1,0:T(8,128)S(1)}, f32[976,128]{1,0:T(8,128)S(1)}, u32[]{:S(2)}, u32[]{:S(2)}) collective-permute-start(f32[976,128]{1,0:T(8,128)S(1)} %get-tuple-element.19), channel_id=1, source_target_pairs={{2,0},{4,2},{6,4},{3,1},{5,3},{7,5},{10,8},{12,10},{14,12},{11,9},... | collective-permute-start | bytes 1499144 | tf_op jit(solution)/shard_map/ppermute | solution.py:254
  38.3 8.4 %collective-permute-start.2 = (f32[192,128]{1,0:T(8,128)S(1)}, f32[192,128]{1,0:T(8,128)S(1)}, u32[]{:S(2)}, u32[]{:S(2)}) collective-permute-start(f32[192,128]{1,0:T(8,128)S(1)} %get-tuple-element.22), channel_id=1, source_target_pairs={{0,2},{2,4},{4,6},{1,3},{3,5},{5,7},{8,10},{10,12},{12,14},{9,11},... | collective-permute-start | bytes 294920 | tf_op jit(solution)/shard_map/ppermute | solution.py:254
  41.7 8.9 %collective-permute-start.3 = (f32[192,128]{1,0:T(8,128)S(1)}, f32[192,128]{1,0:T(8,128)S(1)}, u32[]{:S(2)}, u32[]{:S(2)}) collective-permute-start(f32[192,128]{1,0:T(8,128)S(1)} %get-tuple-element.23), channel_id=1, source_target_pairs={{2,0},{4,2},{6,4},{3,1},{5,3},{7,5},{10,8},{12,10},{14,12},{11,9},... | collective-permute-start | bytes 294920 | tf_op jit(solution)/shard_map/ppermute | solution.py:254

commit v3 on v2

v3 whole, which is shorter than its diff:
```python
import functools
import math

import jax
import jax.numpy as jnp
import numpy as np
from jax import lax
from jax.experimental import pallas as pl
from jax.experimental.pallas import tpu as pltpu
from jax.sharding import Mesh
from jax.sharding import PartitionSpec as P

SUBSTEPS = 4
ADV_COEF = 0.1
SOUND = 0.4
THETA_DIV = 0.3

LANES = 128
RADIX = 16
HALF = RADIX // 2
CIRCLE = LANES * RADIX
WIND_HALO = 10
WINDS = 3
TRACERS = 2
EDGE = 4
PAD = 16
KEEP_ALL = 1 << 20
VMEM_BYTES = 32 * 1024 * 1024
RAW_VMEM_BYTES = 63 * 1024 * 1024


def transform_tables():
    lane = np.arange(LANES)
    angle = 2.0 * np.pi * np.outer(lane, lane) / LANES
    cos, sin = np.cos(angle), np.sin(angle)
    matrix = np.block([[cos, -sin], [sin, cos]]).astype(np.float32)
    high = matrix.astype(jnp.bfloat16)
    low = (matrix - high.astype(np.float32)).astype(jnp.bfloat16)
    turn = 2.0 * np.pi * np.outer(np.arange(HALF + 1), lane) / CIRCLE
    twiddle = np.stack([np.cos(turn), np.sin(turn)], axis=1).astype(np.float32)
    twiddle = np.broadcast_to(twiddle[:, :, None, :], (HALF + 1, 2, 8, LANES))
    return high, low, np.ascontiguousarray(twiddle)


def times_root(value, step, size, sign):
    re, im = value
    if step == 0:
        return value
    if 4 * step == size:
        if im is None:
            return (jnp.zeros_like(re), re if sign > 0 else -re)
        return (-im, re) if sign > 0 else (im, -re)
    c = math.cos(2.0 * math.pi * step / size)
    s = sign * math.sin(2.0 * math.pi * step / size)
    if im is None:
        return (re * c, re * s)
    return (re * c - im * s, re * s + im * c)


def added(a, b):
    im = a[1] if b[1] is None else b[1] if a[1] is None else a[1] + b[1]
    return (a[0] + b[0], im)


def taken(a, b):
    im = a[1] if b[1] is None else -b[1] if a[1] is None else a[1] - b[1]
    return (a[0] - b[0], im)


def conj(a):
    return (a[0], None if a[1] is None else -a[1])


def real_forward(values):
    size = len(values)
    if size == 1:
        return [(values[0], None)]
    even, odd = real_forward(values[0::2]), real_forward(values[1::2])
    out = [None] * (size // 2 + 1)
    for k in range(size // 4 + 1):
        turned = times_root(odd[k], k, size, -1)
        out[k] = added(even[k], turned)
        if k != size // 2 - k:
            out[size // 2 - k] = conj(taken(even[k], turned))
    return out


def real_inverse(spectrum, size):
    if size == 1:
        return [spectrum[0][0]]
    even, odd = [], []
    for k in range(size // 4 + 1):
        mirror = conj(spectrum[size // 2 - k])
        even.append(added(spectrum[k], mirror))
        odd.append(times_root(taken(spectrum[k], mirror), k, size, 1))
    out = [None] * size
    out[0::2] = real_inverse(even, size // 2)
    out[1::2] = real_inverse(odd, size // 2)
    return out


def split_dot(values, high, low):
    top = values.astype(jnp.bfloat16)
    rest = (values - top.astype(jnp.float32)).astype(jnp.bfloat16)
    dot = functools.partial(jnp.dot, preferred_element_type=jnp.float32)
    return dot(top, high) + (dot(rest, high) + dot(top, low))


def rows_at(start, count):
    return pl.ds(start if isinstance(start, int) else pl.multiple_of(start, 8), count)


def tile_rows(index, h, tiles_dev):
    return rows_at((index * tiles_dev + h) * 8, 8)


def staged(field_refs, stage, sems):
    copies = [
        pltpu.make_async_copy(ref, stage.at[f], sems.at[f]) for f, ref in enumerate(field_refs)
    ]
    for copy in copies:
        copy.start()
    return copies


def pack_tiles(stage, f, out_ref):
    _, _, levels, _, cols = stage.shape
    tiles_dev = cols // LANES
    for l in range(levels):
        for h in range(tiles_dev):
            out_ref[:, tile_rows(f * levels + l, h, tiles_dev), :] = stage[
                f, :, l, :, h * LANES : (h + 1) * LANES
            ]


def pack_winds_kernel(*refs):
    *field_refs, map_ref, out_ref, stage, map_row, sems = refs
    peers, size = stage.shape[1], out_ref.shape[1]
    load = pltpu.make_async_copy(map_ref, map_row, sems.at[len(field_refs)])
    load.start()
    copies = staged(field_refs, stage, sems)
    load.wait()
    row = lax.broadcasted_iota(jnp.int32, (8, 8), 0)
    lane = lax.broadcasted_iota(jnp.int32, (8, 8), 1)
    picked = jnp.where(row == lane, jnp.broadcast_to(map_row[...], (8, 8)), 0.0)
    value = jnp.broadcast_to(jnp.sum(picked, axis=1, keepdims=True), (8, LANES))
    out_ref[:, size - 8 :, :] = jnp.broadcast_to(value[None], (peers, 8, LANES))
    for f, copy in enumerate(copies):
        copy.wait()
        pack_tiles(stage, f, out_ref)


def edges_kernel(sub, *refs):
    field_refs, (*out_refs, stage, sems) = refs[:TRACERS], refs[TRACERS:]
    _, _, levels, _, cols = stage.shape
    tiles_dev = cols // LANES
    outer_first = lax.axis_index("sub") == 0
    for f, copy in enumerate(staged(field_refs, stage, sems)):
        copy.wait()
        for l in range(levels):
            for h in range(tiles_dev):
                value = stage[f, :, l, :, h * LANES : (h + 1) * LANES]
                first, last = value[:, :EDGE, :], value[:, EDGE:, :]
                start = ((f * levels + l) * tiles_dev + h) * EDGE
                here = slice(start, start + EDGE)
                if sub == 1:
                    out_refs[0][:, here, :], out_refs[1][:, here, :] = first, last
                else:
                    out_refs[0][:, here, :] = jnp.where(outer_first, first, last)


def pack_tracers_kernel(*refs):
    field_refs, edge_refs = refs[:TRACERS], refs[TRACERS:-3]
    out_ref, stage, sems = refs[-3:]
    _, _, levels, _, cols = stage.shape
    tiles_dev = cols // LANES
    copies = staged(field_refs, stage, sems)
    base, count = TRACERS * levels * tiles_dev * 8, TRACERS * levels * tiles_dev
    if len(edge_refs) == 1:
        out_ref[:, base:, :] = edge_refs[0][...]
    else:
        for i in range(count):
            for side, ref in enumerate(edge_refs):
                start = base + 8 * i + EDGE * side
                out_ref[:, start : start + EDGE, :] = ref[:, i * EDGE : (i + 1) * EDGE, :]
    for f, copy in enumerate(copies):
        copy.wait()
        pack_tiles(stage, f, out_ref)


def unpack_kernel(in_ref, *field_refs):
    _, levels, _, cols = field_refs[0].shape
    tiles_dev = cols // LANES
    for f, ref in enumerate(field_refs):
        for l in range(levels):
            for h in range(tiles_dev):
                ref[:, l, :, h * LANES : (h + 1) * LANES] = in_ref[
                    :, tile_rows(f * levels + l, h, tiles_dev), :
                ]


def tile_of(circles_ref, sub, tiles_dev, base, count, index, t):
    q, h = t // tiles_dev, t % tiles_dev
    start = base + (index * tiles_dev + h) * count
    if count % 8 == 0:
        here = rows_at(start, count)
        parts = [circles_ref[q * sub + c, here, :] for c in range(sub)]
    else:
        parts = [circles_ref[q * sub + c, start : start + count, :] for c in range(sub)]
    return parts[0] if sub == 1 else jnp.concatenate(parts, axis=0)


def turned(twiddle_ref, k, rows):
    c, s = twiddle_ref[k, 0], twiddle_ref[k, 1]
    if rows > 8:
        c, s = (jnp.concatenate([v] * (rows // 8), axis=0) for v in (c, s))
    return c, s


def spread(waves_ref, twiddle_ref, total, start, tiles):
    rows = tiles[0].shape[0]
    spectrum = real_forward(tiles)
    for k in range(HALF + 1):
        re, im = spectrum[k]
        if k == 0:
            im = jnp.zeros_like(re)
        else:
            c, s = turned(twiddle_ref, k, rows)
            if im is None:
                re, im = re * c, -re * s
            else:
                re, im = re * c + im * s, im * c - re * s
        waves_ref[rows_at(k * total + start, rows), :LANES] = re
        waves_ref[rows_at(k * total + start, rows), LANES:] = im


def gathered(waves_ref, twiddle_ref, total, start, rows):
    spectrum = []
    for k in range(HALF + 1):
        re = waves_ref[rows_at(k * total + start, rows), :LANES]
        if k == 0:
            spectrum.append((re, None))
            continue
        im = waves_ref[rows_at(k * total + start, rows), LANES:]
        c, s = turned(twiddle_ref, k, rows)
        spectrum.append((re * c + im * s, None if k == HALF else re * s - im * c))
    return real_inverse(spectrum, RADIX)


def cut_waves(waves_ref, total, high_ref, low_ref, parts):
    high, low = high_ref[...], low_ref[...]
    waves_ref[...] = split_dot(waves_ref[...], high, low)
    for start, groups, cut_ref in parts:
        cut = cut_ref[...]
        rows = cut.shape[0]
        lane = lax.broadcasted_iota(jnp.int32, (rows, LANES), 1)
        for k in range(HALF + 1):
            wave = k + RADIX * lane
            wave = jnp.minimum(wave, CIRCLE - wave)
            kept = jnp.where(wave < cut, 1.0 / CIRCLE, 0.0)
            weight = jnp.concatenate([kept, -kept], axis=1)
            for group in range(groups):
                here = rows_at(k * total + start + group * rows, rows)
                waves_ref[here, :] = waves_ref[here, :] * weight
    waves_ref[...] = split_dot(waves_ref[...], high, low)


def winds_kernel(dims, circles_ref, cut_ref, twiddle_ref, high_ref, low_ref, own_ref, maps_ref, *refs):
    levels, sub, rows, tiles_dev = dims
    *sends, waves_ref = refs
    groups = WINDS * levels
    total = groups * rows
    wide = groups * RADIX * WIND_HALO
    size = circles_ref.shape[1]
    for c in range(sub):
        value = circles_ref[c, size - 8 : size, :]
        maps_ref[8 * c : 8 * c + 8, :] = value
        for ref in sends:
            ref[wide + 8 * c : wide + 8 * c + 8, :] = value

    def tile(group, t):
        return tile_of(circles_ref, sub, tiles_dev, 0, 8, group, t)

    def first(group, carry):
        spread(waves_ref, twiddle_ref, total, group * rows, [tile(group, t) for t in range(RADIX)])
        return carry

    lax.fori_loop(0, groups, first, 0)
    cut_waves(waves_ref, total, high_ref, low_ref, [(0, groups, cut_ref)])
    flagged = cut_ref[...] < KEEP_ALL

    def second(group, carry):
        smooth = gathered(waves_ref, twiddle_ref, total, group * rows, rows)
        part = rows_at(group * RADIX * WIND_HALO, RADIX * WIND_HALO)
        for t in range(RADIX):
            value = jnp.where(flagged, smooth[t], tile(group, t))
            own_ref[group // levels, group % levels, t] = value
            if sends:
                packed = slice(t * WIND_HALO, (t + 1) * WIND_HALO)
                sends[0].at[part][packed, :] = value[:WIND_HALO]
                sends[1].at[part][packed, :] = value[rows - WIND_HALO :]
        return carry

    lax.fori_loop(0, groups, second, 0)


def exchanged(own, maps, sends):
    blocks = lax.axis_size("blk")
    rows = own.shape[3]

    def moved(value, step):
        pairs = [(i, i + step) for i in range(blocks) if 0 <= i + step < blocks]
        return lax.ppermute(value, "blk", pairs)

    if sends:
        first, last = sends
        return moved(last, 1), moved(first, -1)
    hops = -(-WIND_HALO // rows)
    up, down = list(range(hops, 0, -1)), list(range(-1, -hops - 1, -1))
    above = jnp.concatenate([moved(own, h) for h in up], axis=3)[:, :, :, hops * rows - WIND_HALO :]
    below = jnp.concatenate([moved(own, h) for h in down], axis=3)[:, :, :, :WIND_HALO]
    above = jnp.concatenate([above.reshape(-1, LANES)] + [moved(maps, h) for h in up])
    below = jnp.concatenate([below.reshape(-1, LANES)] + [moved(maps, h) for h in down])
    return above, below


class Circle:
    def __init__(self, load):
        self.load = load
        self.cache = {}

    def rolled(self, t, offset):
        t = t % RADIX
        if (t, offset) not in self.cache:
            value = self.load(t)
            self.cache[t, offset] = (
                value if offset == 0 else pltpu.roll(value, (-offset) % LANES, 1)
            )
        return self.cache[t, offset]

    def at(self, t, offset, lane):
        here = self.rolled(t, offset)
        if offset > 0:
            return jnp.where(lane < LANES - offset, here, self.rolled(t + 1, offset))
        return jnp.where(lane >= -offset, here, self.rolled(t - 1, offset))


def upwind(wind, coef):
    u, a = -coef * wind, coef * jnp.abs(wind)
    return (
        [45.0 * u + 15.0 * a, 15.0 * a - 45.0 * u],
        [-9.0 * u - 6.0 * a, 9.0 * u - 6.0 * a],
        [u + a, a - u],
        -20.0 * a,
    )


def advected(field_ref, index, row, t, circle, lane, zonal, merid):
    (x1, x2, x3, x0), (y1, y2, y3, y0) = zonal, merid
    total = (x0 + y0) * circle.rolled(t, 0)
    for offset, (ahead, behind) in ((1, x1), (2, x2), (3, x3)):
        total += ahead * circle.at(t, offset, lane) + behind * circle.at(t, -offset, lane)
    for offset, (ahead, behind) in ((1, y1), (2, y2), (3, y3)):
        total += ahead * field_ref.at[index][t, row + offset : row + offset + 8, :]
        total += behind * field_ref.at[index][t, row - offset : row - offset + 8, :]
    return total


def tracers_kernel(
    dims, circles_ref, cut_ref, edge_cut_ref, twiddle_ref, high_ref, low_ref, wind_ref, maps_ref,
    moist_ref, temp_ref, waves_ref, now_ref,
):
    levels, sub, rows, tiles_dev = dims
    groups = TRACERS * levels
    edges = groups * rows
    total = edges + groups * 8
    base = groups * tiles_dev * 8

    def tile(group, t):
        return tile_of(circles_ref, sub, tiles_dev, 0, 8, group, t)

    def edge(group, t):
        return tile_of(circles_ref, sub, tiles_dev, base, 8 // sub, group, t)

    def first(group, carry):
        spread(waves_ref, twiddle_ref, total, group * rows, [tile(group, t) for t in range(RADIX)])
        return carry

    lax.fori_loop(0, groups, first, 0)
    for group in range(groups):
        spread(waves_ref, twiddle_ref, total, edges + group * 8, [edge(group, t) for t in range(RADIX)])
    cut_waves(
        waves_ref, total, high_ref, low_ref, [(0, groups, cut_ref), (edges, groups, edge_cut_ref)]
    )
    flagged = cut_ref[...] < KEEP_ALL
    edge_flagged = edge_cut_ref[...] < KEEP_ALL

    def second(group, carry):
        smooth = gathered(waves_ref, twiddle_ref, total, group * rows, rows)
        for t in range(RADIX):
            now_ref[group, t, 8 : 8 + rows, :] = jnp.where(flagged, smooth[t], tile(group, t))
        return carry

    lax.fori_loop(0, groups, second, 0)
    for group in range(groups):
        smooth = gathered(waves_ref, twiddle_ref, total, edges + group * 8, 8)
        for t in range(RADIX):
            value = jnp.where(edge_flagged, smooth[t], edge(group, t))
            now_ref[group, t, 8 - EDGE : 8, :] = value[:EDGE]
            now_ref[group, t, 8 + rows : 8 + rows + EDGE, :] = value[EDGE:]

    lane = lax.broadcasted_iota(jnp.int32, (8, LANES), 1)

    def level_step(level, carry):
        for block in range(rows // 8):
            row, own = 8 * block + 8, slice(8 * block, 8 * block + 8)
            circles = [
                Circle(lambda t, i=f * levels + level: now_ref[i, t % RADIX, row : row + 8, :])
                for f in range(TRACERS)
            ]
            coef_x = (ADV_COEF / 60.0) * maps_ref[own, :]
            for t in range(RADIX):
                zonal = upwind(wind_ref[0, level, t, own, :], coef_x)
                merid = upwind(wind_ref[1, level, t, own, :], ADV_COEF / 60.0)
                temp, moist = (
                    circles[f].rolled(t, 0)
                    + advected(now_ref, f * levels + level, row, t, circles[f], lane, zonal, merid)
                    for f in range(TRACERS)
                )
                temp_ref[level, t, own, :] = temp
                q, h = t // tiles_dev, t % tiles_dev
                moist_ref[q * sub + block, tile_rows(level, h, tiles_dev), :] = moist
        return carry

    lax.fori_loop(0, levels, level_step, 0)


def section_kernel(
    dims, own_ref, above_ref, below_ref, maps_ref, temp_ref, coef_ref, out_ref,
    now_ref, tend_ref, free_ref, map_ref,
):
    levels, sub, rows, tiles_dev = dims
    lane = lax.broadcasted_iota(jnp.int32, (8, LANES), 1)
    tau = 1.0 / SUBSTEPS
    y_coef = tau * ADV_COEF / 60.0
    end = PAD + rows
    wide = WINDS * levels * RADIX * WIND_HALO
    reach = above_ref.shape[0] - wide

    map_ref[PAD - reach : PAD, :] = above_ref[wide : wide + reach, :]
    map_ref[PAD:end, :] = maps_ref[...]
    map_ref[end : end + reach, :] = below_ref[wide : wide + reach, :]

    def level_step(level, carry):
        for f in range(WINDS):
            part = rows_at((f * levels + level) * RADIX * WIND_HALO, RADIX * WIND_HALO)
            for t in range(RADIX):
                packed = slice(t * WIND_HALO, (t + 1) * WIND_HALO)
                now_ref[f, t, PAD - WIND_HALO : PAD, :] = above_ref.at[part][packed, :]
                now_ref[f, t, PAD:end, :] = own_ref[f, level, t]
                now_ref[f, t, end : end + WIND_HALO, :] = below_ref.at[part][packed, :]

        def put(field, row, t, value):
            q, h = t // tiles_dev, t % tiles_dev
            out_ref[q * sub + (row - PAD) // 8, tile_rows(field * levels + level, h, tiles_dev), :] = value

        for row in range(PAD - 8, end + 8, 8):
            here = slice(row, row + 8)
            circles = [
                Circle(lambda t, f=f: now_ref[f, t % RADIX, here, :]) for f in range(WINDS)
            ]
            coef_x = (tau * ADV_COEF / 60.0) * map_ref[here, :]
            for t in range(RADIX):
                zonal = upwind(circles[0].rolled(t, 0), coef_x)
                merid = upwind(circles[1].rolled(t, 0), y_coef)
                for f in range(WINDS):
                    tend = advected(now_ref, f, row, t, circles[f], lane, zonal, merid)
                    tend_ref[f, t, here, :] = tend
                if PAD <= row < end:
                    own = slice(row - PAD, row - PAD + 8)
                    free = circles[2].rolled(t, 0) + SUBSTEPS * tend
                    free_ref[t, own, :] = temp_ref[level, t, own, :] - THETA_DIV * free

        for step in range(SUBSTEPS):
            reach = 2 * (SUBSTEPS - step) - 1
            for row in range(PAD - reach, end + reach, 8):
                here = slice(row, row + 8)
                circle = Circle(lambda t: now_ref[2, t % RADIX, here, :])
                grad_x = (tau * SOUND * 0.5) * map_ref[here, :]
                coriolis, grad_y = coef_ref[0, here, :], coef_ref[1, here, :]
                for t in range(RADIX):
                    east, north = now_ref[0, t, here, :], now_ref[1, t, here, :]
                    dx = circle.at(t, 1, lane) - circle.at(t, -1, lane)
                    dy = now_ref[2, t, row + 1 : row + 9, :] - now_ref[2, t, row - 1 : row + 7, :]
                    east = east + (tend_ref[0, t, here, :] - grad_x * dx + coriolis * north)
                    north = north + (tend_ref[1, t, here, :] - grad_y * dy - coriolis * east)
                    now_ref[0, t, here, :] = east
                    now_ref[1, t, here, :] = north
            reach -= 1
            for row in range(PAD - reach, end + reach, 8):
                here = slice(row, row + 8)
                circle = Circle(lambda t: now_ref[0, t % RADIX, here, :])
                grad_x = (tau * SOUND * 0.5) * map_ref[here, :]
                grad_y = coef_ref[1, here, :]
                for t in range(RADIX):
                    dx = circle.at(t, 1, lane) - circle.at(t, -1, lane)
                    dy = now_ref[1, t, row + 1 : row + 9, :] - now_ref[1, t, row - 1 : row + 7, :]
                    now_ref[2, t, here, :] = now_ref[2, t, here, :] + (
                        tend_ref[2, t, here, :] - (grad_x * dx + grad_y * dy)
                    )

        for row in range(PAD, end, 8):
            here = slice(row, row + 8)
            for t in range(RADIX):
                east, north, press = (now_ref[f, t, here, :] for f in range(WINDS))
                put(0, row, t, east)
                put(1, row, t, north)
                put(2, row, t, press)
                put(3, row, t, free_ref[t, row - PAD : row - PAD + 8, :] + THETA_DIV * press)
        return carry

    lax.fori_loop(0, levels, level_step, 0)


def kernel_call(body, shapes, scratch, name, *args, raw=0, cost=2 * 10**6):
    vmem = pl.BlockSpec(memory_space=pltpu.VMEM)
    hbm = pl.BlockSpec(memory_space=pltpu.HBM)
    return pl.pallas_call(
        body,
        out_shape=[jax.ShapeDtypeStruct(s, jnp.float32) for s in shapes],
        in_specs=[hbm] * raw + [vmem] * (len(args) - raw),
        out_specs=[vmem] * len(shapes),
        scratch_shapes=[
            pltpu.VMEM(s, jnp.float32) if isinstance(s, tuple) else s for s in scratch
        ],
        compiler_params=pltpu.CompilerParams(vmem_limit_bytes=RAW_VMEM_BYTES if raw else VMEM_BYTES),
        cost_estimate=pl.CostEstimate(flops=10**6, bytes_accessed=cost, transcendentals=0),
        name=name,
    )(*args)


def shards(tables, east, north, temp, press, moist, map_factor, filter_rows, filter_cutoff):
    levels_all, rows_dev, cols = east.shape
    lon_count, blocks, sub = (lax.axis_size(a) for a in ("lon", "blk", "sub"))
    block = lax.axis_index("blk")
    peers = lon_count * sub
    levels = levels_all // peers
    rows = rows_dev * sub
    total_rows = rows * blocks
    group = ("lon", "sub")

    ring = jnp.arange(rows + 2 * PAD, dtype=jnp.int32) + block * rows - PAD
    inside = (ring >= 0) & (ring < total_rows)
    latitude = -0.5 * math.pi + (ring.astype(jnp.float32) + 0.5) * (math.pi / total_rows)
    tau = 1.0 / SUBSTEPS
    coefs = jnp.stack([(tau * 0.5) * jnp.sin(latitude), jnp.where(inside, tau * SOUND * 0.5, 0.0)])
    coefs = jnp.broadcast_to(coefs[:, :, None], coefs.shape + (LANES,))

    def cutoffs(local):
        matches = filter_rows[:, None] == local[None, :]
        cut = jnp.sum(jnp.where(matches, filter_cutoff[:, None], 0), axis=0)
        cut = jnp.where(jnp.any(matches, axis=0), cut, KEEP_ALL)
        return jnp.broadcast_to(cut[:, None], (local.shape[0], LANES))

    cut = cutoffs(ring[PAD : PAD + rows])
    edge_cut = cutoffs(jnp.concatenate([ring[PAD - EDGE : PAD], ring[PAD + rows : PAD + rows + EDGE]]))

    tiles_dev = cols // LANES
    field = (peers, levels, rows_dev, cols)
    east, north, press, temp, moist = (f.reshape(field) for f in (east, north, press, temp, moist))
    dims = (levels, sub, rows, tiles_dev)
    sides = 2 // sub
    high, low, twiddle = tables
    wind_tiles, tracer_tiles = WINDS * levels * tiles_dev, TRACERS * levels * tiles_dev
    stage, dma = (peers, levels, rows_dev, cols), pltpu.SemaphoreType.DMA

    def all_to_all(value):
        return lax.all_to_all(value, group, split_axis=0, concat_axis=0, tiled=True)

    (packed,) = kernel_call(
        pack_winds_kernel,
        [(peers, (wind_tiles + 1) * 8, LANES)],
        [(WINDS,) + stage, (1, rows_dev), dma((WINDS + 1,))],
        "pack_winds",
        east, north, press, map_factor.reshape(1, rows_dev),
        raw=WINDS + 1,
    )
    wind_circles = all_to_all(packed)

    edges = kernel_call(
        functools.partial(edges_kernel, sub),
        [(peers, tracer_tiles * EDGE, LANES)] * sides,
        [(TRACERS,) + stage, dma((TRACERS,))],
        "edge_rows",
        temp, moist,
        raw=TRACERS,
    )
    if sub == 2:
        pairs = [(2 * b + 1, 2 * b + 2) for b in range(blocks - 1)]
        edges = [lax.ppermute(edges[0], ("blk", "sub"), pairs + [(j, i) for i, j in pairs])]
    else:
        up = [(b, b + 1) for b in range(blocks - 1)]
        edges = [lax.ppermute(edges[1], "blk", up), lax.ppermute(edges[0], "blk", [(j, i) for i, j in up])]
    (packed,) = kernel_call(
        pack_tracers_kernel,
        [(peers, tracer_tiles * (8 + EDGE * sides), LANES)],
        [(TRACERS,) + stage, dma((TRACERS,))],
        "pack_tracers",
        temp, moist, *edges,
        raw=TRACERS,
    )
    tracer_circles = all_to_all(packed)

    outs = [(WINDS, levels, RADIX, rows, LANES), (rows, LANES)]
    if rows >= WIND_HALO:
        outs += [(WINDS * levels * RADIX * WIND_HALO + rows, LANES)] * 2
    winds, maps, *sends = kernel_call(
        functools.partial(winds_kernel, dims),
        outs,
        [((HALF + 1) * WINDS * levels * rows, 2 * LANES)],
        "filter_winds",
        wind_circles, cut, twiddle, high, low,
    )
    halos = exchanged(winds, maps, sends)
    moist_out, temp_part = kernel_call(
        functools.partial(tracers_kernel, dims),
        [(peers, levels * tiles_dev * 8, LANES), (levels, RADIX, rows, LANES)],
        [
            ((HALF + 1) * TRACERS * levels * (rows + 8), 2 * LANES),
            (TRACERS * levels, RADIX, rows + 16, LANES),
        ],
        "tracers",
        tracer_circles, cut, edge_cut, twiddle, high, low, winds, maps,
    )
    moist_out = all_to_all(moist_out)
    tall = rows + 2 * PAD
    (out,) = kernel_call(
        functools.partial(section_kernel, dims),
        [(peers, 4 * levels * tiles_dev * 8, LANES)],
        [(WINDS, RADIX, tall, LANES), (WINDS, RADIX, tall, LANES), (RADIX, rows, LANES), (tall, LANES)],
        "section",
        winds, *halos, maps, temp_part, coefs,
    )
    out = all_to_all(out)
    (new_moist,) = kernel_call(unpack_kernel, [field], [], "unpack_moist", moist_out)
    new_east, new_north, new_press, new_temp = kernel_call(unpack_kernel, [field] * 4, [], "unpack", out)
    return tuple(
        value.reshape(levels_all, rows_dev, cols)
        for value in (new_east, new_north, new_temp, new_press, new_moist)
    )


def solution(mesh):
    lon, lat = mesh.shape["lon"], mesh.shape["lat"]
    tables = transform_tables()

    def section(*args):
        levels = args[0].shape[0]
        sub = 2 if lat % 2 == 0 and levels % (2 * lon) == 0 else 1
        finer = Mesh(mesh.devices.reshape(lon, lat // sub, sub), ("lon", "blk", "sub"))
        field = P(None, ("blk", "sub"), "lon")
        return jax.shard_map(
            functools.partial(shards, tables),
            mesh=finer,
            in_specs=(field,) * 5 + (P(("blk", "sub")), P(), P()),
            out_specs=(field,) * 5,
            check_vma=False,
        )(*args)

    return section
```

time: 80 us -> 74.4 us (0.930)
  blocking collectives: 21.8 us -> 0 us
  Pallas kernels: 13.1 us -> 21.1 us
  waiting for transfers between devices: 21.3 us -> 27.4 us
  starting transfers between devices: 18.4 us -> 22.7 us
  local copies, waits for them, and re-layouts: 3.75 us -> 0.97 us
    all_to_all x1 -> x0, blocking collectives: 21.8 us -> none  [shards(): out = lax.all_to_all(out, group, split_axis=0, concat_axis=0, tiled=True)]
    all_to_all x2 -> x4, waiting for transfers between devices: 13.8 us -> 24.6 us  [all_to_all(): return lax.all_to_all(value, group, split_axis=0, concat_axis=0, tiled=True)]
    pallas_call x6 -> x8, Pallas kernels: 13.1 us -> 21.1 us  [kernel_call(): pl.pallas_call(body, out_shape=[jax.ShapeDtypeStruct(s, jnp.float32) for...]
    all_to_all x2 -> x4, starting transfers between devices: 8.79 us -> 16.5 us  [all_to_all(): return lax.all_to_all(value, group, split_axis=0, concat_axis=0, tiled=True)]
    ppermute x4 -> x2, waiting for transfers between devices: 7.57 us -> 2.8 us  [moved(): return lax.ppermute(value, 'blk', pairs)]
    ppermute x4 -> x2, starting transfers between devices: 9.57 us -> 4.85 us  [moved(): return lax.ppermute(value, 'blk', pairs)]
    unnamed x20 -> x10, local copies, waits for them, and re-layouts: 2.88 us -> 0.62 us
    ppermute x0 -> x1, starting transfers between devices: none -> 1.37 us  [shards(): lax.ppermute(edges[0], ('blk', 'sub'), pairs + [(j, i) for i, j in pairs])]
  transfers between devices with their start and end apart: 6 -> 7, of which waited for: 4 -> 4; matrix products, arithmetic and copies ran while one was open for 1% -> 2% of each run, Pallas kernels for 6% -> 24%
where the time goes in v3:
time: 74.4 us; the launch traced here: 73.9 us
  waiting for transfers between devices  27.4 us (37%)
  starting transfers between devices  22.7 us (31%)
  Pallas kernels  21.1 us (28%)
  local copies, waits for them, and re-layouts  0.97 us (1%)
  other arithmetic  0.88 us (1%)
    all_to_all x4, waiting for transfers between devices, all_to_all(): return lax.all_to_all(value, group, split_axis=0, concat_axis=0, tiled=True)  24.6 us
    pallas_call x8, Pallas kernels, kernel_call(): pl.pallas_call(body, out_shape=[jax.ShapeDtypeStruct(s, jnp.float32) for...  21.1 us
    all_to_all x4, starting transfers between devices, all_to_all(): return lax.all_to_all(value, group, split_axis=0, concat_axis=0, tiled=True)  16.5 us
    ppermute x2, starting transfers between devices, moved(): return lax.ppermute(value, 'blk', pairs)  4.85 us
    ppermute x2, waiting for transfers between devices, moved(): return lax.ppermute(value, 'blk', pairs)  2.8 us
  transfers between devices with their start and end apart: 7, of which 4 were waited for; matrix products, arithmetic and copies ran while one was open for 2% of the time, Pallas kernels for 24%

profile of v3, /device:TPU:0, one launch (start us, length us, event | category | flops | bytes accessed | tf_op | source)
XLA Modules:
  0.0 73.9 jit_solution(6675335069522226928)
XLA Ops:
  0.6 2.1 %pack_winds.1 = f32[8,200,128]{2,1,0:T(8,128)} custom-call(f32[8,2,8,512]{3,2,1,0:T(8,128)} %bitcast.16, f32[8,2,8,512]{3,2,1,0:T(8,128)} %bitcast.17, f32[8,2,8,512]{3,2,1,0:T(8,128)} %bitcast.18, f32[1,8]{1,0:T(1,128)} %bitcast.19), custom_call_target="tpu_custom_call" | custom-call | flops 1000000 | bytes 2000000 | tf_op jit(solution)/shard_map/pack_winds/pallas_call | solution.py:528
  2.7 5.2 %all-to-all-start = ((f32[8,200,128]{2,1,0:T(8,128)}), f32[8,200,128]{2,1,0:T(8,128)S(1)}, u32[]{:S(2)}, u32[]{:S(2)}) async-start(f32[8,200,128]{2,1,0:T(8,128)} %pack_winds.1), calls=%async_computation | async-start | bytes 1638400 | tf_op jit(solution)/shard_map/all_to_all | solution.py:578
  7.9 1.8 %edge_rows.1 = f32[8,64,128]{2,1,0:T(8,128)} custom-call(f32[8,2,8,512]{3,2,1,0:T(8,128)} %bitcast.11, f32[8,2,8,512]{3,2,1,0:T(8,128)} %bitcast.13), custom_call_target="tpu_custom_call" | custom-call | flops 1000000 | bytes 2000000 | tf_op jit(solution)/shard_map/edge_rows/pallas_call | solution.py:528
  9.7 1.4 %collective-permute-start.2 = (f32[8,64,128]{2,1,0:T(8,128)}, f32[8,64,128]{2,1,0:T(8,128)}, u32[]{:S(2)}, u32[]{:S(2)}) collective-permute-start(f32[8,64,128]{2,1,0:T(8,128)} %edge_rows.1), channel_id=1, source_target_pairs={{1,2},{3,4},{5,6},{2,1},{4,3},{6,5},{9,10},{11,12},{13,14},{10,9},... | collective-permute-start | bytes 786440 | tf_op jit(solution)/shard_map/ppermute | solution.py:600
  11.2 0.6 copy-done.3
  11.7 0.2 fusion
  11.9 0.2 compare_reduce_fusion
  12.2 2.9 %pack_tracers.1 = f32[8,192,128]{2,1,0:T(8,128)} custom-call(f32[8,2,8,512]{3,2,1,0:T(8,128)} %bitcast.12, f32[8,2,8,512]{3,2,1,0:T(8,128)} %bitcast.14, f32[8,64,128]{2,1,0:T(8,128)} %collective-permute-done.2.refs_2_), custom_call_target="tpu_custom_call" | custom-call | flops 1000000 | bytes 2000000 | tf_op jit(solution)/shard_map/pack_tracers/pallas_call | solution.py:528
  15.1 5.7 %all-to-all-done.circles_ref = f32[8,200,128]{2,1,0:T(8,128)S(1)} async-done(((f32[8,200,128]{2,1,0:T(8,128)}), f32[8,200,128]{2,1,0:T(8,128)S(1)}, u32[]{:S(2)}, u32[]{:S(2)}) %all-to-all-start) | async-done | bytes 819232 | tf_op jit(solution)/shard_map/all_to_all | solution.py:578
  20.9 4.1 %all-to-all-start.1 = ((f32[8,192,128]{2,1,0:T(8,128)}), f32[8,192,128]{2,1,0:T(8,128)S(1)}, u32[]{:S(2)}, u32[]{:S(2)}) async-start(f32[8,192,128]{2,1,0:T(8,128)} %pack_tracers.1), calls=%async_computation.1 | async-start | bytes 1572864 | tf_op jit(solution)/shard_map/all_to_all | solution.py:578
  25.0 0.2 fusion.1
  25.3 3.0 %filter_winds.1 = (f32[3,2,16,16,128]{4,3,2,1,0:T(8,128)S(1)}, f32[16,128]{1,0:T(8,128)S(1)}, f32[976,128]{1,0:T(8,128)}, f32[976,128]{1,0:T(8,128)}) custom-call(f32[8,200,128]{2,1,0:T(8,128)S(1)} %all-to-all-done.circles_ref, s32[16,128]{1,0:T(8,128)S(1)} %broadcast_in_dim.67.cut_ref, f32[9,2,8,128]{3,2,1,0:T(8,128)S(1)} %copy-done.2, ...), custom_call_target="tpu_custom_call" | custom-call | flops 1000000 | bytes 2000000 | tf_op jit(solution)/shard_map/filter_winds/pallas_call | solution.py:528
  28.3 3.6 %collective-permute-start = (f32[976,128]{1,0:T(8,128)}, f32[976,128]{1,0:T(8,128)S(1)}, u32[]{:S(2)}, u32[]{:S(2)}) collective-permute-start(f32[976,128]{1,0:T(8,128)} %get-tuple-element.16), channel_id=1, source_target_pairs={{0,2},{2,4},{4,6},{1,3},{3,5},{5,7},{8,10},{10,12},{12,14},{9,11},... | collective-permute-start | bytes 1499144 | tf_op jit(solution)/shard_map/ppermute | solution.py:313
  31.9 1.3 %collective-permute-start.1 = (f32[976,128]{1,0:T(8,128)}, f32[976,128]{1,0:T(8,128)S(1)}, u32[]{:S(2)}, u32[]{:S(2)}) collective-permute-start(f32[976,128]{1,0:T(8,128)} %get-tuple-element.17), channel_id=1, source_target_pairs={{2,0},{4,2},{6,4},{3,1},{5,3},{7,5},{10,8},{12,10},{14,12},{11,9},... | collective-permute-start | bytes 1499144 | tf_op jit(solution)/shard_map/ppermute | solution.py:313
  33.2 0.2 compare_reduce_fusion.1
  33.4 4.2 %all-to-all-done.1.circles_ref = f32[8,192,128]{2,1,0:T(8,128)S(1)} async-done(((f32[8,192,128]{2,1,0:T(8,128)}), f32[8,192,128]{2,1,0:T(8,128)S(1)}, u32[]{:S(2)}, u32[]{:S(2)}) %all-to-all-start.1) | async-done | bytes 786464 | tf_op jit(solution)/shard_map/all_to_all | solution.py:578
  37.6 3.6 %tracers.1 = (f32[8,64,128]{2,1,0:T(8,128)}, f32[2,16,16,128]{3,2,1,0:T(8,128)S(1)}) custom-call(f32[8,192,128]{2,1,0:T(8,128)S(1)} %all-to-all-done.1.circles_ref, s32[16,128]{1,0:T(8,128)S(1)} %broadcast_in_dim.67.cut_ref, s32[8,128]{1,0:T(8,128)S(1)} %broadcast_in_dim.71.edge_cut_ref, f32[9,2,8,128]{3,2,1,0:T(8,128)S(1)} %copy-done.2, ...), custom_call_target="tpu_custom_call" | custom-call | flops 1000000 | bytes 2000000 | tf_op jit(solution)/shard_map/tracers/pallas_call | solution.py:528
  41.2 3.4 %all-to-all-start.3 = ((f32[8,64,128]{2,1,0:T(8,128)}), f32[8,64,128]{2,1,0:T(8,128)S(1)}, u32[]{:S(2)}, u32[]{:S(2)}) async-start(f32[8,64,128]{2,1,0:T(8,128)} %get-tuple-element.24), calls=%async_computation.3 | async-start | bytes 524288 | tf_op jit(solution)/shard_map/all_to_all | solution.py:578
  44.7 2.8 %collective-permute-done.1.below_ref = f32[976,128]{1,0:T(8,128)S(1)} collective-permute-done((f32[976,128]{1,0:T(8,128)}, f32[976,128]{1,0:T(8,128)S(1)}, u32[]{:S(2)}, u32[]{:S(2)}) %collective-permute-start.1) | collective-permute-done | bytes 499744 | tf_op jit(solution)/shard_map/ppermute | solution.py:313
  47.6 6.0 %section.1 = f32[8,256,128]{2,1,0:T(8,128)} custom-call(f32[3,2,16,16,128]{4,3,2,1,0:T(8,128)S(1)} %get-tuple-element.15.wind_ref.own_ref, f32[976,128]{1,0:T(8,128)S(1)} %collective-permute-done.above_ref, f32[976,128]{1,0:T(8,128)S(1)} %collective-permute-done.1.below_ref, f32[16,128]{1,0:T(8,128)S(1)} %get-tuple-element.18.maps_ref, ...), custom_call_target="tpu_custom_call" | custom-call | flops 1000000 | bytes 2000000 | tf_op jit(solution)/shard_map/section/pallas_call | solution.py:528
  53.6 3.8 %all-to-all-start.2 = ((f32[8,256,128]{2,1,0:T(8,128)}), f32[8,256,128]{2,1,0:T(8,128)S(1)}, u32[]{:S(2)}, u32[]{:S(2)}) async-start(f32[8,256,128]{2,1,0:T(8,128)} %section.1), calls=%async_computation.2 | async-start | bytes 2097152 | tf_op jit(solution)/shard_map/all_to_all | solution.py:578
  57.4 0.7 unpack_moist.1
  58.1 14.7 %all-to-all-done.2.in_ref = f32[8,256,128]{2,1,0:T(8,128)S(1)} async-done(((f32[8,256,128]{2,1,0:T(8,128)}), f32[8,256,128]{2,1,0:T(8,128)S(1)}, u32[]{:S(2)}, u32[]{:S(2)}) %all-to-all-start.2) | async-done | bytes 1048608 | tf_op jit(solution)/shard_map/all_to_all | solution.py:578
  72.8 1.0 %unpack.1 = (f32[8,2,8,512]{3,2,1,0:T(8,128)}, f32[8,2,8,512]{3,2,1,0:T(8,128)}, f32[8,2,8,512]{3,2,1,0:T(8,128)}, f32[8,2,8,512]{3,2,1,0:T(8,128)}) custom-call(f32[8,256,128]{2,1,0:T(8,128)S(1)} %all-to-all-done.2.in_ref), custom_call_target="tpu_custom_call" | custom-call | flops 1000000 | bytes 2000000 | tf_op jit(solution)/shard_map/unpack/pallas_call | solution.py:528
  (23 shorter events, 0.6 us)
Async XLA Ops:
  2.7 18.1 %all-to-all-start = ((f32[8,200,128]{2,1,0:T(8,128)}), f32[8,200,128]{2,1,0:T(8,128)S(1)}, u32[]{:S(2)}, u32[]{:S(2)}) async-start(f32[8,200,128]{2,1,0:T(8,128)} %pack_winds.1), calls=%async_computation | async-start | bytes 1638400 | tf_op jit(solution)/shard_map/all_to_all | solution.py:578
  9.7 2.5 %collective-permute-start.2 = (f32[8,64,128]{2,1,0:T(8,128)}, f32[8,64,128]{2,1,0:T(8,128)}, u32[]{:S(2)}, u32[]{:S(2)}) collective-permute-start(f32[8,64,128]{2,1,0:T(8,128)} %edge_rows.1), channel_id=1, source_target_pairs={{1,2},{3,4},{5,6},{2,1},{4,3},{6,5},{9,10},{11,12},{13,14},{10,9},... | collective-permute-start | bytes 786440 | tf_op jit(solution)/shard_map/ppermute | solution.py:600
  11.1 0.7 copy-start.3
  11.1 0.7 copy-start.4
  15.1 10.2 %copy-start = (bf16[256,256]{1,0:T(8,128)(2,1)S(1)}, bf16[256,256]{1,0:T(8,128)(2,1)}, u32[]{:S(2)}) copy-start(bf16[256,256]{1,0:T(8,128)(2,1)} %constant.39.clone.high_ref) | copy-start | bytes 393220
  15.1 10.2 %copy-start.1 = (bf16[256,256]{1,0:T(8,128)(2,1)S(1)}, bf16[256,256]{1,0:T(8,128)(2,1)}, u32[]{:S(2)}) copy-start(bf16[256,256]{1,0:T(8,128)(2,1)} %constant.40.clone.low_ref) | copy-start | bytes 393220
  15.1 10.2 %copy-start.2 = (f32[9,2,8,128]{3,2,1,0:T(8,128)S(1)}, f32[9,2,8,128]{3,2,1,0:T(8,128)}, u32[]{:S(2)}) copy-start(f32[9,2,8,128]{3,2,1,0:T(8,128)} %constant.38.clone.twiddle_ref) | copy-start | bytes 221188
  20.9 16.7 %all-to-all-start.1 = ((f32[8,192,128]{2,1,0:T(8,128)}), f32[8,192,128]{2,1,0:T(8,128)S(1)}, u32[]{:S(2)}, u32[]{:S(2)}) async-start(f32[8,192,128]{2,1,0:T(8,128)} %pack_tracers.1), calls=%async_computation.1 | async-start | bytes 1572864 | tf_op jit(solution)/shard_map/all_to_all | solution.py:578
  28.3 16.4 %collective-permute-start = (f32[976,128]{1,0:T(8,128)}, f32[976,128]{1,0:T(8,128)S(1)}, u32[]{:S(2)}, u32[]{:S(2)}) collective-permute-start(f32[976,128]{1,0:T(8,128)} %get-tuple-element.16), channel_id=1, source_target_pairs={{0,2},{2,4},{4,6},{1,3},{3,5},{5,7},{8,10},{10,12},{12,14},{9,11},... | collective-permute-start | bytes 1499144 | tf_op jit(solution)/shard_map/ppermute | solution.py:313
  31.9 15.6 %collective-permute-start.1 = (f32[976,128]{1,0:T(8,128)}, f32[976,128]{1,0:T(8,128)S(1)}, u32[]{:S(2)}, u32[]{:S(2)}) collective-permute-start(f32[976,128]{1,0:T(8,128)} %get-tuple-element.17), channel_id=1, source_target_pairs={{2,0},{4,2},{6,4},{3,1},{5,3},{7,5},{10,8},{12,10},{14,12},{11,9},... | collective-permute-start | bytes 1499144 | tf_op jit(solution)/shard_map/ppermute | solution.py:313
  41.2 12.4 %all-to-all-start.3 = ((f32[8,64,128]{2,1,0:T(8,128)}), f32[8,64,128]{2,1,0:T(8,128)S(1)}, u32[]{:S(2)}, u32[]{:S(2)}) async-start(f32[8,64,128]{2,1,0:T(8,128)} %get-tuple-element.24), calls=%async_computation.3 | async-start | bytes 524288 | tf_op jit(solution)/shard_map/all_to_all | solution.py:578
  53.6 19.3 %all-to-all-start.2 = ((f32[8,256,128]{2,1,0:T(8,128)}), f32[8,256,128]{2,1,0:T(8,128)S(1)}, u32[]{:S(2)}, u32[]{:S(2)}) async-start(f32[8,256,128]{2,1,0:T(8,128)} %section.1), calls=%async_computation.2 | async-start | bytes 2097152 | tf_op jit(solution)/shard_map/all_to_all | solution.py:578

commit v4 on v3

--- a/solution.py
+++ b/solution.py
@@ -134,20 +134,43 @@
 
 
 def pack_winds_kernel(*refs):
-    *field_refs, map_ref, out_ref, stage, map_row, sems = refs
-    peers, size = stage.shape[1], out_ref.shape[1]
-    load = pltpu.make_async_copy(map_ref, map_row, sems.at[len(field_refs)])
+    field_refs, (map_ref, out_ref, stage, packed, map_row, load_sems, store_sems) = refs[:WINDS], refs[WINDS:]
+    _, peers, levels, _, cols = stage.shape
+    tiles_dev, size = cols // LANES, out_ref.shape[1]
+    half = peers // 2
+    pieces = [(f, slice(p * half, (p + 1) * half)) for f in range(WINDS) for p in range(2)]
+    load = pltpu.make_async_copy(map_ref, map_row, load_sems.at[len(pieces)])
     load.start()
-    copies = staged(field_refs, stage, sems)
+    loads = [
+        pltpu.make_async_copy(field_refs[f].at[p], stage.at[f, p], load_sems.at[i])
+        for i, (f, p) in enumerate(pieces)
+    ]
+    for copy in loads:
+        copy.start()
     load.wait()
     row = lax.broadcasted_iota(jnp.int32, (8, 8), 0)
     lane = lax.broadcasted_iota(jnp.int32, (8, 8), 1)
     picked = jnp.where(row == lane, jnp.broadcast_to(map_row[...], (8, 8)), 0.0)
     value = jnp.broadcast_to(jnp.sum(picked, axis=1, keepdims=True), (8, LANES))
-    out_ref[:, size - 8 :, :] = jnp.broadcast_to(value[None], (peers, 8, LANES))
-    for f, copy in enumerate(copies):
+    packed[:, size - 8 :, :] = jnp.broadcast_to(value[None], (peers, 8, LANES))
+
+    def store(i, p, rows):
+        copy = pltpu.make_async_copy(packed.at[p, rows, :], out_ref.at[p, rows, :], store_sems.at[i])
+        copy.start()
+        return copy
+
+    stores = [store(len(pieces), slice(0, peers), slice(size - 8, size))]
+    wide = levels * tiles_dev * 8
+    for i, (f, p) in enumerate(pieces):
+        loads[i].wait()
+        for l in range(levels):
+            for h in range(tiles_dev):
+                packed[p, tile_rows(f * levels + l, h, tiles_dev), :] = stage[
+                    f, p, l, :, h * LANES : (h + 1) * LANES
+                ]
+        stores.append(store(i, p, slice(f * wide, (f + 1) * wide)))
+    for copy in stores:
         copy.wait()
-        pack_tiles(stage, f, out_ref)
 
 
 def edges_kernel(sub, *refs):
@@ -188,15 +211,23 @@
         pack_tiles(stage, f, out_ref)
 
 
-def unpack_kernel(in_ref, *field_refs):
-    _, levels, _, cols = field_refs[0].shape
-    tiles_dev = cols // LANES
+def unpack_kernel(*refs):
+    in_ref, *field_refs, stage, sems = refs
+    _, peers, levels, _, cols = stage.shape
+    tiles_dev, half = cols // LANES, peers // 2
+    copies = []
     for f, ref in enumerate(field_refs):
-        for l in range(levels):
-            for h in range(tiles_dev):
-                ref[:, l, :, h * LANES : (h + 1) * LANES] = in_ref[
-                    :, tile_rows(f * levels + l, h, tiles_dev), :
-                ]
+        for i in range(2):
+            p = slice(i * half, (i + 1) * half)
+            for l in range(levels):
+                for h in range(tiles_dev):
+                    stage[f, p, l, :, h * LANES : (h + 1) * LANES] = in_ref[
+                        p, tile_rows(f * levels + l, h, tiles_dev), :
+                    ]
+            copies.append(pltpu.make_async_copy(stage.at[f, p], ref.at[p], sems.at[2 * f + i]))
+            copies[-1].start()
+    for copy in copies:
+        copy.wait()
 
 
 def tile_of(circles_ref, sub, tiles_dev, base, count, index, t):
@@ -249,7 +280,13 @@
 
 def cut_waves(waves_ref, total, high_ref, low_ref, parts):
     high, low = high_ref[...], low_ref[...]
-    waves_ref[...] = split_dot(waves_ref[...], high, low)
+
+    def lanes_transformed():
+        for k in range(HALF + 1):
+            here = rows_at(k * total, total)
+            waves_ref[here, :] = split_dot(waves_ref[here, :], high, low)
+
+    lanes_transformed()
     for start, groups, cut_ref in parts:
         cut = cut_ref[...]
         rows = cut.shape[0]
@@ -262,7 +299,7 @@
             for group in range(groups):
                 here = rows_at(k * total + start + group * rows, rows)
                 waves_ref[here, :] = waves_ref[here, :] * weight
-    waves_ref[...] = split_dot(waves_ref[...], high, low)
+    lanes_transformed()
 
 
 def winds_kernel(dims, circles_ref, cut_ref, twiddle_ref, high_ref, low_ref, own_ref, maps_ref, *refs):
@@ -285,7 +322,7 @@
         spread(waves_ref, twiddle_ref, total, group * rows, [tile(group, t) for t in range(RADIX)])
         return carry
 
-    lax.fori_loop(0, groups, first, 0)
+    lax.fori_loop(0, groups, first, 0, unroll=True)
     cut_waves(waves_ref, total, high_ref, low_ref, [(0, groups, cut_ref)])
     flagged = cut_ref[...] < KEEP_ALL
 
@@ -301,7 +338,7 @@
                 sends[1].at[part][packed, :] = value[rows - WIND_HALO :]
         return carry
 
-    lax.fori_loop(0, groups, second, 0)
+    lax.fori_loop(0, groups, second, 0, unroll=True)
 
 
 def exchanged(own, maps, sends):
@@ -386,7 +423,7 @@
         spread(waves_ref, twiddle_ref, total, group * rows, [tile(group, t) for t in range(RADIX)])
         return carry
 
-    lax.fori_loop(0, groups, first, 0)
+    lax.fori_loop(0, groups, first, 0, unroll=True)
     for group in range(groups):
         spread(waves_ref, twiddle_ref, total, edges + group * 8, [edge(group, t) for t in range(RADIX)])
     cut_waves(
@@ -401,7 +438,7 @@
             now_ref[group, t, 8 : 8 + rows, :] = jnp.where(flagged, smooth[t], tile(group, t))
         return carry
 
-    lax.fori_loop(0, groups, second, 0)
+    lax.fori_loop(0, groups, second, 0, unroll=True)
     for group in range(groups):
         smooth = gathered(waves_ref, twiddle_ref, total, edges + group * 8, 8)
         for t in range(RADIX):
@@ -435,8 +472,38 @@
     lax.fori_loop(0, levels, level_step, 0)
 
 
+def inner_kernel(dims, own_ref, maps_ref, out_ref, now_ref):
+    levels, sub, rows, tiles_dev = dims
+    lane = lax.broadcasted_iota(jnp.int32, (8, LANES), 1)
+    tau = 1.0 / SUBSTEPS
+    outside = jnp.zeros((8, LANES), jnp.float32)
+
+    def level_step(level, carry):
+        for f in range(WINDS):
+            for t in range(RADIX):
+                now_ref[f, t, 0:8, :] = outside
+                now_ref[f, t, 8 : 8 + rows, :] = own_ref[f, level, t]
+                now_ref[f, t, 8 + rows : 16 + rows, :] = outside
+        for block in range(rows // 8):
+            row, own = 8 * block + 8, slice(8 * block, 8 * block + 8)
+            circles = [
+                Circle(lambda t, f=f: now_ref[f, t % RADIX, row : row + 8, :]) for f in range(WINDS)
+            ]
+            coef_x = (tau * ADV_COEF / 60.0) * maps_ref[own, :]
+            for t in range(RADIX):
+                zonal = upwind(circles[0].rolled(t, 0), coef_x)
+                merid = upwind(circles[1].rolled(t, 0), tau * ADV_COEF / 60.0)
+                for f in range(WINDS):
+                    out_ref[f, level, t, own, :] = advected(
+                        now_ref, f, row, t, circles[f], lane, zonal, merid
+                    )
+        return carry
+
+    lax.fori_loop(0, levels, level_step, 0)
+
+
 def section_kernel(
-    dims, own_ref, above_ref, below_ref, maps_ref, temp_ref, coef_ref, out_ref,
+    dims, own_ref, inner_ref, above_ref, below_ref, maps_ref, temp_ref, coef_ref, out_ref,
     now_ref, tend_ref, free_ref, map_ref,
 ):
     levels, sub, rows, tiles_dev = dims
@@ -464,7 +531,7 @@
             q, h = t // tiles_dev, t % tiles_dev
             out_ref[q * sub + (row - PAD) // 8, tile_rows(field * levels + level, h, tiles_dev), :] = value
 
-        for row in range(PAD - 8, end + 8, 8):
+        for row in (PAD - 8, end):
             here = slice(row, row + 8)
             circles = [
                 Circle(lambda t, f=f: now_ref[f, t % RADIX, here, :]) for f in range(WINDS)
@@ -474,12 +541,28 @@
                 zonal = upwind(circles[0].rolled(t, 0), coef_x)
                 merid = upwind(circles[1].rolled(t, 0), y_coef)
                 for f in range(WINDS):
-                    tend = advected(now_ref, f, row, t, circles[f], lane, zonal, merid)
+                    tend_ref[f, t, here, :] = advected(
+                        now_ref, f, row, t, circles[f], lane, zonal, merid
+                    )
+
+        place = lax.broadcasted_iota(jnp.int32, (8, LANES), 0)
+        for row in range(PAD, end, 8):
+            here, own = slice(row, row + 8), slice(row - PAD, row - PAD + 8)
+            for t in range(RADIX):
+                merid = upwind(now_ref[1, t, here, :], y_coef)
+                for f in range(WINDS):
+                    tend = inner_ref[f, level, t, own, :]
+                    for k in (1, 2, 3):
+                        ahead, behind = merid[k - 1]
+                        if row == PAD:
+                            beyond = now_ref[f, t, row - k : row - k + 8, :]
+                            tend += behind * jnp.where(place < k, beyond, 0.0)
+                        if row == end - 8:
+                            beyond = now_ref[f, t, row + k : row + k + 8, :]
+                            tend += ahead * jnp.where(place >= 8 - k, beyond, 0.0)
                     tend_ref[f, t, here, :] = tend
-                if PAD <= row < end:
-                    own = slice(row - PAD, row - PAD + 8)
-                    free = circles[2].rolled(t, 0) + SUBSTEPS * tend
-                    free_ref[t, own, :] = temp_ref[level, t, own, :] - THETA_DIV * free
+                free = now_ref[2, t, here, :] + SUBSTEPS * tend
+                free_ref[t, own, :] = temp_ref[level, t, own, :] - THETA_DIV * free
 
         for step in range(SUBSTEPS):
             reach = 2 * (SUBSTEPS - step) - 1
@@ -522,14 +605,14 @@
     lax.fori_loop(0, levels, level_step, 0)
 
 
-def kernel_call(body, shapes, scratch, name, *args, raw=0, cost=2 * 10**6):
+def kernel_call(body, shapes, scratch, name, *args, raw=0, raw_out=False, cost=2 * 10**6):
     vmem = pl.BlockSpec(memory_space=pltpu.VMEM)
     hbm = pl.BlockSpec(memory_space=pltpu.HBM)
     return pl.pallas_call(
         body,
         out_shape=[jax.ShapeDtypeStruct(s, jnp.float32) for s in shapes],
         in_specs=[hbm] * raw + [vmem] * (len(args) - raw),
-        out_specs=[vmem] * len(shapes),
+        out_specs=[hbm if raw_out else vmem] * len(shapes),
         scratch_shapes=[
             pltpu.VMEM(s, jnp.float32) if isinstance(s, tuple) else s for s in scratch
         ],
@@ -574,16 +657,27 @@
     wind_tiles, tracer_tiles = WINDS * levels * tiles_dev, TRACERS * levels * tiles_dev
     stage, dma = (peers, levels, rows_dev, cols), pltpu.SemaphoreType.DMA
 
+    def unpacked(count, name, value):
+        scratch = [(count,) + stage, dma((2 * count,))]
+        return kernel_call(unpack_kernel, [field] * count, scratch, name, value, raw_out=True)
+
     def all_to_all(value):
         return lax.all_to_all(value, group, split_axis=0, concat_axis=0, tiled=True)
 
     (packed,) = kernel_call(
         pack_winds_kernel,
         [(peers, (wind_tiles + 1) * 8, LANES)],
-        [(WINDS,) + stage, (1, rows_dev), dma((WINDS + 1,))],
+        [
+            (WINDS,) + stage,
+            (peers, (wind_tiles + 1) * 8, LANES),
+            (1, rows_dev),
+            dma((2 * WINDS + 1,)),
+            dma((2 * WINDS + 1,)),
+        ],
         "pack_winds",
         east, north, press, map_factor.reshape(1, rows_dev),
         raw=WINDS + 1,
+        raw_out=True,
     )
     wind_circles = all_to_all(packed)
 
@@ -622,6 +716,13 @@
         wind_circles, cut, twiddle, high, low,
     )
     halos = exchanged(winds, maps, sends)
+    (inner,) = kernel_call(
+        functools.partial(inner_kernel, dims),
+        [(WINDS, levels, RADIX, rows, LANES)],
+        [(WINDS, RADIX, rows + 16, LANES)],
+        "inner_tendencies",
+        winds, maps,
+    )
     moist_out, temp_part = kernel_call(
         functools.partial(tracers_kernel, dims),
         [(peers, levels * tiles_dev * 8, LANES), (levels, RADIX, rows, LANES)],
@@ -639,11 +740,11 @@
         [(peers, 4 * levels * tiles_dev * 8, LANES)],
         [(WINDS, RADIX, tall, LANES), (WINDS, RADIX, tall, LANES), (RADIX, rows, LANES), (tall, LANES)],
         "section",
-        winds, *halos, maps, temp_part, coefs,
+        winds, inner, *halos, maps, temp_part, coefs,
     )
     out = all_to_all(out)
-    (new_moist,) = kernel_call(unpack_kernel, [field], [], "unpack_moist", moist_out)
-    new_east, new_north, new_press, new_temp = kernel_call(unpack_kernel, [field] * 4, [], "unpack", out)
+    (new_moist,) = unpacked(1, "unpack_moist", moist_out)
+    new_east, new_north, new_press, new_temp = unpacked(4, "unpack", out)
     return tuple(
         value.reshape(levels_all, rows_dev, cols)
         for value in (new_east, new_north, new_temp, new_press, new_moist)

time: 74.4 us -> 73 us (0.981)
  waiting for transfers between devices: 27.4 us -> 26.3 us
    ppermute x2, waiting for transfers between devices: 2.8 us -> 1.2 us  [moved(): return lax.ppermute(value, 'blk', pairs)]
    pallas_call x8 -> x9, Pallas kernels: 21.1 us -> 20.8 us  [kernel_call(): pl.pallas_call(body, out_shape=[jax.ShapeDtypeStruct(s, jnp.float32) for...]
  transfers between devices with their start and end apart: 7 -> 7, of which waited for: 4 -> 4; matrix products, arithmetic and copies ran while one was open for 2% -> 2% of each run, Pallas kernels for 24% -> 25%
where the time goes in v4:
time: 73 us; the launch traced here: 72.5 us
  waiting for transfers between devices  26.3 us (36%)
  starting transfers between devices  22.7 us (31%)
  Pallas kernels  20.8 us (28%)
  local copies, waits for them, and re-layouts  0.97 us (1%)
  other arithmetic  0.88 us (1%)
  between operations  0.75 us (1%)
    all_to_all x4, waiting for transfers between devices, all_to_all(): return lax.all_to_all(value, group, split_axis=0, concat_axis=0, tiled=True)  25.1 us
    pallas_call x9, Pallas kernels, kernel_call(): pl.pallas_call(body, out_shape=[jax.ShapeDtypeStruct(s, jnp.float32) for...  20.8 us
    all_to_all x4, starting transfers between devices, all_to_all(): return lax.all_to_all(value, group, split_axis=0, concat_axis=0, tiled=True)  16.5 us
    ppermute x2, starting transfers between devices, moved(): return lax.ppermute(value, 'blk', pairs)  4.85 us
  transfers between devices with their start and end apart: 7, of which 4 were waited for; matrix products, arithmetic and copies ran while one was open for 2% of the time, Pallas kernels for 25%

profile of v4, /device:TPU:0, one launch (start us, length us, event | category | flops | bytes accessed | tf_op | source)
XLA Modules:
  0.0 72.5 jit_solution(3893189785494406292)
XLA Ops:
  0.6 2.0 %pack_winds.1 = f32[8,200,128]{2,1,0:T(8,128)} custom-call(f32[8,2,8,512]{3,2,1,0:T(8,128)} %bitcast.16, f32[8,2,8,512]{3,2,1,0:T(8,128)} %bitcast.17, f32[8,2,8,512]{3,2,1,0:T(8,128)} %bitcast.18, f32[1,8]{1,0:T(1,128)} %bitcast.19), custom_call_target="tpu_custom_call" | custom-call | flops 1000000 | bytes 2000000 | tf_op jit(solution)/shard_map/pack_winds/pallas_call | solution.py:611
  2.6 5.2 %all-to-all-start = ((f32[8,200,128]{2,1,0:T(8,128)}), f32[8,200,128]{2,1,0:T(8,128)S(1)}, u32[]{:S(2)}, u32[]{:S(2)}) async-start(f32[8,200,128]{2,1,0:T(8,128)} %pack_winds.1), calls=%async_computation | async-start | bytes 1638400 | tf_op jit(solution)/shard_map/all_to_all | solution.py:665
  7.8 1.8 %edge_rows.1 = f32[8,64,128]{2,1,0:T(8,128)} custom-call(f32[8,2,8,512]{3,2,1,0:T(8,128)} %bitcast.11, f32[8,2,8,512]{3,2,1,0:T(8,128)} %bitcast.13), custom_call_target="tpu_custom_call" | custom-call | flops 1000000 | bytes 2000000 | tf_op jit(solution)/shard_map/edge_rows/pallas_call | solution.py:611
  9.6 1.4 %collective-permute-start.2 = (f32[8,64,128]{2,1,0:T(8,128)}, f32[8,64,128]{2,1,0:T(8,128)}, u32[]{:S(2)}, u32[]{:S(2)}) collective-permute-start(f32[8,64,128]{2,1,0:T(8,128)} %edge_rows.1), channel_id=1, source_target_pairs={{1,2},{3,4},{5,6},{2,1},{4,3},{6,5},{9,10},{11,12},{13,14},{10,9},... | collective-permute-start | bytes 786440 | tf_op jit(solution)/shard_map/ppermute | solution.py:694
  11.1 0.6 copy-done.3
  11.8 0.2 compare_reduce_fusion
  12.1 2.9 %pack_tracers.1 = f32[8,192,128]{2,1,0:T(8,128)} custom-call(f32[8,2,8,512]{3,2,1,0:T(8,128)} %bitcast.12, f32[8,2,8,512]{3,2,1,0:T(8,128)} %bitcast.14, f32[8,64,128]{2,1,0:T(8,128)} %collective-permute-done.2.refs_2_), custom_call_target="tpu_custom_call" | custom-call | flops 1000000 | bytes 2000000 | tf_op jit(solution)/shard_map/pack_tracers/pallas_call | solution.py:611
  15.0 5.7 %all-to-all-done.circles_ref = f32[8,200,128]{2,1,0:T(8,128)S(1)} async-done(((f32[8,200,128]{2,1,0:T(8,128)}), f32[8,200,128]{2,1,0:T(8,128)S(1)}, u32[]{:S(2)}, u32[]{:S(2)}) %all-to-all-start) | async-done | bytes 819232 | tf_op jit(solution)/shard_map/all_to_all | solution.py:665
  20.8 4.1 %all-to-all-start.1 = ((f32[8,192,128]{2,1,0:T(8,128)}), f32[8,192,128]{2,1,0:T(8,128)S(1)}, u32[]{:S(2)}, u32[]{:S(2)}) async-start(f32[8,192,128]{2,1,0:T(8,128)} %pack_tracers.1), calls=%async_computation.1 | async-start | bytes 1572864 | tf_op jit(solution)/shard_map/all_to_all | solution.py:665
  24.9 0.2 fusion.1
  25.2 2.5 %filter_winds.1 = (f32[3,2,16,16,128]{4,3,2,1,0:T(8,128)S(1)}, f32[16,128]{1,0:T(8,128)S(1)}, f32[976,128]{1,0:T(8,128)}, f32[976,128]{1,0:T(8,128)}) custom-call(f32[8,200,128]{2,1,0:T(8,128)S(1)} %all-to-all-done.circles_ref, s32[16,128]{1,0:T(8,128)S(1)} %broadcast_in_dim.67.cut_ref, f32[9,2,8,128]{3,2,1,0:T(8,128)S(1)} %copy-done.2, ...), custom_call_target="tpu_custom_call" | custom-call | flops 1000000 | bytes 2000000 | tf_op jit(solution)/shard_map/filter_winds/pallas_call | solution.py:611
  27.7 3.6 %collective-permute-start = (f32[976,128]{1,0:T(8,128)}, f32[976,128]{1,0:T(8,128)S(1)}, u32[]{:S(2)}, u32[]{:S(2)}) collective-permute-start(f32[976,128]{1,0:T(8,128)} %get-tuple-element.17), channel_id=1, source_target_pairs={{0,2},{2,4},{4,6},{1,3},{3,5},{5,7},{8,10},{10,12},{12,14},{9,11},... | collective-permute-start | bytes 1499144 | tf_op jit(solution)/shard_map/ppermute | solution.py:350
  31.3 1.3 %collective-permute-start.1 = (f32[976,128]{1,0:T(8,128)}, f32[976,128]{1,0:T(8,128)S(1)}, u32[]{:S(2)}, u32[]{:S(2)}) collective-permute-start(f32[976,128]{1,0:T(8,128)} %get-tuple-element.18), channel_id=1, source_target_pairs={{2,0},{4,2},{6,4},{3,1},{5,3},{7,5},{10,8},{12,10},{14,12},{11,9},... | collective-permute-start | bytes 1499144 | tf_op jit(solution)/shard_map/ppermute | solution.py:350
  32.6 0.2 compare_reduce_fusion.1
  32.8 4.7 %all-to-all-done.1.circles_ref = f32[8,192,128]{2,1,0:T(8,128)S(1)} async-done(((f32[8,192,128]{2,1,0:T(8,128)}), f32[8,192,128]{2,1,0:T(8,128)S(1)}, u32[]{:S(2)}, u32[]{:S(2)}) %all-to-all-start.1) | async-done | bytes 786464 | tf_op jit(solution)/shard_map/all_to_all | solution.py:665
  37.5 3.3 %tracers.1 = (f32[8,64,128]{2,1,0:T(8,128)}, f32[2,16,16,128]{3,2,1,0:T(8,128)S(1)}) custom-call(f32[8,192,128]{2,1,0:T(8,128)S(1)} %all-to-all-done.1.circles_ref, s32[16,128]{1,0:T(8,128)S(1)} %broadcast_in_dim.67.cut_ref, s32[8,128]{1,0:T(8,128)S(1)} %broadcast_in_dim.71.edge_cut_ref, f32[9,2,8,128]{3,2,1,0:T(8,128)S(1)} %copy-done.2, ...), custom_call_target="tpu_custom_call" | custom-call | flops 1000000 | bytes 2000000 | tf_op jit(solution)/shard_map/tracers/pallas_call | solution.py:611
  40.8 3.4 %all-to-all-start.3 = ((f32[8,64,128]{2,1,0:T(8,128)}), f32[8,64,128]{2,1,0:T(8,128)S(1)}, u32[]{:S(2)}, u32[]{:S(2)}) async-start(f32[8,64,128]{2,1,0:T(8,128)} %get-tuple-element.24), calls=%async_computation.3 | async-start | bytes 524288 | tf_op jit(solution)/shard_map/all_to_all | solution.py:665
  44.3 1.4 %inner_tendencies.1.inner_ref = f32[3,2,16,16,128]{4,3,2,1,0:T(8,128)S(1)} custom-call(f32[3,2,16,16,128]{4,3,2,1,0:T(8,128)S(1)} %get-tuple-element.15.own_ref.wind_ref, f32[16,128]{1,0:T(8,128)S(1)} %get-tuple-element.16.maps_ref), custom_call_target="tpu_custom_call" | custom-call | flops 1000000 | bytes 2000000 | tf_op jit(solution)/shard_map/inner_tendencies/pallas_call | solution.py:611
  45.7 1.2 %collective-permute-done.1.below_ref = f32[976,128]{1,0:T(8,128)S(1)} collective-permute-done((f32[976,128]{1,0:T(8,128)}, f32[976,128]{1,0:T(8,128)S(1)}, u32[]{:S(2)}, u32[]{:S(2)}) %collective-permute-start.1) | collective-permute-done | bytes 499744 | tf_op jit(solution)/shard_map/ppermute | solution.py:350
  47.0 5.2 %section.1 = f32[8,256,128]{2,1,0:T(8,128)} custom-call(f32[3,2,16,16,128]{4,3,2,1,0:T(8,128)S(1)} %get-tuple-element.15.own_ref.wind_ref, f32[3,2,16,16,128]{4,3,2,1,0:T(8,128)S(1)} %inner_tendencies.1.inner_ref, f32[976,128]{1,0:T(8,128)S(1)} %collective-permute-done.above_ref, f32[976,128]{1,0:T(8,128)S(1)} %collective-permute-done.1.below_ref, ...), custom_call_target="tpu_custom_call" | custom-call | flops 1000000 | bytes 2000000 | tf_op jit(solution)/shard_map/section/pallas_call | solution.py:611
  52.2 3.8 %all-to-all-start.2 = ((f32[8,256,128]{2,1,0:T(8,128)}), f32[8,256,128]{2,1,0:T(8,128)S(1)}, u32[]{:S(2)}, u32[]{:S(2)}) async-start(f32[8,256,128]{2,1,0:T(8,128)} %section.1), calls=%async_computation.2 | async-start | bytes 2097152 | tf_op jit(solution)/shard_map/all_to_all | solution.py:665
  56.0 0.7 unpack_moist.1
  56.8 14.7 %all-to-all-done.2.refs_0_ = f32[8,256,128]{2,1,0:T(8,128)S(1)} async-done(((f32[8,256,128]{2,1,0:T(8,128)}), f32[8,256,128]{2,1,0:T(8,128)S(1)}, u32[]{:S(2)}, u32[]{:S(2)}) %all-to-all-start.2) | async-done | bytes 1048608 | tf_op jit(solution)/shard_map/all_to_all | solution.py:665
  71.4 1.0 %unpack.1 = (f32[8,2,8,512]{3,2,1,0:T(8,128)}, f32[8,2,8,512]{3,2,1,0:T(8,128)}, f32[8,2,8,512]{3,2,1,0:T(8,128)}, f32[8,2,8,512]{3,2,1,0:T(8,128)}) custom-call(f32[8,256,128]{2,1,0:T(8,128)S(1)} %all-to-all-done.2.refs_0_), custom_call_target="tpu_custom_call" | custom-call | flops 1000000 | bytes 2000000 | tf_op jit(solution)/shard_map/unpack/pallas_call | solution.py:611
  (24 shorter events, 0.7 us)
Async XLA Ops:
  2.6 18.1 %all-to-all-start = ((f32[8,200,128]{2,1,0:T(8,128)}), f32[8,200,128]{2,1,0:T(8,128)S(1)}, u32[]{:S(2)}, u32[]{:S(2)}) async-start(f32[8,200,128]{2,1,0:T(8,128)} %pack_winds.1), calls=%async_computation | async-start | bytes 1638400 | tf_op jit(solution)/shard_map/all_to_all | solution.py:665
  9.6 2.5 %collective-permute-start.2 = (f32[8,64,128]{2,1,0:T(8,128)}, f32[8,64,128]{2,1,0:T(8,128)}, u32[]{:S(2)}, u32[]{:S(2)}) collective-permute-start(f32[8,64,128]{2,1,0:T(8,128)} %edge_rows.1), channel_id=1, source_target_pairs={{1,2},{3,4},{5,6},{2,1},{4,3},{6,5},{9,10},{11,12},{13,14},{10,9},... | collective-permute-start | bytes 786440 | tf_op jit(solution)/shard_map/ppermute | solution.py:694
  11.0 0.7 copy-start.3
  11.0 0.7 copy-start.4
  15.0 10.2 %copy-start = (bf16[256,256]{1,0:T(8,128)(2,1)S(1)}, bf16[256,256]{1,0:T(8,128)(2,1)}, u32[]{:S(2)}) copy-start(bf16[256,256]{1,0:T(8,128)(2,1)} %constant.40.clone.low_ref) | copy-start | bytes 393220
  15.0 10.2 %copy-start.1 = (bf16[256,256]{1,0:T(8,128)(2,1)S(1)}, bf16[256,256]{1,0:T(8,128)(2,1)}, u32[]{:S(2)}) copy-start(bf16[256,256]{1,0:T(8,128)(2,1)} %constant.39.clone.high_ref) | copy-start | bytes 393220
  15.0 10.2 %copy-start.2 = (f32[9,2,8,128]{3,2,1,0:T(8,128)S(1)}, f32[9,2,8,128]{3,2,1,0:T(8,128)}, u32[]{:S(2)}) copy-start(f32[9,2,8,128]{3,2,1,0:T(8,128)} %constant.38.clone.twiddle_ref) | copy-start | bytes 221188
  20.8 16.7 %all-to-all-start.1 = ((f32[8,192,128]{2,1,0:T(8,128)}), f32[8,192,128]{2,1,0:T(8,128)S(1)}, u32[]{:S(2)}, u32[]{:S(2)}) async-start(f32[8,192,128]{2,1,0:T(8,128)} %pack_tracers.1), calls=%async_computation.1 | async-start | bytes 1572864 | tf_op jit(solution)/shard_map/all_to_all | solution.py:665
  27.7 18.0 %collective-permute-start = (f32[976,128]{1,0:T(8,128)}, f32[976,128]{1,0:T(8,128)S(1)}, u32[]{:S(2)}, u32[]{:S(2)}) collective-permute-start(f32[976,128]{1,0:T(8,128)} %get-tuple-element.17), channel_id=1, source_target_pairs={{0,2},{2,4},{4,6},{1,3},{3,5},{5,7},{8,10},{10,12},{12,14},{9,11},... | collective-permute-start | bytes 1499144 | tf_op jit(solution)/shard_map/ppermute | solution.py:350
  31.3 15.6 %collective-permute-start.1 = (f32[976,128]{1,0:T(8,128)}, f32[976,128]{1,0:T(8,128)S(1)}, u32[]{:S(2)}, u32[]{:S(2)}) collective-permute-start(f32[976,128]{1,0:T(8,128)} %get-tuple-element.18), channel_id=1, source_target_pairs={{2,0},{4,2},{6,4},{3,1},{5,3},{7,5},{10,8},{12,10},{14,12},{11,9},... | collective-permute-start | bytes 1499144 | tf_op jit(solution)/shard_map/ppermute | solution.py:350
  40.8 11.4 %all-to-all-start.3 = ((f32[8,64,128]{2,1,0:T(8,128)}), f32[8,64,128]{2,1,0:T(8,128)S(1)}, u32[]{:S(2)}, u32[]{:S(2)}) async-start(f32[8,64,128]{2,1,0:T(8,128)} %get-tuple-element.24), calls=%async_computation.3 | async-start | bytes 524288 | tf_op jit(solution)/shard_map/all_to_all | solution.py:665
  52.2 19.3 %all-to-all-start.2 = ((f32[8,256,128]{2,1,0:T(8,128)}), f32[8,256,128]{2,1,0:T(8,128)S(1)}, u32[]{:S(2)}, u32[]{:S(2)}) async-start(f32[8,256,128]{2,1,0:T(8,128)} %section.1), calls=%async_computation.2 | async-start | bytes 2097152 | tf_op jit(solution)/shard_map/all_to_all | solution.py:665

commit v5 on v4

--- a/solution.py
+++ b/solution.py
@@ -20,6 +20,7 @@
 HALF = RADIX // 2
 CIRCLE = LANES * RADIX
 WIND_HALO = 10
+FAR = (2, 2, 1)
 WINDS = 3
 TRACERS = 2
 EDGE = 4
@@ -112,6 +113,10 @@
 
 def tile_rows(index, h, tiles_dev):
     return rows_at((index * tiles_dev + h) * 8, 8)
+
+
+def far_start(field, levels):
+    return levels * RADIX * (8 * WINDS + sum(FAR[:field]))
 
 
 def staged(field_refs, stage, sems):
@@ -280,26 +285,17 @@
 
 def cut_waves(waves_ref, total, high_ref, low_ref, parts):
     high, low = high_ref[...], low_ref[...]
-
-    def lanes_transformed():
-        for k in range(HALF + 1):
-            here = rows_at(k * total, total)
-            waves_ref[here, :] = split_dot(waves_ref[here, :], high, low)
-
-    lanes_transformed()
-    for start, groups, cut_ref in parts:
-        cut = cut_ref[...]
-        rows = cut.shape[0]
-        lane = lax.broadcasted_iota(jnp.int32, (rows, LANES), 1)
-        for k in range(HALF + 1):
-            wave = k + RADIX * lane
+    for k in range(HALF + 1):
+        weights = []
+        for groups, cut_ref in parts:
+            cut = cut_ref[...]
+            wave = k + RADIX * lax.broadcasted_iota(jnp.int32, cut.shape, 1)
             wave = jnp.minimum(wave, CIRCLE - wave)
             kept = jnp.where(wave < cut, 1.0 / CIRCLE, 0.0)
-            weight = jnp.concatenate([kept, -kept], axis=1)
-            for group in range(groups):
-                here = rows_at(k * total + start + group * rows, rows)
-                waves_ref[here, :] = waves_ref[here, :] * weight
-    lanes_transformed()
+            weights += [jnp.concatenate([kept, -kept], axis=1)] * groups
+        here = rows_at(k * total, total)
+        spectra = split_dot(waves_ref[here, :], high, low) * jnp.concatenate(weights, axis=0)
+        waves_ref[here, :] = split_dot(spectra, high, low)
 
 
 def winds_kernel(dims, circles_ref, cut_ref, twiddle_ref, high_ref, low_ref, own_ref, maps_ref, *refs):
@@ -307,7 +303,7 @@
     *sends, waves_ref = refs
     groups = WINDS * levels
     total = groups * rows
-    wide = groups * RADIX * WIND_HALO
+    wide = far_start(WINDS, levels)
     size = circles_ref.shape[1]
     for c in range(sub):
         value = circles_ref[c, size - 8 : size, :]
@@ -318,27 +314,22 @@
     def tile(group, t):
         return tile_of(circles_ref, sub, tiles_dev, 0, 8, group, t)
 
-    def first(group, carry):
+    for group in range(groups):
         spread(waves_ref, twiddle_ref, total, group * rows, [tile(group, t) for t in range(RADIX)])
-        return carry
-
-    lax.fori_loop(0, groups, first, 0, unroll=True)
-    cut_waves(waves_ref, total, high_ref, low_ref, [(0, groups, cut_ref)])
+    cut_waves(waves_ref, total, high_ref, low_ref, [(groups, cut_ref)])
     flagged = cut_ref[...] < KEEP_ALL
-
-    def second(group, carry):
+    for group in range(groups):
+        f, l = group // levels, group % levels
         smooth = gathered(waves_ref, twiddle_ref, total, group * rows, rows)
-        part = rows_at(group * RADIX * WIND_HALO, RADIX * WIND_HALO)
         for t in range(RADIX):
             value = jnp.where(flagged, smooth[t], tile(group, t))
-            own_ref[group // levels, group % levels, t] = value
+            own_ref[f, l, t] = value
             if sends:
-                packed = slice(t * WIND_HALO, (t + 1) * WIND_HALO)
-                sends[0].at[part][packed, :] = value[:WIND_HALO]
-                sends[1].at[part][packed, :] = value[rows - WIND_HALO :]
-        return carry
-
-    lax.fori_loop(0, groups, second, 0, unroll=True)
+                near = slice((group * RADIX + t) * 8, (group * RADIX + t) * 8 + 8)
+                start = far_start(f, levels) + (l * RADIX + t) * FAR[f]
+                far = slice(start, start + FAR[f])
+                sends[0][near, :], sends[0][far, :] = value[:8], value[8 : 8 + FAR[f]]
+                sends[1][near, :], sends[1][far, :] = value[rows - 8 :], value[rows - 8 - FAR[f] : rows - 8]
 
 
 def exchanged(own, maps, sends):
@@ -353,12 +344,19 @@
         first, last = sends
         return moved(last, 1), moved(first, -1)
     hops = -(-WIND_HALO // rows)
-    up, down = list(range(hops, 0, -1)), list(range(-1, -hops - 1, -1))
-    above = jnp.concatenate([moved(own, h) for h in up], axis=3)[:, :, :, hops * rows - WIND_HALO :]
-    below = jnp.concatenate([moved(own, h) for h in down], axis=3)[:, :, :, :WIND_HALO]
-    above = jnp.concatenate([above.reshape(-1, LANES)] + [moved(maps, h) for h in up])
-    below = jnp.concatenate([below.reshape(-1, LANES)] + [moved(maps, h) for h in down])
-    return above, below
+    sides = []
+    for steps in (range(hops, 0, -1), range(-1, -hops - 1, -1)):
+        wide = jnp.concatenate([moved(own, h) for h in steps], axis=3)
+        size = hops * rows
+        if steps[0] > 0:
+            near, far = slice(size - 8, size), [slice(size - 8 - n, size - 8) for n in FAR]
+        else:
+            near, far = slice(0, 8), [slice(8, 8 + n) for n in FAR]
+        parts = [wide[:, :, :, near]] + [wide[f, :, :, rest] for f, rest in enumerate(far)]
+        sides.append(
+            jnp.concatenate([p.reshape(-1, LANES) for p in parts] + [moved(maps, h) for h in steps])
+        )
+    return sides
 
 
 class Circle:
@@ -427,7 +425,7 @@
     for group in range(groups):
         spread(waves_ref, twiddle_ref, total, edges + group * 8, [edge(group, t) for t in range(RADIX)])
     cut_waves(
-        waves_ref, total, high_ref, low_ref, [(0, groups, cut_ref), (edges, groups, edge_cut_ref)]
+        waves_ref, total, high_ref, low_ref, [(groups, cut_ref), (groups, edge_cut_ref)]
     )
     flagged = cut_ref[...] < KEEP_ALL
     edge_flagged = edge_cut_ref[...] < KEEP_ALL
@@ -511,7 +509,7 @@
     tau = 1.0 / SUBSTEPS
     y_coef = tau * ADV_COEF / 60.0
     end = PAD + rows
-    wide = WINDS * levels * RADIX * WIND_HALO
+    wide = far_start(WINDS, levels)
     reach = above_ref.shape[0] - wide
 
     map_ref[PAD - reach : PAD, :] = above_ref[wide : wide + reach, :]
@@ -520,12 +518,15 @@
 
     def level_step(level, carry):
         for f in range(WINDS):
-            part = rows_at((f * levels + level) * RADIX * WIND_HALO, RADIX * WIND_HALO)
+            near = rows_at((f * levels + level) * RADIX * 8, RADIX * 8)
+            far = rows_at(far_start(f, levels) + level * RADIX * FAR[f], RADIX * FAR[f])
             for t in range(RADIX):
-                packed = slice(t * WIND_HALO, (t + 1) * WIND_HALO)
-                now_ref[f, t, PAD - WIND_HALO : PAD, :] = above_ref.at[part][packed, :]
+                close, remote = slice(8 * t, 8 * t + 8), slice(FAR[f] * t, FAR[f] * (t + 1))
+                now_ref[f, t, PAD - 8 - FAR[f] : PAD - 8, :] = above_ref.at[far][remote, :]
+                now_ref[f, t, PAD - 8 : PAD, :] = above_ref.at[near][close, :]
                 now_ref[f, t, PAD:end, :] = own_ref[f, level, t]
-                now_ref[f, t, end : end + WIND_HALO, :] = below_ref.at[part][packed, :]
+                now_ref[f, t, end : end + 8, :] = below_ref.at[near][close, :]
+                now_ref[f, t, end + 8 : end + 8 + FAR[f], :] = below_ref.at[far][remote, :]
 
         def put(field, row, t, value):
             q, h = t // tiles_dev, t % tiles_dev
@@ -566,7 +567,7 @@
 
         for step in range(SUBSTEPS):
             reach = 2 * (SUBSTEPS - step) - 1
-            for row in range(PAD - reach, end + reach, 8):
+            for row in range((PAD - reach) // 8 * 8, end + reach, 8):
                 here = slice(row, row + 8)
                 circle = Circle(lambda t: now_ref[2, t % RADIX, here, :])
                 grad_x = (tau * SOUND * 0.5) * map_ref[here, :]
@@ -580,7 +581,7 @@
                     now_ref[0, t, here, :] = east
                     now_ref[1, t, here, :] = north
             reach -= 1
-            for row in range(PAD - reach, end + reach, 8):
+            for row in range((PAD - reach) // 8 * 8, end + reach, 8):
                 here = slice(row, row + 8)
                 circle = Circle(lambda t: now_ref[0, t % RADIX, here, :])
                 grad_x = (tau * SOUND * 0.5) * map_ref[here, :]
@@ -707,7 +708,7 @@
 
     outs = [(WINDS, levels, RADIX, rows, LANES), (rows, LANES)]
     if rows >= WIND_HALO:
-        outs += [(WINDS * levels * RADIX * WIND_HALO + rows, LANES)] * 2
+        outs += [(far_start(WINDS, levels) + rows, LANES)] * 2
     winds, maps, *sends = kernel_call(
         functools.partial(winds_kernel, dims),
         outs,

time: 73 us -> 72.2 us (0.989)
  transfers between devices with their start and end apart: 7 -> 7, of which waited for: 4 -> 4; matrix products, arithmetic and copies ran while one was open for 2% -> 2% of each run, Pallas kernels for 25% -> 24%
where the time goes in v5:
time: 72.2 us; the launch traced here: 71.7 us
  waiting for transfers between devices  26.1 us (36%)
  starting transfers between devices  22.7 us (31%)
  Pallas kernels  20.2 us (28%)
  local copies, waits for them, and re-layouts  0.97 us (1%)
  other arithmetic  0.88 us (1%)
  between operations  0.75 us (1%)
    all_to_all x4, waiting for transfers between devices, all_to_all(): return lax.all_to_all(value, group, split_axis=0, concat_axis=0, tiled=True)  25.2 us
    pallas_call x9, Pallas kernels, kernel_call(): pl.pallas_call(body, out_shape=[jax.ShapeDtypeStruct(s, jnp.float32) for...  20.2 us
    all_to_all x4, starting transfers between devices, all_to_all(): return lax.all_to_all(value, group, split_axis=0, concat_axis=0, tiled=True)  16.5 us
    ppermute x2, starting transfers between devices, moved(): return lax.ppermute(value, 'blk', pairs)  4.85 us
  transfers between devices with their start and end apart: 7, of which 4 were waited for; matrix products, arithmetic and copies ran while one was open for 2% of the time, Pallas kernels for 24%

profile of v5, /device:TPU:0, one launch (start us, length us, event | category | flops | bytes accessed | tf_op | source)
XLA Modules:
  0.0 71.7 jit_solution(882314037473714549)
XLA Ops:
  0.6 2.0 %pack_winds.1 = f32[8,200,128]{2,1,0:T(8,128)} custom-call(f32[8,2,8,512]{3,2,1,0:T(8,128)} %bitcast.16, f32[8,2,8,512]{3,2,1,0:T(8,128)} %bitcast.17, f32[8,2,8,512]{3,2,1,0:T(8,128)} %bitcast.18, f32[1,8]{1,0:T(1,128)} %bitcast.19), custom_call_target="tpu_custom_call" | custom-call | flops 1000000 | bytes 2000000 | tf_op jit(solution)/shard_map/pack_winds/pallas_call | solution.py:612
  2.6 5.2 %all-to-all-start = ((f32[8,200,128]{2,1,0:T(8,128)}), f32[8,200,128]{2,1,0:T(8,128)S(1)}, u32[]{:S(2)}, u32[]{:S(2)}) async-start(f32[8,200,128]{2,1,0:T(8,128)} %pack_winds.1), calls=%async_computation | async-start | bytes 1638400 | tf_op jit(solution)/shard_map/all_to_all | solution.py:666
  7.8 1.8 %edge_rows.1 = f32[8,64,128]{2,1,0:T(8,128)} custom-call(f32[8,2,8,512]{3,2,1,0:T(8,128)} %bitcast.11, f32[8,2,8,512]{3,2,1,0:T(8,128)} %bitcast.13), custom_call_target="tpu_custom_call" | custom-call | flops 1000000 | bytes 2000000 | tf_op jit(solution)/shard_map/edge_rows/pallas_call | solution.py:612
  9.6 1.4 %collective-permute-start.2 = (f32[8,64,128]{2,1,0:T(8,128)}, f32[8,64,128]{2,1,0:T(8,128)}, u32[]{:S(2)}, u32[]{:S(2)}) collective-permute-start(f32[8,64,128]{2,1,0:T(8,128)} %edge_rows.1), channel_id=1, source_target_pairs={{1,2},{3,4},{5,6},{2,1},{4,3},{6,5},{9,10},{11,12},{13,14},{10,9},... | collective-permute-start | bytes 786440 | tf_op jit(solution)/shard_map/ppermute | solution.py:695
  11.1 0.6 copy-done.3
  11.8 0.2 compare_reduce_fusion
  12.1 2.9 %pack_tracers.1 = f32[8,192,128]{2,1,0:T(8,128)} custom-call(f32[8,2,8,512]{3,2,1,0:T(8,128)} %bitcast.12, f32[8,2,8,512]{3,2,1,0:T(8,128)} %bitcast.14, f32[8,64,128]{2,1,0:T(8,128)} %collective-permute-done.2.refs_2_), custom_call_target="tpu_custom_call" | custom-call | flops 1000000 | bytes 2000000 | tf_op jit(solution)/shard_map/pack_tracers/pallas_call | solution.py:612
  15.0 5.7 %all-to-all-done.circles_ref = f32[8,200,128]{2,1,0:T(8,128)S(1)} async-done(((f32[8,200,128]{2,1,0:T(8,128)}), f32[8,200,128]{2,1,0:T(8,128)S(1)}, u32[]{:S(2)}, u32[]{:S(2)}) %all-to-all-start) | async-done | bytes 819232 | tf_op jit(solution)/shard_map/all_to_all | solution.py:666
  20.8 4.1 %all-to-all-start.1 = ((f32[8,192,128]{2,1,0:T(8,128)}), f32[8,192,128]{2,1,0:T(8,128)S(1)}, u32[]{:S(2)}, u32[]{:S(2)}) async-start(f32[8,192,128]{2,1,0:T(8,128)} %pack_tracers.1), calls=%async_computation.1 | async-start | bytes 1572864 | tf_op jit(solution)/shard_map/all_to_all | solution.py:666
  24.9 0.2 fusion.1
  25.2 2.4 %filter_winds.1 = (f32[3,2,16,16,128]{4,3,2,1,0:T(8,128)S(1)}, f32[16,128]{1,0:T(8,128)S(1)}, f32[944,128]{1,0:T(8,128)}, f32[944,128]{1,0:T(8,128)}) custom-call(f32[8,200,128]{2,1,0:T(8,128)S(1)} %all-to-all-done.circles_ref, s32[16,128]{1,0:T(8,128)S(1)} %broadcast_in_dim.67.cut_ref, f32[9,2,8,128]{3,2,1,0:T(8,128)S(1)} %copy-done.2, ...), custom_call_target="tpu_custom_call" | custom-call | flops 1000000 | bytes 2000000 | tf_op jit(solution)/shard_map/filter_winds/pallas_call | solution.py:612
  27.6 3.6 %collective-permute-start = (f32[944,128]{1,0:T(8,128)}, f32[944,128]{1,0:T(8,128)S(1)}, u32[]{:S(2)}, u32[]{:S(2)}) collective-permute-start(f32[944,128]{1,0:T(8,128)} %get-tuple-element.17), channel_id=1, source_target_pairs={{0,2},{2,4},{4,6},{1,3},{3,5},{5,7},{8,10},{10,12},{12,14},{9,11},... | collective-permute-start | bytes 1449992 | tf_op jit(solution)/shard_map/ppermute | solution.py:341
  31.2 1.3 %collective-permute-start.1 = (f32[944,128]{1,0:T(8,128)}, f32[944,128]{1,0:T(8,128)S(1)}, u32[]{:S(2)}, u32[]{:S(2)}) collective-permute-start(f32[944,128]{1,0:T(8,128)} %get-tuple-element.18), channel_id=1, source_target_pairs={{2,0},{4,2},{6,4},{3,1},{5,3},{7,5},{10,8},{12,10},{14,12},{11,9},... | collective-permute-start | bytes 1449992 | tf_op jit(solution)/shard_map/ppermute | solution.py:341
  32.5 0.2 compare_reduce_fusion.1
  32.7 4.8 %all-to-all-done.1.circles_ref = f32[8,192,128]{2,1,0:T(8,128)S(1)} async-done(((f32[8,192,128]{2,1,0:T(8,128)}), f32[8,192,128]{2,1,0:T(8,128)S(1)}, u32[]{:S(2)}, u32[]{:S(2)}) %all-to-all-start.1) | async-done | bytes 786464 | tf_op jit(solution)/shard_map/all_to_all | solution.py:666
  37.5 3.1 %tracers.1 = (f32[8,64,128]{2,1,0:T(8,128)}, f32[2,16,16,128]{3,2,1,0:T(8,128)S(1)}) custom-call(f32[8,192,128]{2,1,0:T(8,128)S(1)} %all-to-all-done.1.circles_ref, s32[16,128]{1,0:T(8,128)S(1)} %broadcast_in_dim.67.cut_ref, s32[8,128]{1,0:T(8,128)S(1)} %broadcast_in_dim.71.edge_cut_ref, f32[9,2,8,128]{3,2,1,0:T(8,128)S(1)} %copy-done.2, ...), custom_call_target="tpu_custom_call" | custom-call | flops 1000000 | bytes 2000000 | tf_op jit(solution)/shard_map/tracers/pallas_call | solution.py:612
  40.7 3.4 %all-to-all-start.3 = ((f32[8,64,128]{2,1,0:T(8,128)}), f32[8,64,128]{2,1,0:T(8,128)S(1)}, u32[]{:S(2)}, u32[]{:S(2)}) async-start(f32[8,64,128]{2,1,0:T(8,128)} %get-tuple-element.24), calls=%async_computation.3 | async-start | bytes 524288 | tf_op jit(solution)/shard_map/all_to_all | solution.py:666
  44.1 1.4 %inner_tendencies.1.inner_ref = f32[3,2,16,16,128]{4,3,2,1,0:T(8,128)S(1)} custom-call(f32[3,2,16,16,128]{4,3,2,1,0:T(8,128)S(1)} %get-tuple-element.15.own_ref.wind_ref, f32[16,128]{1,0:T(8,128)S(1)} %get-tuple-element.16.maps_ref), custom_call_target="tpu_custom_call" | custom-call | flops 1000000 | bytes 2000000 | tf_op jit(solution)/shard_map/inner_tendencies/pallas_call | solution.py:612
  45.6 0.9 %collective-permute-done.1.below_ref = f32[944,128]{1,0:T(8,128)S(1)} collective-permute-done((f32[944,128]{1,0:T(8,128)}, f32[944,128]{1,0:T(8,128)S(1)}, u32[]{:S(2)}, u32[]{:S(2)}) %collective-permute-start.1) | collective-permute-done | bytes 483360 | tf_op jit(solution)/shard_map/ppermute | solution.py:341
  46.5 4.9 %section.1 = f32[8,256,128]{2,1,0:T(8,128)} custom-call(f32[3,2,16,16,128]{4,3,2,1,0:T(8,128)S(1)} %get-tuple-element.15.own_ref.wind_ref, f32[3,2,16,16,128]{4,3,2,1,0:T(8,128)S(1)} %inner_tendencies.1.inner_ref, f32[944,128]{1,0:T(8,128)S(1)} %collective-permute-done.above_ref, f32[944,128]{1,0:T(8,128)S(1)} %collective-permute-done.1.below_ref, ...), custom_call_target="tpu_custom_call" | custom-call | flops 1000000 | bytes 2000000 | tf_op jit(solution)/shard_map/section/pallas_call | solution.py:612
  51.4 3.8 %all-to-all-start.2 = ((f32[8,256,128]{2,1,0:T(8,128)}), f32[8,256,128]{2,1,0:T(8,128)S(1)}, u32[]{:S(2)}, u32[]{:S(2)}) async-start(f32[8,256,128]{2,1,0:T(8,128)} %section.1), calls=%async_computation.2 | async-start | bytes 2097152 | tf_op jit(solution)/shard_map/all_to_all | solution.py:666
  55.2 0.7 %unpack_moist.1 = f32[8,2,8,512]{3,2,1,0:T(8,128)} custom-call(f32[8,64,128]{2,1,0:T(8,128)S(1)} %all-to-all-done.3.refs_0_), custom_call_target="tpu_custom_call" | custom-call | flops 1000000 | bytes 2000000 | tf_op jit(solution)/shard_map/unpack_moist/pallas_call | solution.py:612
  56.0 14.7 %all-to-all-done.2.refs_0_ = f32[8,256,128]{2,1,0:T(8,128)S(1)} async-done(((f32[8,256,128]{2,1,0:T(8,128)}), f32[8,256,128]{2,1,0:T(8,128)S(1)}, u32[]{:S(2)}, u32[]{:S(2)}) %all-to-all-start.2) | async-done | bytes 1048608 | tf_op jit(solution)/shard_map/all_to_all | solution.py:666
  70.7 1.0 %unpack.1 = (f32[8,2,8,512]{3,2,1,0:T(8,128)}, f32[8,2,8,512]{3,2,1,0:T(8,128)}, f32[8,2,8,512]{3,2,1,0:T(8,128)}, f32[8,2,8,512]{3,2,1,0:T(8,128)}) custom-call(f32[8,256,128]{2,1,0:T(8,128)S(1)} %all-to-all-done.2.refs_0_), custom_call_target="tpu_custom_call" | custom-call | flops 1000000 | bytes 2000000 | tf_op jit(solution)/shard_map/unpack/pallas_call | solution.py:612
  (24 shorter events, 0.7 us)
Async XLA Ops:
  2.6 18.1 %all-to-all-start = ((f32[8,200,128]{2,1,0:T(8,128)}), f32[8,200,128]{2,1,0:T(8,128)S(1)}, u32[]{:S(2)}, u32[]{:S(2)}) async-start(f32[8,200,128]{2,1,0:T(8,128)} %pack_winds.1), calls=%async_computation | async-start | bytes 1638400 | tf_op jit(solution)/shard_map/all_to_all | solution.py:666
  9.6 2.5 %collective-permute-start.2 = (f32[8,64,128]{2,1,0:T(8,128)}, f32[8,64,128]{2,1,0:T(8,128)}, u32[]{:S(2)}, u32[]{:S(2)}) collective-permute-start(f32[8,64,128]{2,1,0:T(8,128)} %edge_rows.1), channel_id=1, source_target_pairs={{1,2},{3,4},{5,6},{2,1},{4,3},{6,5},{9,10},{11,12},{13,14},{10,9},... | collective-permute-start | bytes 786440 | tf_op jit(solution)/shard_map/ppermute | solution.py:695
  11.0 0.7 copy-start.3
  11.0 0.7 copy-start.4
  15.0 10.2 %copy-start = (bf16[256,256]{1,0:T(8,128)(2,1)S(1)}, bf16[256,256]{1,0:T(8,128)(2,1)}, u32[]{:S(2)}) copy-start(bf16[256,256]{1,0:T(8,128)(2,1)} %constant.40.clone.low_ref) | copy-start | bytes 393220
  15.0 10.2 %copy-start.1 = (bf16[256,256]{1,0:T(8,128)(2,1)S(1)}, bf16[256,256]{1,0:T(8,128)(2,1)}, u32[]{:S(2)}) copy-start(bf16[256,256]{1,0:T(8,128)(2,1)} %constant.39.clone.high_ref) | copy-start | bytes 393220
  15.0 10.2 %copy-start.2 = (f32[9,2,8,128]{3,2,1,0:T(8,128)S(1)}, f32[9,2,8,128]{3,2,1,0:T(8,128)}, u32[]{:S(2)}) copy-start(f32[9,2,8,128]{3,2,1,0:T(8,128)} %constant.38.clone.twiddle_ref) | copy-start | bytes 221188
  20.8 16.7 %all-to-all-start.1 = ((f32[8,192,128]{2,1,0:T(8,128)}), f32[8,192,128]{2,1,0:T(8,128)S(1)}, u32[]{:S(2)}, u32[]{:S(2)}) async-start(f32[8,192,128]{2,1,0:T(8,128)} %pack_tracers.1), calls=%async_computation.1 | async-start | bytes 1572864 | tf_op jit(solution)/shard_map/all_to_all | solution.py:666
  27.6 17.9 %collective-permute-start = (f32[944,128]{1,0:T(8,128)}, f32[944,128]{1,0:T(8,128)S(1)}, u32[]{:S(2)}, u32[]{:S(2)}) collective-permute-start(f32[944,128]{1,0:T(8,128)} %get-tuple-element.17), channel_id=1, source_target_pairs={{0,2},{2,4},{4,6},{1,3},{3,5},{5,7},{8,10},{10,12},{12,14},{9,11},... | collective-permute-start | bytes 1449992 | tf_op jit(solution)/shard_map/ppermute | solution.py:341
  31.2 15.3 %collective-permute-start.1 = (f32[944,128]{1,0:T(8,128)}, f32[944,128]{1,0:T(8,128)S(1)}, u32[]{:S(2)}, u32[]{:S(2)}) collective-permute-start(f32[944,128]{1,0:T(8,128)} %get-tuple-element.18), channel_id=1, source_target_pairs={{2,0},{4,2},{6,4},{3,1},{5,3},{7,5},{10,8},{12,10},{14,12},{11,9},... | collective-permute-start | bytes 1449992 | tf_op jit(solution)/shard_map/ppermute | solution.py:341
  40.7 10.7 %all-to-all-start.3 = ((f32[8,64,128]{2,1,0:T(8,128)}), f32[8,64,128]{2,1,0:T(8,128)S(1)}, u32[]{:S(2)}, u32[]{:S(2)}) async-start(f32[8,64,128]{2,1,0:T(8,128)} %get-tuple-element.24), calls=%async_computation.3 | async-start | bytes 524288 | tf_op jit(solution)/shard_map/all_to_all | solution.py:666
  51.4 19.3 %all-to-all-start.2 = ((f32[8,256,128]{2,1,0:T(8,128)}), f32[8,256,128]{2,1,0:T(8,128)S(1)}, u32[]{:S(2)}, u32[]{:S(2)}) async-start(f32[8,256,128]{2,1,0:T(8,128)} %section.1), calls=%async_computation.2 | async-start | bytes 2097152 | tf_op jit(solution)/shard_map/all_to_all | solution.py:666

commit v6 on v5

--- a/solution.py
+++ b/solution.py
@@ -300,7 +300,15 @@
 
 def winds_kernel(dims, circles_ref, cut_ref, twiddle_ref, high_ref, low_ref, own_ref, maps_ref, *refs):
     levels, sub, rows, tiles_dev = dims
-    *sends, waves_ref = refs
+    *refs, waves_ref = refs
+    send_refs, sends, sems = (refs[:2], refs[2:4], refs[4]) if refs else ([], [], None)
+    copies = []
+
+    def leave(here):
+        for ref, send in zip(sends, send_refs):
+            copies.append(pltpu.make_async_copy(ref.at[here], send.at[here], sems.at[len(copies)]))
+            copies[-1].start()
+
     groups = WINDS * levels
     total = groups * rows
     wide = far_start(WINDS, levels)
@@ -330,6 +338,10 @@
                 far = slice(start, start + FAR[f])
                 sends[0][near, :], sends[0][far, :] = value[:8], value[8 : 8 + FAR[f]]
                 sends[1][near, :], sends[1][far, :] = value[rows - 8 :], value[rows - 8 - FAR[f] : rows - 8]
+        leave(slice(group * RADIX * 8, (group + 1) * RADIX * 8))
+    leave(slice(groups * RADIX * 8, wide + rows))
+    for copy in copies:
+        copy.wait()
 
 
 def exchanged(own, maps, sends):
@@ -502,7 +514,7 @@
 
 def section_kernel(
     dims, own_ref, inner_ref, above_ref, below_ref, maps_ref, temp_ref, coef_ref, out_ref,
-    now_ref, tend_ref, free_ref, map_ref,
+    now_ref, tend_ref, free_ref, map_ref, stage_ref, sems,
 ):
     levels, sub, rows, tiles_dev = dims
     lane = lax.broadcasted_iota(jnp.int32, (8, LANES), 1)
@@ -516,7 +528,9 @@
     map_ref[PAD:end, :] = maps_ref[...]
     map_ref[end : end + reach, :] = below_ref[wide : wide + reach, :]
 
-    def level_step(level, carry):
+    copies = []
+
+    def level_step(level):
         for f in range(WINDS):
             near = rows_at((f * levels + level) * RADIX * 8, RADIX * 8)
             far = rows_at(far_start(f, levels) + level * RADIX * FAR[f], RADIX * FAR[f])
@@ -530,7 +544,14 @@
 
         def put(field, row, t, value):
             q, h = t // tiles_dev, t % tiles_dev
-            out_ref[q * sub + (row - PAD) // 8, tile_rows(field * levels + level, h, tiles_dev), :] = value
+            stage_ref[q * sub + (row - PAD) // 8, tile_rows(field * levels + level, h, tiles_dev), :] = value
+
+        def leave(field):
+            here = rows_at((field * levels + level) * tiles_dev * 8, tiles_dev * 8)
+            copies.append(
+                pltpu.make_async_copy(stage_ref.at[:, here, :], out_ref.at[:, here, :], sems.at[len(copies)])
+            )
+            copies[-1].start()
 
         for row in (PAD - 8, end):
             here = slice(row, row + 8)
@@ -580,6 +601,12 @@
                     north = north + (tend_ref[1, t, here, :] - grad_y * dy - coriolis * east)
                     now_ref[0, t, here, :] = east
                     now_ref[1, t, here, :] = north
+            if step == SUBSTEPS - 1:
+                for field in range(2):
+                    for row in range(PAD, end, 8):
+                        for t in range(RADIX):
+                            put(field, row, t, now_ref[field, t, row : row + 8, :])
+                    leave(field)
             reach -= 1
             for row in range((PAD - reach) // 8 * 8, end + reach, 8):
                 here = slice(row, row + 8)
@@ -594,26 +621,27 @@
                     )
 
         for row in range(PAD, end, 8):
-            here = slice(row, row + 8)
             for t in range(RADIX):
-                east, north, press = (now_ref[f, t, here, :] for f in range(WINDS))
-                put(0, row, t, east)
-                put(1, row, t, north)
+                press = now_ref[2, t, row : row + 8, :]
                 put(2, row, t, press)
                 put(3, row, t, free_ref[t, row - PAD : row - PAD + 8, :] + THETA_DIV * press)
-        return carry
-
-    lax.fori_loop(0, levels, level_step, 0)
-
-
-def kernel_call(body, shapes, scratch, name, *args, raw=0, raw_out=False, cost=2 * 10**6):
+        leave(2)
+        leave(3)
+
+    for level in range(levels):
+        level_step(level)
+    for copy in copies:
+        copy.wait()
+
+
+def kernel_call(body, shapes, scratch, name, *args, raw=0, raw_out=0, cost=2 * 10**6):
     vmem = pl.BlockSpec(memory_space=pltpu.VMEM)
     hbm = pl.BlockSpec(memory_space=pltpu.HBM)
     return pl.pallas_call(
         body,
         out_shape=[jax.ShapeDtypeStruct(s, jnp.float32) for s in shapes],
         in_specs=[hbm] * raw + [vmem] * (len(args) - raw),
-        out_specs=[hbm if raw_out else vmem] * len(shapes),
+        out_specs=[vmem] * (len(shapes) - raw_out) + [hbm] * raw_out,
         scratch_shapes=[
             pltpu.VMEM(s, jnp.float32) if isinstance(s, tuple) else s for s in scratch
         ],
@@ -660,7 +688,7 @@
 
     def unpacked(count, name, value):
         scratch = [(count,) + stage, dma((2 * count,))]
-        return kernel_call(unpack_kernel, [field] * count, scratch, name, value, raw_out=True)
+        return kernel_call(unpack_kernel, [field] * count, scratch, name, value, raw_out=count)
 
     def all_to_all(value):
         return lax.all_to_all(value, group, split_axis=0, concat_axis=0, tiled=True)
@@ -678,7 +706,7 @@
         "pack_winds",
         east, north, press, map_factor.reshape(1, rows_dev),
         raw=WINDS + 1,
-        raw_out=True,
+        raw_out=1,
     )
     wind_circles = all_to_all(packed)
 
@@ -707,14 +735,19 @@
     tracer_circles = all_to_all(packed)
 
     outs = [(WINDS, levels, RADIX, rows, LANES), (rows, LANES)]
-    if rows >= WIND_HALO:
-        outs += [(far_start(WINDS, levels) + rows, LANES)] * 2
+    scratch = [((HALF + 1) * WINDS * levels * rows, 2 * LANES)]
+    with_sends = rows >= WIND_HALO
+    if with_sends:
+        send = (far_start(WINDS, levels) + rows, LANES)
+        outs += [send] * 2
+        scratch = [send] * 2 + [dma((2 * (WINDS * levels + 1),))] + scratch
     winds, maps, *sends = kernel_call(
         functools.partial(winds_kernel, dims),
         outs,
-        [((HALF + 1) * WINDS * levels * rows, 2 * LANES)],
+        scratch,
         "filter_winds",
         wind_circles, cut, twiddle, high, low,
+        raw_out=2 * with_sends,
     )
     halos = exchanged(winds, maps, sends)
     (inner,) = kernel_call(
@@ -739,9 +772,17 @@
     (out,) = kernel_call(
         functools.partial(section_kernel, dims),
         [(peers, 4 * levels * tiles_dev * 8, LANES)],
-        [(WINDS, RADIX, tall, LANES), (WINDS, RADIX, tall, LANES), (RADIX, rows, LANES), (tall, LANES)],
+        [
+            (WINDS, RADIX, tall, LANES),
+            (WINDS, RADIX, tall, LANES),
+            (RADIX, rows, LANES),
+            (tall, LANES),
+            (peers, 4 * levels * tiles_dev * 8, LANES),
+            dma((4 * levels,)),
+        ],
         "section",
         winds, inner, *halos, maps, temp_part, coefs,
+        raw_out=1,
     )
     out = all_to_all(out)
     (new_moist,) = unpacked(1, "unpack_moist", moist_out)

time: 72.2 us -> 72.1 us (level)
  no operation moved by 1% of the time
where the time goes in v6:
time: 72.1 us; the launch traced here: 71.6 us
  waiting for transfers between devices  26.1 us (36%)
  starting transfers between devices  22.8 us (32%)
  Pallas kernels  20.1 us (28%)
  local copies, waits for them, and re-layouts  0.97 us (1%)
  other arithmetic  0.88 us (1%)
  between operations  0.78 us (1%)
    all_to_all x4, waiting for transfers between devices, all_to_all(): return lax.all_to_all(value, group, split_axis=0, concat_axis=0, tiled=True)  25.2 us
    pallas_call x9, Pallas kernels, kernel_call(): pl.pallas_call(body, out_shape=[jax.ShapeDtypeStruct(s, jnp.float32) for...  20.1 us
    all_to_all x4, starting transfers between devices, all_to_all(): return lax.all_to_all(value, group, split_axis=0, concat_axis=0, tiled=True)  16.5 us
    ppermute x2, starting transfers between devices, moved(): return lax.ppermute(value, 'blk', pairs)  4.86 us
  transfers between devices with their start and end apart: 7, of which 4 were waited for; matrix products, arithmetic and copies ran while one was open for 2% of the time, Pallas kernels for 24%

profile of v6, /device:TPU:0, one launch (start us, length us, event | category | flops | bytes accessed | tf_op | source)
XLA Modules:
  0.0 71.6 jit_solution(17511697875942127071)
XLA Ops:
  0.6 2.0 %pack_winds.1 = f32[8,200,128]{2,1,0:T(8,128)} custom-call(f32[8,2,8,512]{3,2,1,0:T(8,128)} %bitcast.16, f32[8,2,8,512]{3,2,1,0:T(8,128)} %bitcast.17, f32[8,2,8,512]{3,2,1,0:T(8,128)} %bitcast.18, f32[1,8]{1,0:T(1,128)} %bitcast.19), custom_call_target="tpu_custom_call" | custom-call | flops 1000000 | bytes 2000000 | tf_op jit(solution)/shard_map/pack_winds/pallas_call | solution.py:640
  2.6 5.2 %all-to-all-start = ((f32[8,200,128]{2,1,0:T(8,128)}), f32[8,200,128]{2,1,0:T(8,128)S(1)}, u32[]{:S(2)}, u32[]{:S(2)}) async-start(f32[8,200,128]{2,1,0:T(8,128)} %pack_winds.1), calls=%async_computation | async-start | bytes 1638400 | tf_op jit(solution)/shard_map/all_to_all | solution.py:694
  7.8 1.8 %edge_rows.1 = f32[8,64,128]{2,1,0:T(8,128)} custom-call(f32[8,2,8,512]{3,2,1,0:T(8,128)} %bitcast.11, f32[8,2,8,512]{3,2,1,0:T(8,128)} %bitcast.13), custom_call_target="tpu_custom_call" | custom-call | flops 1000000 | bytes 2000000 | tf_op jit(solution)/shard_map/edge_rows/pallas_call | solution.py:640
  9.6 1.4 %collective-permute-start.2 = (f32[8,64,128]{2,1,0:T(8,128)}, f32[8,64,128]{2,1,0:T(8,128)}, u32[]{:S(2)}, u32[]{:S(2)}) collective-permute-start(f32[8,64,128]{2,1,0:T(8,128)} %edge_rows.1), channel_id=1, source_target_pairs={{1,2},{3,4},{5,6},{2,1},{4,3},{6,5},{9,10},{11,12},{13,14},{10,9},... | collective-permute-start | bytes 786440 | tf_op jit(solution)/shard_map/ppermute | solution.py:723
  11.1 0.6 copy-done.3
  11.8 0.2 compare_reduce_fusion
  12.1 2.9 %pack_tracers.1 = f32[8,192,128]{2,1,0:T(8,128)} custom-call(f32[8,2,8,512]{3,2,1,0:T(8,128)} %bitcast.12, f32[8,2,8,512]{3,2,1,0:T(8,128)} %bitcast.14, f32[8,64,128]{2,1,0:T(8,128)} %collective-permute-done.2.refs_2_), custom_call_target="tpu_custom_call" | custom-call | flops 1000000 | bytes 2000000 | tf_op jit(solution)/shard_map/pack_tracers/pallas_call | solution.py:640
  15.0 5.7 %all-to-all-done.circles_ref = f32[8,200,128]{2,1,0:T(8,128)S(1)} async-done(((f32[8,200,128]{2,1,0:T(8,128)}), f32[8,200,128]{2,1,0:T(8,128)S(1)}, u32[]{:S(2)}, u32[]{:S(2)}) %all-to-all-start) | async-done | bytes 819232 | tf_op jit(solution)/shard_map/all_to_all | solution.py:694
  20.8 4.1 %all-to-all-start.1 = ((f32[8,192,128]{2,1,0:T(8,128)}), f32[8,192,128]{2,1,0:T(8,128)S(1)}, u32[]{:S(2)}, u32[]{:S(2)}) async-start(f32[8,192,128]{2,1,0:T(8,128)} %pack_tracers.1), calls=%async_computation.1 | async-start | bytes 1572864 | tf_op jit(solution)/shard_map/all_to_all | solution.py:694
  24.9 0.2 fusion.1
  25.2 2.4 %filter_winds.1 = (f32[3,2,16,16,128]{4,3,2,1,0:T(8,128)S(1)}, f32[16,128]{1,0:T(8,128)S(1)}, f32[944,128]{1,0:T(8,128)}, f32[944,128]{1,0:T(8,128)}) custom-call(f32[8,200,128]{2,1,0:T(8,128)S(1)} %all-to-all-done.circles_ref, s32[16,128]{1,0:T(8,128)S(1)} %broadcast_in_dim.67.cut_ref, f32[9,2,8,128]{3,2,1,0:T(8,128)S(1)} %copy-done.2, ...), custom_call_target="tpu_custom_call" | custom-call | flops 1000000 | bytes 2000000 | tf_op jit(solution)/shard_map/filter_winds/pallas_call | solution.py:640
  27.6 3.6 %collective-permute-start = (f32[944,128]{1,0:T(8,128)}, f32[944,128]{1,0:T(8,128)S(1)}, u32[]{:S(2)}, u32[]{:S(2)}) collective-permute-start(f32[944,128]{1,0:T(8,128)} %get-tuple-element.17), channel_id=1, source_target_pairs={{0,2},{2,4},{4,6},{1,3},{3,5},{5,7},{8,10},{10,12},{12,14},{9,11},... | collective-permute-start | bytes 1449992 | tf_op jit(solution)/shard_map/ppermute | solution.py:353
  31.2 1.3 %collective-permute-start.1 = (f32[944,128]{1,0:T(8,128)}, f32[944,128]{1,0:T(8,128)S(1)}, u32[]{:S(2)}, u32[]{:S(2)}) collective-permute-start(f32[944,128]{1,0:T(8,128)} %get-tuple-element.18), channel_id=1, source_target_pairs={{2,0},{4,2},{6,4},{3,1},{5,3},{7,5},{10,8},{12,10},{14,12},{11,9},... | collective-permute-start | bytes 1449992 | tf_op jit(solution)/shard_map/ppermute | solution.py:353
  32.5 0.2 compare_reduce_fusion.1
  32.7 4.8 %all-to-all-done.1.circles_ref = f32[8,192,128]{2,1,0:T(8,128)S(1)} async-done(((f32[8,192,128]{2,1,0:T(8,128)}), f32[8,192,128]{2,1,0:T(8,128)S(1)}, u32[]{:S(2)}, u32[]{:S(2)}) %all-to-all-start.1) | async-done | bytes 786464 | tf_op jit(solution)/shard_map/all_to_all | solution.py:694
  37.5 3.1 %tracers.1 = (f32[8,64,128]{2,1,0:T(8,128)}, f32[2,16,16,128]{3,2,1,0:T(8,128)S(1)}) custom-call(f32[8,192,128]{2,1,0:T(8,128)S(1)} %all-to-all-done.1.circles_ref, s32[16,128]{1,0:T(8,128)S(1)} %broadcast_in_dim.67.cut_ref, s32[8,128]{1,0:T(8,128)S(1)} %broadcast_in_dim.71.edge_cut_ref, f32[9,2,8,128]{3,2,1,0:T(8,128)S(1)} %copy-done.2, ...), custom_call_target="tpu_custom_call" | custom-call | flops 1000000 | bytes 2000000 | tf_op jit(solution)/shard_map/tracers/pallas_call | solution.py:640
  40.7 3.4 %all-to-all-start.3 = ((f32[8,64,128]{2,1,0:T(8,128)}), f32[8,64,128]{2,1,0:T(8,128)S(1)}, u32[]{:S(2)}, u32[]{:S(2)}) async-start(f32[8,64,128]{2,1,0:T(8,128)} %get-tuple-element.24), calls=%async_computation.3 | async-start | bytes 524288 | tf_op jit(solution)/shard_map/all_to_all | solution.py:694
  44.1 1.4 %inner_tendencies.1.inner_ref = f32[3,2,16,16,128]{4,3,2,1,0:T(8,128)S(1)} custom-call(f32[3,2,16,16,128]{4,3,2,1,0:T(8,128)S(1)} %get-tuple-element.15.own_ref.wind_ref, f32[16,128]{1,0:T(8,128)S(1)} %get-tuple-element.16.maps_ref), custom_call_target="tpu_custom_call" | custom-call | flops 1000000 | bytes 2000000 | tf_op jit(solution)/shard_map/inner_tendencies/pallas_call | solution.py:640
  45.6 0.9 %collective-permute-done.1.below_ref = f32[944,128]{1,0:T(8,128)S(1)} collective-permute-done((f32[944,128]{1,0:T(8,128)}, f32[944,128]{1,0:T(8,128)S(1)}, u32[]{:S(2)}, u32[]{:S(2)}) %collective-permute-start.1) | collective-permute-done | bytes 483360 | tf_op jit(solution)/shard_map/ppermute | solution.py:353
  46.5 4.7 %section.1 = f32[8,256,128]{2,1,0:T(8,128)} custom-call(f32[3,2,16,16,128]{4,3,2,1,0:T(8,128)S(1)} %get-tuple-element.15.own_ref.wind_ref, f32[3,2,16,16,128]{4,3,2,1,0:T(8,128)S(1)} %inner_tendencies.1.inner_ref, f32[944,128]{1,0:T(8,128)S(1)} %collective-permute-done.above_ref, f32[944,128]{1,0:T(8,128)S(1)} %collective-permute-done.1.below_ref, ...), custom_call_target="tpu_custom_call" | custom-call | flops 1000000 | bytes 2000000 | tf_op jit(solution)/shard_map/section/pallas_call | solution.py:640
  51.3 3.9 %all-to-all-start.2 = ((f32[8,256,128]{2,1,0:T(8,128)}), f32[8,256,128]{2,1,0:T(8,128)S(1)}, u32[]{:S(2)}, u32[]{:S(2)}) async-start(f32[8,256,128]{2,1,0:T(8,128)} %section.1), calls=%async_computation.2 | async-start | bytes 2097152 | tf_op jit(solution)/shard_map/all_to_all | solution.py:694
  55.1 0.7 %unpack_moist.1 = f32[8,2,8,512]{3,2,1,0:T(8,128)} custom-call(f32[8,64,128]{2,1,0:T(8,128)S(1)} %all-to-all-done.3.refs_0_), custom_call_target="tpu_custom_call" | custom-call | flops 1000000 | bytes 2000000 | tf_op jit(solution)/shard_map/unpack_moist/pallas_call | solution.py:640
  55.9 14.7 %all-to-all-done.2.refs_0_ = f32[8,256,128]{2,1,0:T(8,128)S(1)} async-done(((f32[8,256,128]{2,1,0:T(8,128)}), f32[8,256,128]{2,1,0:T(8,128)S(1)}, u32[]{:S(2)}, u32[]{:S(2)}) %all-to-all-start.2) | async-done | bytes 1048608 | tf_op jit(solution)/shard_map/all_to_all | solution.py:694
  70.5 1.0 %unpack.1 = (f32[8,2,8,512]{3,2,1,0:T(8,128)}, f32[8,2,8,512]{3,2,1,0:T(8,128)}, f32[8,2,8,512]{3,2,1,0:T(8,128)}, f32[8,2,8,512]{3,2,1,0:T(8,128)}) custom-call(f32[8,256,128]{2,1,0:T(8,128)S(1)} %all-to-all-done.2.refs_0_), custom_call_target="tpu_custom_call" | custom-call | flops 1000000 | bytes 2000000 | tf_op jit(solution)/shard_map/unpack/pallas_call | solution.py:640
  (24 shorter events, 0.7 us)
Async XLA Ops:
  2.6 18.1 %all-to-all-start = ((f32[8,200,128]{2,1,0:T(8,128)}), f32[8,200,128]{2,1,0:T(8,128)S(1)}, u32[]{:S(2)}, u32[]{:S(2)}) async-start(f32[8,200,128]{2,1,0:T(8,128)} %pack_winds.1), calls=%async_computation | async-start | bytes 1638400 | tf_op jit(solution)/shard_map/all_to_all | solution.py:694
  9.6 2.5 %collective-permute-start.2 = (f32[8,64,128]{2,1,0:T(8,128)}, f32[8,64,128]{2,1,0:T(8,128)}, u32[]{:S(2)}, u32[]{:S(2)}) collective-permute-start(f32[8,64,128]{2,1,0:T(8,128)} %edge_rows.1), channel_id=1, source_target_pairs={{1,2},{3,4},{5,6},{2,1},{4,3},{6,5},{9,10},{11,12},{13,14},{10,9},... | collective-permute-start | bytes 786440 | tf_op jit(solution)/shard_map/ppermute | solution.py:723
  11.0 0.7 copy-start.3
  11.0 0.7 copy-start.4
  15.0 10.2 %copy-start = (bf16[256,256]{1,0:T(8,128)(2,1)S(1)}, bf16[256,256]{1,0:T(8,128)(2,1)}, u32[]{:S(2)}) copy-start(bf16[256,256]{1,0:T(8,128)(2,1)} %constant.40.clone.low_ref) | copy-start | bytes 393220
  15.0 10.2 %copy-start.1 = (bf16[256,256]{1,0:T(8,128)(2,1)S(1)}, bf16[256,256]{1,0:T(8,128)(2,1)}, u32[]{:S(2)}) copy-start(bf16[256,256]{1,0:T(8,128)(2,1)} %constant.39.clone.high_ref) | copy-start | bytes 393220
  15.0 10.2 %copy-start.2 = (f32[9,2,8,128]{3,2,1,0:T(8,128)S(1)}, f32[9,2,8,128]{3,2,1,0:T(8,128)}, u32[]{:S(2)}) copy-start(f32[9,2,8,128]{3,2,1,0:T(8,128)} %constant.38.clone.twiddle_ref) | copy-start | bytes 221188
  20.8 16.7 %all-to-all-start.1 = ((f32[8,192,128]{2,1,0:T(8,128)}), f32[8,192,128]{2,1,0:T(8,128)S(1)}, u32[]{:S(2)}, u32[]{:S(2)}) async-start(f32[8,192,128]{2,1,0:T(8,128)} %pack_tracers.1), calls=%async_computation.1 | async-start | bytes 1572864 | tf_op jit(solution)/shard_map/all_to_all | solution.py:694
  27.6 18.0 %collective-permute-start = (f32[944,128]{1,0:T(8,128)}, f32[944,128]{1,0:T(8,128)S(1)}, u32[]{:S(2)}, u32[]{:S(2)}) collective-permute-start(f32[944,128]{1,0:T(8,128)} %get-tuple-element.17), channel_id=1, source_target_pairs={{0,2},{2,4},{4,6},{1,3},{3,5},{5,7},{8,10},{10,12},{12,14},{9,11},... | collective-permute-start | bytes 1449992 | tf_op jit(solution)/shard_map/ppermute | solution.py:353
  31.2 15.3 %collective-permute-start.1 = (f32[944,128]{1,0:T(8,128)}, f32[944,128]{1,0:T(8,128)S(1)}, u32[]{:S(2)}, u32[]{:S(2)}) collective-permute-start(f32[944,128]{1,0:T(8,128)} %get-tuple-element.18), channel_id=1, source_target_pairs={{2,0},{4,2},{6,4},{3,1},{5,3},{7,5},{10,8},{12,10},{14,12},{11,9},... | collective-permute-start | bytes 1449992 | tf_op jit(solution)/shard_map/ppermute | solution.py:353
  40.7 10.6 %all-to-all-start.3 = ((f32[8,64,128]{2,1,0:T(8,128)}), f32[8,64,128]{2,1,0:T(8,128)S(1)}, u32[]{:S(2)}, u32[]{:S(2)}) async-start(f32[8,64,128]{2,1,0:T(8,128)} %get-tuple-element.24), calls=%async_computation.3 | async-start | bytes 524288 | tf_op jit(solution)/shard_map/all_to_all | solution.py:694
  51.3 19.3 %all-to-all-start.2 = ((f32[8,256,128]{2,1,0:T(8,128)}), f32[8,256,128]{2,1,0:T(8,128)S(1)}, u32[]{:S(2)}, u32[]{:S(2)}) async-start(f32[8,256,128]{2,1,0:T(8,128)} %section.1), calls=%async_computation.2 | async-start | bytes 2097152 | tf_op jit(solution)/shard_map/all_to_all | solution.py:694
